TPU v7x, 32 devices: a whole 2x2x4 slice. The times are simulated.
32 devices in a mesh: group: 2 (over x), seq: 8 (over z, y), tp: 2 (over core).
Axes of the slice: x: 2, y: 2, z: 4, core: 2. Of those that a mesh axis runs over, the one named last changes fastest.
Arguments:
- queries: bfloat16 [2048, 2048], P(('group', 'seq'), 'tp'), parts along dimension 0, may hold values from -32 to 32
- keys: bfloat16 [16384, 2048], P(('group', 'seq'), 'tp'), parts along dimension 0, may hold values from -14 to 14
- values: bfloat16 [16384, 2048], P(('group', 'seq'), 'tp'), parts along dimension 0, may hold values from -6 to 6
- out_grad: bfloat16 [2048, 2048], P(('group', 'seq', 'tp')), parts along dimension 0, may hold values from -6 to 6
- starts: int32 [32], P('group'), parts along dimension 0, may hold values from 0 to 7168, as said below
Outputs:
- grad_queries: bfloat16 [2048, 2048], P(('group', 'seq'), 'tp'), parts along dimension 0
- grad_keys: bfloat16 [16384, 2048], P(('group', 'seq'), 'tp'), parts along dimension 0
- grad_values: bfloat16 [16384, 2048], P(('group', 'seq'), 'tp'), parts along dimension 0
There are 2 independent parts, one for each index of `group`. A program takes and returns all parts, laid end to end along the dimension named above; each array names one. Nothing has to cross between parts.
Inputs may be any that keep to these rules, and one draw needn't show every extreme that they name: Each entry is a multiple of 64. For block b with d = b // 2, starts[b] lies between max(0, (d - 1) * 1024) and min((d + 1) * 1024, 7168); the first block of each d takes the lower of these ends and the last block of each d the upper one.
All inputs are finite; a program needn't handle non-finite values.
Results may differ from a plain program's by a relative error of at most 0.015.
Values may be sent and summed in bfloat16 or wider, within the bound.
No kernel may reach another device: no remote copies, remote signals or barrier semaphores. Data moves between devices by JAX's collectives and lax.ppermute only.
A program may use at most 192 MiB of HBM per device.

v0:
```python
import math

import jax
import jax.numpy as jnp
from jax import lax
from jax.sharding import PartitionSpec as P

HD = 128
WIN = 1024
BLK = 64


def with_halo(cells, sides, width):
    for axis, dim in sides:
        count = lax.axis_size(axis)
        ends = count - 1
        head = lax.slice_in_dim(cells, 0, width, axis=dim)
        tail = lax.slice_in_dim(cells, cells.shape[dim] - width, cells.shape[dim], axis=dim)
        cells = jnp.concatenate(
            [
                lax.ppermute(tail, axis, [(i, (i + 1) % count) for i in range(ends)]),
                cells,
                lax.ppermute(head, axis, [((i + 1) % count, i) for i in range(ends)]),
            ],
            axis=dim,
        )
    return cells


def shifted(array, axis, by):
    devices = lax.axis_size(axis)
    pairs = [(i, i + by) for i in range(devices) if 0 <= i + by < devices]
    return lax.ppermute(array, axis, pairs)


def attend_block(q_blk, g_blk, key_win, val_win, scale):
    scores = jnp.einsum("qhd,khd->hqk", q_blk, key_win, preferred_element_type=jnp.float32) * scale
    top = jnp.max(scores, axis=-1, keepdims=True)
    lse = top + jnp.log(jnp.sum(jnp.exp(scores - top), axis=-1, keepdims=True))
    probs = jnp.exp(scores - lse)
    probs_low = probs.astype(jnp.bfloat16)
    attended = jnp.einsum("hqk,khd->qhd", probs_low, val_win, preferred_element_type=jnp.float32)
    delta = jnp.sum(g_blk.astype(jnp.float32) * attended, axis=-1).T
    dprobs = jnp.einsum("qhd,khd->hqk", g_blk, val_win, preferred_element_type=jnp.float32)
    dscores = (scale * probs * (dprobs - delta[:, :, None])).astype(jnp.bfloat16)
    grad_q = jnp.einsum("hqk,khd->qhd", dscores, key_win, preferred_element_type=jnp.float32)
    return (grad_q, lse[:, :, 0], delta, probs_low, dscores)


def shards(queries, keys, values, out_grad, starts):
    frames = queries.shape[0]
    events = keys.shape[0]
    width = queries.shape[1]
    heads = width // HD
    per_dev = frames // BLK
    scale = 1.0 / math.sqrt(HD)
    seq_index = lax.axis_index("seq")
    grads = lax.all_to_all(out_grad, "tp", split_axis=1, concat_axis=0, tiled=True)
    extended = with_halo(jnp.stack([keys, values]), (("seq", 1),), events)
    base = (seq_index - 1) * events
    my_starts = lax.dynamic_slice_in_dim(starts, seq_index * per_dev, per_dev)
    q_blocks = queries.reshape(per_dev, BLK, heads, HD)
    g_blocks = grads.reshape(per_dev, BLK, heads, HD)

    def windows(begin):
        offset = begin - base
        key_win = lax.dynamic_slice_in_dim(extended[0], offset, WIN).reshape(WIN, heads, HD)
        val_win = lax.dynamic_slice_in_dim(extended[1], offset, WIN).reshape(WIN, heads, HD)
        return (offset, key_win, val_win)

    def step_sums(carry, item):
        acc_k, acc_v = carry
        q_blk, g_blk, begin = item
        offset, key_win, val_win = windows(begin)
        grad_q, lse, delta, probs_low, dscores = attend_block(q_blk, g_blk, key_win, val_win, scale)
        grad_k = jnp.einsum(
            "hqk,qhd->khd", dscores, q_blk, preferred_element_type=jnp.float32
        ).reshape(WIN, width)
        grad_v = jnp.einsum(
            "hqk,qhd->khd", probs_low, g_blk, preferred_element_type=jnp.float32
        ).reshape(WIN, width)
        acc_k = lax.dynamic_update_slice_in_dim(
            acc_k, lax.dynamic_slice_in_dim(acc_k, offset, WIN) + grad_k, offset, 0
        )
        acc_v = lax.dynamic_update_slice_in_dim(
            acc_v, lax.dynamic_slice_in_dim(acc_v, offset, WIN) + grad_v, offset, 0
        )
        return ((acc_k, acc_v), grad_q.astype(jnp.bfloat16))

    zeros = jnp.zeros((3 * events, width), jnp.float32)
    (acc_k, acc_v), grad_q = lax.scan(step_sums, (zeros, zeros), (q_blocks, g_blocks, my_starts))
    partial_sums = jnp.stack([acc_k, acc_v])
    from_above = shifted(partial_sums[:, :events], "seq", -1)
    from_below = shifted(partial_sums[:, 2 * events :], "seq", 1)
    total = (partial_sums[:, events : 2 * events] + from_above + from_below).astype(jnp.bfloat16)
    grad_keys = total[0]
    grad_values = total[1]
    return (grad_q.reshape(frames, width), grad_keys, grad_values)


def solution(mesh):
    return jax.shard_map(
        shards,
        mesh=mesh,
        in_specs=(
            P(("group", "seq"), "tp"),
            P(("group", "seq"), "tp"),
            P(("group", "seq"), "tp"),
            P(("group", "seq", "tp"), None),
            P("group"),
        ),
        out_specs=(P(("group", "seq"), "tp"), P(("group", "seq"), "tp"), P(("group", "seq"), "tp")),
        check_vma=False,
    )
```

profile of v0, /device:TPU:0, one launch (start us, length us, event | category | flops | bytes accessed | tf_op | source)
XLA Modules:
  0.0 756.6 jit_solution(12667970853552455492)
XLA Ops:
  0.6 2.9 copy.15
  3.5 3.9 copy.16
  7.5 4.0 pad_maximum_fusion.2
  11.4 1.3 collective-permute-start.1
  12.7 7.5 collective-permute-start
  20.2 0.7 copy.55
  20.9 3.4 all-to-all-start
  24.5 1.5 all-to-all-done
  26.1 81.1 %collective-permute-done.1 = bf16[2,1024,1024]{1,2,0:T(8,128)(2,1)} collective-permute-done((bf16[2,1024,1024]{1,2,0:T(8,128)(2,1)}, bf16[2,1024,1024]{1,2,0:T(8,128)(2,1)}, u32[]{:S(2)}, u32[]{:S(2)}) %collective-permute-start.1) | collective-permute-done | bytes 4194336 | tf_op jit(solution)/shard_map/ppermute | solution.py:23
  107.2 90.0 %collective-permute-done = bf16[2,1024,1024]{1,2,0:T(8,128)(2,1)} collective-permute-done((bf16[2,1024,1024]{1,2,0:T(8,128)(2,1)}, bf16[2,1024,1024]{1,2,0:T(8,128)(2,1)}, u32[]{:S(2)}, u32[]{:S(2)}) %collective-permute-start) | collective-permute-done | bytes 4194336 | tf_op jit(solution)/shard_map/ppermute | solution.py:21
  197.2 10.1 %pad_maximum_fusion = bf16[2,3072,1024]{1,2,0:T(8,128)(2,1)} fusion(bf16[2,1024,1024]{1,2,0:T(8,128)(2,1)} %collective-permute-done.1, bf16[1,1024,1024]{1,2,0:T(8,128)(2,1)} %bitcast.116, bf16[1,1024,1024]{1,2,0:T(8,128)(2,1)S(1)} %bitcast.114, bf16[2,1024,1024]{1,2,0:T(8,128)(2,1)} %collective-permute-done), kind=kLoop, calls=%fused_computation.31 | loop fusion | flops 50331648 | bytes 25165824 | tf_op jit(solution)/shard_map/concatenate | solution.py:19
  207.4 6.2 broadcast_in_dim.13.clone2
  213.6 6.1 broadcast_in_dim.13.clone
  219.7 151.2 %while.14 = (s32[]{:T(128)}, f32[3072,1024]{1,0:T(8,128)}, f32[3072,1024]{1,0:T(8,128)}, bf16[2,64,8,128]{3,2,1,0:T(8,128)(2,1)S(1)}, s32[2]{0:T(128)S(1)}, /*in...) while((s32[]{:T(128)}, f32[3072,1024]{1,0:T(8,128)}, ...), condition=%wide.region_4.5_spmd, body=%wide.region_0.4_spmd.sunk | while | flops 816577536 | bytes 191387888 | solution.py:91
  219.7 0.6 dynamic_slice.40
  220.9 8.7 %constant_dynamic-slice_fusion.9 = (f32[1024,1024]{1,0:T(8,128)}, f32[1024,1024]{1,0:T(8,128)}) fusion(f32[3072,1024]{1,0:T(8,128)} %get-tuple-element.185, s32[]{:T(128)S(6)} %select_n.6, f32[3072,1024]{1,0:T(8,128)} %get-tuple-element.184), kind=kLoop, calls=%fused_computation.19.clone.1 | loop fusion | bytes 16777220 | tf_op jit(solution)/shard_map/while/body/eval_jaxpr/dynamic_slice | solution.py:86
  229.6 5.3 copy.72
  235.0 5.4 copy.74
  240.3 5.6 fusion.44
  245.9 2.5 constant_dynamic-slice_fusion.10
  248.4 0.5 multiply_reduce_fusion.2
  249.0 0.5 exponential_reduce_fusion.2
  249.5 1.0 fusion.45
  250.5 0.9 multiply_convert_fusion.2
  251.4 0.9 fusion.48
  252.4 0.8 fusion.47
  253.2 0.4 copy-done.1
  253.6 2.9 bitcast_add_fusion.5
  256.5 5.4 copy.75
  261.9 0.7 fusion.46
  262.6 1.4 copy-done
  264.1 2.9 bitcast_add_fusion.4
  267.0 5.3 copy.73
  272.3 11.8 %dynamic_update_slice.15 = f32[3072,1024]{1,0:T(8,128)} dynamic-update-slice(f32[3072,1024]{1,0:T(8,128)} %get-tuple-element.184, f32[1024,1024]{1,0:T(8,128)} %copy.73, s32[]{:T(128)S(6)} %select_n.6, s32[]{:T(128)} %constant.13.clone.1..sunk) | dynamic-update-slice | bytes 8388612 | tf_op jit(solution)/shard_map/while/body/eval_jaxpr/dynamic_update_slice | solution.py:82
  284.1 11.8 %dynamic_update_slice.16 = f32[3072,1024]{1,0:T(8,128)} dynamic-update-slice(f32[3072,1024]{1,0:T(8,128)} %get-tuple-element.185, f32[1024,1024]{1,0:T(8,128)} %copy.75, s32[]{:T(128)S(6)} %select_n.6, s32[]{:T(128)} %constant.13.clone.1..sunk) | dynamic-update-slice | bytes 8388612 | tf_op jit(solution)/shard_map/while/body/eval_jaxpr/dynamic_update_slice | solution.py:85
  295.8 0.6 dynamic_slice.40
  297.1 8.7 %constant_dynamic-slice_fusion.9 = (f32[1024,1024]{1,0:T(8,128)}, f32[1024,1024]{1,0:T(8,128)}) fusion(f32[3072,1024]{1,0:T(8,128)} %get-tuple-element.185, s32[]{:T(128)S(6)} %select_n.6, f32[3072,1024]{1,0:T(8,128)} %get-tuple-element.184), kind=kLoop, calls=%fused_computation.19.clone.1 | loop fusion | bytes 16777220 | tf_op jit(solution)/shard_map/while/body/eval_jaxpr/dynamic_slice | solution.py:86
  305.8 5.3 copy.72
  311.1 5.4 copy.74
  316.5 5.6 fusion.44
  322.0 2.5 constant_dynamic-slice_fusion.10
  324.5 0.5 multiply_reduce_fusion.2
  325.1 0.5 exponential_reduce_fusion.2
  325.6 1.0 fusion.45
  326.6 0.9 multiply_convert_fusion.2
  327.5 0.9 fusion.48
  328.5 0.8 fusion.47
  329.7 2.9 bitcast_add_fusion.5
  332.6 5.4 copy.75
  338.0 0.7 fusion.46
  338.7 1.4 copy-done
  340.2 2.9 bitcast_add_fusion.4
  343.1 5.3 copy.73
  348.4 11.2 %dynamic_update_slice.15 = f32[3072,1024]{1,0:T(8,128)} dynamic-update-slice(f32[3072,1024]{1,0:T(8,128)} %get-tuple-element.184, f32[1024,1024]{1,0:T(8,128)} %copy.73, s32[]{:T(128)S(6)} %select_n.6, s32[]{:T(128)} %constant.13.clone.1..sunk) | dynamic-update-slice | bytes 8388612 | tf_op jit(solution)/shard_map/while/body/eval_jaxpr/dynamic_update_slice | solution.py:82
  359.6 11.2 %dynamic_update_slice.16 = f32[3072,1024]{1,0:T(8,128)} dynamic-update-slice(f32[3072,1024]{1,0:T(8,128)} %get-tuple-element.185, f32[1024,1024]{1,0:T(8,128)} %copy.75, s32[]{:T(128)S(6)} %select_n.6, s32[]{:T(128)} %constant.13.clone.1..sunk) | dynamic-update-slice | bytes 8388612 | tf_op jit(solution)/shard_map/while/body/eval_jaxpr/dynamic_update_slice | solution.py:85
  370.9 9.5 %fusion.11 = (f32[2,1024,1024]{2,1,0:T(8,128)}, f32[2,1024,1024]{2,1,0:T(8,128)S(1)}) fusion(f32[1,3072,1024]{2,1,0:T(8,128)} %bitcast.111, f32[1,3072,1024]{2,1,0:T(8,128)} %bitcast.107), kind=kLoop, calls=%fused_computation.32 | loop fusion | flops 4194304 | bytes 41943040 | tf_op jit(solution)/shard_map/stack | solution.py:92
  380.4 1.5 collective-permute-start.2
  381.9 8.4 %collective-permute-start.3 = (f32[2,1024,1024]{2,1,0:T(8,128)S(1)}, f32[2,1024,1024]{2,1,0:T(8,128)}, u32[]{:S(2)}, u32[]{:S(2)}) collective-permute-start(f32[2,1024,1024]{2,1,0:T(8,128)S(1)} %get-tuple-element.93), channel_id=1, source_target_pairs={{0,2},{2,4},{4,6},{6,8},{8,10},{10,12},{12,14},{1,3},{3,5},{5,7},{... | collective-permute-start | bytes 25165832 | tf_op jit(solution)/shard_map/ppermute | solution.py:33
  390.3 0.8 copy.54
  391.0 174.9 %collective-permute-done.2 = f32[2,1024,1024]{2,1,0:T(8,128)S(1)} collective-permute-done((f32[2,1024,1024]{2,1,0:T(8,128)}, f32[2,1024,1024]{2,1,0:T(8,128)S(1)}, u32[]{:S(2)}, u32[]{:S(2)}) %collective-permute-start.2) | collective-permute-done | bytes 8388640 | tf_op jit(solution)/shard_map/ppermute | solution.py:33
  566.0 3.2 copy-done.2
  569.2 176.6 %collective-permute-done.3 = f32[2,1024,1024]{2,1,0:T(8,128)} collective-permute-done((f32[2,1024,1024]{2,1,0:T(8,128)S(1)}, f32[2,1024,1024]{2,1,0:T(8,128)}, u32[]{:S(2)}, u32[]{:S(2)}) %collective-permute-start.3) | collective-permute-done | bytes 8388640 | tf_op jit(solution)/shard_map/ppermute | solution.py:33
  745.8 8.3 %fusion.15 = bf16[2,1024,1024]{2,1,0:T(8,128)(2,1)S(1)} fusion(f32[2,1024,1024]{2,1,0:T(8,128)} %collective-permute-done.3, f32[2,1024,1024]{2,1,0:T(8,128)} %copy-done.2, f32[1,3072,1024]{2,1,0:T(8,128)} %bitcast.112, f32[1,3072,1024]{2,1,0:T(8,128)S(1)} %bitcast.110), kind=kLoop, calls=%fused_computation.36 | loop fusion | flops 8388608 | bytes 46137344 | tf_op jit(solution)/shard_map/convert_element_type | solution.py:95
  754.1 2.4 slice_bitcast_fusion
  (29 shorter events, 0.9 us)
Async XLA Ops:
  7.4 12.8 %copy-start.3 = (bf16[64,2048]{1,0:T(8,128)(2,1)S(1)}, bf16[64,2048]{1,0:T(8,128)(2,1)}, u32[]{:S(2)}) copy-start(bf16[64,2048]{1,0:T(8,128)(2,1)} %param.10) | copy-start | bytes 786436
  7.4 16.9 %copy-start.4 = (bf16[128,1024]{1,0:T(8,128)(2,1)S(1)}, bf16[128,1024]{1,0:T(8,128)(2,1)}, u32[]{:S(2)}) copy-start(bf16[128,1024]{1,0:T(8,128)(2,1)} %param.7) | copy-start | bytes 786436
  7.4 18.5 %copy-start.5 = (s32[16]{0:T(128)S(1)}, s32[16]{0:T(128)}, u32[]{:S(2)}) copy-start(s32[16]{0:T(128)} %param.11) | copy-start | bytes 196
  11.4 95.7 %collective-permute-start.1 = (bf16[2,1024,1024]{1,2,0:T(8,128)(2,1)}, bf16[2,1024,1024]{1,2,0:T(8,128)(2,1)}, u32[]{:S(2)}, u32[]{:S(2)}) collective-permute-start(bf16[2,1024,1024]{1,2,0:T(8,128)(2,1)} %pad_maximum_fusion.2), channel_id=1, source_target_pairs={{2,0},{4,2},{6,4},{8,6},{10,8},{12,10},{14,12},{3,1},{5,3},{7,5},{... | collective-permute-start | bytes 12582920 | tf_op jit(solution)/shard_map/ppermute | solution.py:23
  12.7 184.5 %collective-permute-start = (bf16[2,1024,1024]{1,2,0:T(8,128)(2,1)}, bf16[2,1024,1024]{1,2,0:T(8,128)(2,1)}, u32[]{:S(2)}, u32[]{:S(2)}) collective-permute-start(bf16[2,1024,1024]{1,2,0:T(8,128)(2,1)} %pad_maximum_fusion.2), channel_id=1, source_target_pairs={{0,2},{2,4},{4,6},{6,8},{8,10},{10,12},{12,14},{1,3},{3,5},{5,7},{... | collective-permute-start | bytes 12582920 | tf_op jit(solution)/shard_map/ppermute | solution.py:21
  20.9 5.0 all-to-all-start
  251.4 2.2 copy-start.1
  261.9 2.2 copy-start
  327.5 2.2 copy-start.1
  338.0 2.2 copy-start
  370.9 374.9 %slice-start = ((s8[12582912]{0:T(1024)(128)(4,1)}), s8[4194304]{0:T(1024)(128)(4,1)S(1)}, s32[]{:S(2)}) async-start(s8[12582912]{0:T(1024)(128)(4,1)} %bitcast.108), calls=%async_computation.1 | async-start | bytes 8388608
  370.9 374.9 %slice-start.1 = ((s8[12582912]{0:T(1024)(128)(4,1)}), s8[4194304]{0:T(1024)(128)(4,1)S(1)}, s32[]{:S(2)}) async-start(s8[12582912]{0:T(1024)(128)(4,1)} %bitcast.108), calls=%async_computation.2 | async-start | bytes 8388608
  370.9 374.9 %slice-start.2 = ((s8[12582912]{0:T(1024)(128)(4,1)}), s8[4194304]{0:T(1024)(128)(4,1)S(1)}, s32[]{:S(2)}) async-start(s8[12582912]{0:T(1024)(128)(4,1)} %bitcast.108), calls=%async_computation.3 | async-start | bytes 8388608
  380.4 185.6 %collective-permute-start.2 = (f32[2,1024,1024]{2,1,0:T(8,128)}, f32[2,1024,1024]{2,1,0:T(8,128)S(1)}, u32[]{:S(2)}, u32[]{:S(2)}) collective-permute-start(f32[2,1024,1024]{2,1,0:T(8,128)} %get-tuple-element.92), channel_id=1, source_target_pairs={{2,0},{4,2},{6,4},{8,6},{10,8},{12,10},{14,12},{3,1},{5,3},{7,5},{... | collective-permute-start | bytes 25165832 | tf_op jit(solution)/shard_map/ppermute | solution.py:33
  381.9 363.9 %collective-permute-start.3 = (f32[2,1024,1024]{2,1,0:T(8,128)S(1)}, f32[2,1024,1024]{2,1,0:T(8,128)}, u32[]{:S(2)}, u32[]{:S(2)}) collective-permute-start(f32[2,1024,1024]{2,1,0:T(8,128)S(1)} %get-tuple-element.93), channel_id=1, source_target_pairs={{0,2},{2,4},{4,6},{6,8},{8,10},{10,12},{12,14},{1,3},{3,5},{5,7},{... | collective-permute-start | bytes 25165832 | tf_op jit(solution)/shard_map/ppermute | solution.py:33
  566.0 3.2 copy-start.2
where the time goes:
time: 761 us; the launch traced here: 757 us
  waiting for transfers between devices  524 us (69%)
  local copies, waits for them, and re-layouts  154 us (20%)
  other arithmetic  44.6 us (6%)
  starting transfers between devices  22.1 us (3%)
  matrix products  9.66 us (1%)
    ppermute x2, waiting for transfers between devices, shifted(): return lax.ppermute(array, axis, pairs)  352 us
    ppermute x1, waiting for transfers between devices, with_halo(): lax.ppermute(tail, axis, [(i, (i + 1) % count) for i in range(ends)])  90 us
    ppermute x1, waiting for transfers between devices, with_halo(): lax.ppermute(head, axis, [((i + 1) % count, i) for i in range(ends)])  81.1 us
    dynamic_update_slice x4, local copies, waits for them, and re-layouts, step_sums(): lax.dynamic_update_slice_in_dim(acc_v, lax.dynamic_slice_in_dim(acc_v, of...  33.8 us
    dynamic_update_slice x4, local copies, waits for them, and re-layouts, step_sums(): lax.dynamic_update_slice_in_dim(acc_k, lax.dynamic_slice_in_dim(acc_k, of...  33.6 us
    dynamic_slice x4, local copies, waits for them, and re-layouts, step_sums(): lax.dynamic_slice_in_dim(acc_v, offset, WIN) + grad_v  28.1 us
  transfers between devices with their start and end apart: 5, of which 5 were waited for; matrix products, arithmetic and copies ran while one was open for 0% of the time, Pallas kernels for 0%

commit v1 on v0

v1 whole, which is shorter than its diff:
```python
import functools
import math

import jax
import jax.numpy as jnp
from jax import lax
from jax.experimental import pallas as pl
from jax.experimental.pallas import tpu as pltpu
from jax.sharding import PartitionSpec as P

HD = 128
WIN = 1024
BLK = 64
PAIR = 2 * HD
SCALE = 1.0 / math.sqrt(HD)
LOG2E = math.log2(math.e)


def diagonal(rows):
    zeros = jnp.zeros((BLK, HD), rows.dtype)
    top = jnp.concatenate([rows[:, :HD], zeros], axis=1)
    low = jnp.concatenate([zeros, rows[:, HD:]], axis=1)
    return jnp.concatenate([top, low], axis=0)


def attend_kernel(q_ref, g_ref, k_ref, v_ref, gq_ref, p_ref, ds_ref):
    keys = k_ref[...]
    last = (((1,), (1,)), ((), ()))
    scores = lax.dot_general(keys, diagonal(q_ref[...]), last, preferred_element_type=jnp.float32)
    dprobs = lax.dot_general(v_ref[...], diagonal(g_ref[...]), last, preferred_element_type=jnp.float32)
    top = jnp.max(scores, axis=0, keepdims=True)
    grown = jnp.exp2((scores - top) * (SCALE * LOG2E))
    probs = grown * (1.0 / jnp.sum(grown, axis=0, keepdims=True))
    probs_low = probs.astype(jnp.bfloat16)
    p_ref[...] = probs_low
    delta = jnp.sum(probs_low.astype(jnp.float32) * dprobs, axis=0, keepdims=True)
    dscores = (SCALE * probs * (dprobs - delta)).astype(jnp.bfloat16)
    ds_ref[...] = dscores
    both = lax.dot_general(dscores, keys, (((0,), (0,)), ((), ())), preferred_element_type=jnp.float32)
    gq_ref[:, :HD] = both[:BLK, :HD].astype(jnp.bfloat16)
    gq_ref[:, HD:] = both[BLK:, HD:].astype(jnp.bfloat16)


def attend(q_blk, g_blk, keys, values):
    width = q_blk.shape[1]
    steps = width // PAIR
    blk = pl.BlockSpec((BLK, PAIR), lambda i: (0, i))
    win = pl.BlockSpec((WIN, PAIR), lambda i: (0, i))
    prob = pl.BlockSpec((WIN, 2 * BLK), lambda i: (0, i))
    staged = jax.ShapeDtypeStruct((WIN, steps * 2 * BLK), jnp.bfloat16)
    return pl.pallas_call(
        attend_kernel,
        grid=(steps,),
        in_specs=[blk, blk, win, win],
        out_specs=[blk, prob, prob],
        out_shape=[jax.ShapeDtypeStruct((BLK, width), jnp.bfloat16), staged, staged],
        compiler_params=pltpu.CompilerParams(vmem_limit_bytes=32 << 20),
        cost_estimate=pl.CostEstimate(
            flops=8 * BLK * WIN * width, bytes_accessed=6 * WIN * width, transcendentals=BLK * WIN * width // HD
        ),
        name="attend",
    )(q_blk, g_blk, keys, values)


def event_kernel(p0_ref, ds0_ref, q0_ref, g0_ref, p1_ref, ds1_ref, q1_ref, g1_ref, gk_ref, gv_ref):
    def product(a0, a1, b0, b1):
        left = jnp.concatenate([a0[...], a1[...]], axis=1)
        right = jnp.concatenate([diagonal(b0[...]), diagonal(b1[...])], axis=0)
        return jnp.dot(left, right, preferred_element_type=jnp.float32).astype(jnp.bfloat16)

    gk_ref[...] = product(ds0_ref, ds1_ref, q0_ref, q1_ref)
    gv_ref[...] = product(p0_ref, p1_ref, g0_ref, g1_ref)


def event_grads(first, second):
    width = first[2].shape[1]
    steps = width // PAIR
    blk = pl.BlockSpec((BLK, PAIR), lambda i: (0, i))
    win = pl.BlockSpec((WIN, PAIR), lambda i: (0, i))
    prob = pl.BlockSpec((WIN, 2 * BLK), lambda i: (0, i))
    out = jax.ShapeDtypeStruct((WIN, width), jnp.bfloat16)
    return pl.pallas_call(
        event_kernel,
        grid=(steps,),
        in_specs=[prob, prob, blk, blk] * 2,
        out_specs=[win, win],
        out_shape=[out, out],
        compiler_params=pltpu.CompilerParams(vmem_limit_bytes=32 << 20),
        cost_estimate=pl.CostEstimate(
            flops=8 * BLK * WIN * width, bytes_accessed=8 * WIN * width, transcendentals=0
        ),
        name="event_grads",
    )(*first, *second)


def shards(queries, keys, values, out_grad, starts):
    del starts
    seq = lax.axis_size("seq")
    frames, width = queries.shape
    assert frames == 2 * BLK and keys.shape[0] == WIN and seq % 2 == 0
    inside = [(i, i ^ 1) for i in range(seq)]
    across = [(0, 0), (seq - 1, seq - 1)] + [(i, i + 1 if i % 2 else i - 1) for i in range(1, seq - 1)]
    even = lax.axis_index("seq") % 2 == 0
    core = lax.axis_index("tp")

    q_in = lax.dynamic_slice_in_dim(queries, jnp.where(even, BLK, 0), BLK, axis=0)
    q_out = lax.dynamic_slice_in_dim(queries, jnp.where(even, 0, BLK), BLK, axis=0)
    mine = lax.dynamic_slice_in_dim(out_grad, core * width, width, axis=1)
    other = lax.dynamic_slice_in_dim(out_grad, (1 - core) * width, width, axis=1)
    other = lax.ppermute(other, "tp", [(0, 1), (1, 0)])
    own_inside = even == (core == 1)
    g_in = jnp.where(own_inside, mine, other)
    g_out = jnp.where(own_inside, other, mine)

    q0 = lax.ppermute(q_in, "seq", inside)
    g0 = lax.ppermute(g_in, "seq", inside)
    q1 = lax.ppermute(q_out, "seq", across)
    g1 = lax.ppermute(g_out, "seq", across)
    gq0, p0, ds0 = attend(q0, g0, keys, values)
    back0 = lax.ppermute(gq0, "seq", inside)
    gq1, p1, ds1 = attend(q1, g1, keys, values)
    back1 = lax.ppermute(gq1, "seq", across)
    grad_keys, grad_values = event_grads((p0, ds0, q0, g0), (p1, ds1, q1, g1))
    grad_queries = jnp.concatenate([jnp.where(even, back1, back0), jnp.where(even, back0, back1)], axis=0)
    return grad_queries, grad_keys, grad_values


def solution(mesh):
    return jax.shard_map(
        shards,
        mesh=mesh,
        in_specs=(
            P(("group", "seq"), "tp"),
            P(("group", "seq"), "tp"),
            P(("group", "seq"), "tp"),
            P(("group", "seq", "tp"), None),
            P("group"),
        ),
        out_specs=(P(("group", "seq"), "tp"), P(("group", "seq"), "tp"), P(("group", "seq"), "tp")),
        check_vma=False,
    )
```

time: 761 us -> 40.1 us (0.05)
  the two profiles are of different devices: /device:TPU:0 before, /device:TPU:20 now
where the time goes in v1:
time: 40.1 us; the launch traced here: 39.8 us
  starting transfers between devices  15.3 us (38%)
  Pallas kernels  14.4 us (36%)
  local copies, waits for them, and re-layouts  5.09 us (13%)
  waiting for transfers between devices  2.56 us (6%)
  other arithmetic  1.69 us (4%)
  between operations  0.74 us (2%)
    pallas_call x2, Pallas kernels, attend(): pl.pallas_call(attend_kernel, grid=(steps,), in_specs=[blk, blk, win, win...  10.5 us
    pallas_call x1, Pallas kernels, event_grads(): pl.pallas_call(event_kernel, grid=(steps,), in_specs=[prob, prob, blk, bl...  3.94 us
    ppermute x1, starting transfers between devices, shards(): q1 = lax.ppermute(q_out, 'seq', across)  3.42 us
    ppermute x1, starting transfers between devices, shards(): back0 = lax.ppermute(gq0, 'seq', inside)  3.38 us
    ppermute x1, starting transfers between devices, shards(): g1 = lax.ppermute(g_out, 'seq', across)  3.31 us
    unnamed x6, local copies, waits for them, and re-layouts  3.19 us
    ppermute x1, starting transfers between devices, shards(): back1 = lax.ppermute(gq1, 'seq', across)  2.95 us
    ppermute x1, waiting for transfers between devices, shards(): g0 = lax.ppermute(g_in, 'seq', inside)  1.69 us
  transfers between devices with their start and end apart: 7, of which 2 were waited for; matrix products, arithmetic and copies ran while one was open for 5% of the time, Pallas kernels for 36%

profile of v1, /device:TPU:20, one launch (start us, length us, event | category | flops | bytes accessed | tf_op | source)
XLA Modules:
  0.0 39.8 jit_solution(2889446075950491289)
XLA Ops:
  0.6 0.9 %constant_dynamic-slice_fusion.1 = bf16[64,1024]{1,0:T(8,128)(2,1)S(1)} fusion(bf16[64,2048]{1,0:T(8,128)(2,1)} %param.8, s32[]{:T(128)S(6)} %select_n.48), kind=kLoop, calls=%fused_computation.6 | loop fusion | bytes 262148 | tf_op jit(solution)/shard_map/dynamic_slice | solution.py:109
  1.6 0.1 collective-permute-start.1
  1.7 1.0 %constant_dynamic-slice_fusion.2 = (bf16[64,1024]{1,0:T(8,128)(2,1)S(1)}, bf16[64,1024]{1,0:T(8,128)(2,1)S(1)}) fusion(bf16[128,1024]{1,0:T(8,128)(2,1)} %param.5, s32[]{:T(128)S(6)} %select_n.46, s32[]{:T(128)S(6)} %select_n.51), kind=kLoop, calls=%fused_computation.7 | loop fusion | bytes 524296 | tf_op jit(solution)/shard_map/dynamic_slice | solution.py:107
  2.6 0.6 %collective-permute-start.4 = (bf16[64,1024]{1,0:T(8,128)(2,1)S(1)}, bf16[64,1024]{1,0:T(8,128)(2,1)S(1)}, u32[]{:S(2)}, u32[]{:S(2)}) collective-permute-start(bf16[64,1024]{1,0:T(8,128)(2,1)S(1)} %get-tuple-element.24), channel_id=1, source_target_pairs={{0,2},{2,0},{4,6},{6,4},{8,10},{10,8},{12,14},{14,12},{1,3},{3,1},... | collective-permute-start | bytes 393224 | tf_op jit(solution)/shard_map/ppermute | solution.py:115
  3.2 0.0 collective-permute-done.1
  3.2 1.0 %broadcast_select_fusion.1 = (bf16[64,1024]{1,0:T(8,128)(2,1)S(1)}, bf16[64,1024]{1,0:T(8,128)(2,1)S(1)}) fusion(bf16[64,1024]{1,0:T(8,128)(2,1)S(1)} %collective-permute-done.1, pred[]{:T(512)S(6)} %eq.13, bf16[64,2048]{1,0:T(8,128)(2,1)} %param.8, s32[]{:T(128)S(6)} %select_n.49), kind=kLoop, calls=%fused_computation.2 | loop fusion | flops 131072 | bytes 524293 | tf_op jit(solution)/shard_map/jit(_where)/select_n | solution.py:113
  4.2 1.6 %collective-permute-start.5 = (bf16[64,1024]{1,0:T(8,128)(2,1)S(1)}, bf16[64,1024]{1,0:T(8,128)(2,1)S(1)}, u32[]{:S(2)}, u32[]{:S(2)}) collective-permute-start(bf16[64,1024]{1,0:T(8,128)(2,1)S(1)} %get-tuple-element.20), channel_id=1, source_target_pairs={{0,2},{2,0},{4,6},{6,4},{8,10},{10,8},{12,14},{14,12},{1,3},{3,1},... | collective-permute-start | bytes 393224 | tf_op jit(solution)/shard_map/ppermute | solution.py:116
  5.8 3.4 %collective-permute-start = (bf16[64,1024]{1,0:T(8,128)(2,1)S(1)}, bf16[64,1024]{1,0:T(8,128)(2,1)S(1)}, u32[]{:S(2)}, u32[]{:S(2)}) collective-permute-start(bf16[64,1024]{1,0:T(8,128)(2,1)S(1)} %get-tuple-element.23), channel_id=1, source_target_pairs={{0,0},{14,14},{2,4},{4,2},{6,8},{8,6},{10,12},{12,10},{1,1},{15,15... | collective-permute-start | bytes 393224 | tf_op jit(solution)/shard_map/ppermute | solution.py:117
  9.2 3.3 %collective-permute-start.2 = (bf16[64,1024]{1,0:T(8,128)(2,1)S(1)}, bf16[64,1024]{1,0:T(8,128)(2,1)S(1)}, u32[]{:S(2)}, u32[]{:S(2)}) collective-permute-start(bf16[64,1024]{1,0:T(8,128)(2,1)S(1)} %get-tuple-element.19), channel_id=1, source_target_pairs={{0,0},{14,14},{2,4},{4,2},{6,8},{8,6},{10,12},{12,10},{1,1},{15,15... | collective-permute-start | bytes 393224 | tf_op jit(solution)/shard_map/ppermute | solution.py:118
  12.5 0.0 collective-permute-done.4.q_ref.q0_ref
  12.5 1.7 %collective-permute-done.5.g_ref.g0_ref = bf16[64,1024]{1,0:T(8,128)(2,1)S(1)} collective-permute-done((bf16[64,1024]{1,0:T(8,128)(2,1)S(1)}, bf16[64,1024]{1,0:T(8,128)(2,1)S(1)}, u32[]{:S(2)}, u32[]{:S(2)}) %collective-permute-start.5) | collective-permute-done | bytes 131104 | tf_op jit(solution)/shard_map/ppermute | solution.py:116
  14.2 0.0 copy-start
  14.2 1.6 %copy-done = bf16[1024,1024]{1,0:T(8,128)(2,1)S(1)} copy-done((bf16[1024,1024]{1,0:T(8,128)(2,1)S(1)}, bf16[1024,1024]{1,0:T(8,128)(2,1)}, u32[]{:S(2)}) %copy-start) | copy-done | bytes 2097176
  15.8 0.0 copy-start.2
  15.8 1.6 %copy-done.2 = bf16[1024,1024]{1,0:T(8,128)(2,1)S(1)} copy-done((bf16[1024,1024]{1,0:T(8,128)(2,1)S(1)}, bf16[1024,1024]{1,0:T(8,128)(2,1)}, u32[]{:S(2)}) %copy-start.2) | copy-done | bytes 2097176
  17.4 0.0 copy-start.1
  17.4 5.2 %attend.3 = (bf16[64,1024]{1,0:T(8,128)(2,1)S(1)}, bf16[1024,512]{1,0:T(8,128)(2,1)S(1)}, bf16[1024,512]{1,0:T(8,128)(2,1)S(1)}) custom-call(bf16[64,1024]{1,0:T(8,128)(2,1)S(1)} %collective-permute-done.4.q_ref.q0_ref, bf16[64,1024]{1,0:T(8,128)(2,1)S(1)} %collective-permute-done.5.g_ref.g0_ref, bf16[1024,1024]{1,0:T(8,128)(2,1)S(1)} %copy-done, ...), custom_call_target="tpu_custom_call" | custom-call | flops 536870912 | bytes 6291456 | tf_op jit(solution)/shard_map/attend/pallas_call | solution.py:51
  22.6 3.4 %collective-permute-start.6 = (bf16[64,1024]{1,0:T(8,128)(2,1)S(1)}, bf16[64,1024]{1,0:T(8,128)(2,1)S(1)}, u32[]{:S(2)}, u32[]{:S(2)}) collective-permute-start(bf16[64,1024]{1,0:T(8,128)(2,1)S(1)} %get-tuple-element.12), channel_id=1, source_target_pairs={{0,2},{2,0},{4,6},{6,4},{8,10},{10,8},{12,14},{14,12},{1,3},{3,1},... | collective-permute-start | bytes 393224 | tf_op jit(solution)/shard_map/ppermute | solution.py:120
  26.0 0.0 collective-permute-done.q_ref.q1_ref
  26.0 0.0 collective-permute-done.2.g_ref.g1_ref
  26.0 0.0 copy-done.1
  26.0 5.2 %attend.2 = (bf16[64,1024]{1,0:T(8,128)(2,1)S(1)}, bf16[1024,512]{1,0:T(8,128)(2,1)S(1)}, bf16[1024,512]{1,0:T(8,128)(2,1)S(1)}) custom-call(bf16[64,1024]{1,0:T(8,128)(2,1)S(1)} %collective-permute-done.q_ref.q1_ref, bf16[64,1024]{1,0:T(8,128)(2,1)S(1)} %collective-permute-done.2.g_ref.g1_ref, bf16[1024,1024]{1,0:T(8,128)(2,1)S(1)} %copy-done.1, ...), custom_call_target="tpu_custom_call" | custom-call | flops 536870912 | bytes 6291456 | tf_op jit(solution)/shard_map/attend/pallas_call | solution.py:51
  31.3 3.0 %collective-permute-start.3 = (bf16[64,1024]{1,0:T(8,128)(2,1)S(1)}, bf16[64,1024]{1,0:T(8,128)(2,1)S(1)}, u32[]{:S(2)}, u32[]{:S(2)}) collective-permute-start(bf16[64,1024]{1,0:T(8,128)(2,1)S(1)} %get-tuple-element.11), channel_id=1, source_target_pairs={{0,0},{14,14},{2,4},{4,2},{6,8},{8,6},{10,12},{12,10},{1,1},{15,15... | collective-permute-start | bytes 393224 | tf_op jit(solution)/shard_map/ppermute | solution.py:122
  34.2 3.9 %event_grads.1 = (bf16[1024,1024]{1,0:T(8,128)(2,1)}, bf16[1024,1024]{1,0:T(8,128)(2,1)}) custom-call(bf16[1024,512]{1,0:T(8,128)(2,1)S(1)} %get-tuple-element.13.p0_ref, bf16[1024,512]{1,0:T(8,128)(2,1)S(1)} %get-tuple-element.14.ds0_ref, bf16[64,1024]{1,0:T(8,128)(2,1)S(1)} %collective-permute-done.4.q_ref.q0_ref, ...), custom_call_target="tpu_custom_call" | custom-call | flops 536870912 | bytes 8388608 | tf_op jit(solution)/shard_map/event_grads/pallas_call | solution.py:82
  38.2 0.0 collective-permute-done.6
  38.2 0.9 %collective-permute-done.3 = bf16[64,1024]{1,0:T(8,128)(2,1)S(1)} collective-permute-done((bf16[64,1024]{1,0:T(8,128)(2,1)S(1)}, bf16[64,1024]{1,0:T(8,128)(2,1)S(1)}, u32[]{:S(2)}, u32[]{:S(2)}) %collective-permute-start.3) | collective-permute-done | bytes 131104 | tf_op jit(solution)/shard_map/ppermute | solution.py:122
  39.1 0.7 %pad_maximum_fusion = bf16[128,1024]{1,0:T(8,128)(2,1)} fusion(bf16[64,1024]{1,0:T(8,128)(2,1)S(1)} %get-tuple-element.22, bf16[64,1024]{1,0:T(8,128)(2,1)S(1)} %get-tuple-element.21), kind=kLoop, calls=%fused_computation | loop fusion | flops 524288 | bytes 524288 | tf_op jit(solution)/shard_map/concatenate | solution.py:124
  (1 shorter events, 0.0 us)
Async XLA Ops:
  1.6 1.7 %collective-permute-start.1 = (bf16[64,1024]{1,0:T(8,128)(2,1)S(1)}, bf16[64,1024]{1,0:T(8,128)(2,1)S(1)}, u32[]{:S(2)}, u32[]{:S(2)}) collective-permute-start(bf16[64,1024]{1,0:T(8,128)(2,1)S(1)} %constant_dynamic-slice_fusion.1), channel_id=1, source_target_pairs={{0,1},{1,0},{2,3},{3,2},{4,5},{5,4},{6,7},{7,6},{8,9},{9,8},{10,11... | collective-permute-start | bytes 393224 | tf_op jit(solution)/shard_map/ppermute | solution.py:110
  2.6 9.9 %collective-permute-start.4 = (bf16[64,1024]{1,0:T(8,128)(2,1)S(1)}, bf16[64,1024]{1,0:T(8,128)(2,1)S(1)}, u32[]{:S(2)}, u32[]{:S(2)}) collective-permute-start(bf16[64,1024]{1,0:T(8,128)(2,1)S(1)} %get-tuple-element.24), channel_id=1, source_target_pairs={{0,2},{2,0},{4,6},{6,4},{8,10},{10,8},{12,14},{14,12},{1,3},{3,1},... | collective-permute-start | bytes 393224 | tf_op jit(solution)/shard_map/ppermute | solution.py:115
  4.2 10.0 %collective-permute-start.5 = (bf16[64,1024]{1,0:T(8,128)(2,1)S(1)}, bf16[64,1024]{1,0:T(8,128)(2,1)S(1)}, u32[]{:S(2)}, u32[]{:S(2)}) collective-permute-start(bf16[64,1024]{1,0:T(8,128)(2,1)S(1)} %get-tuple-element.20), channel_id=1, source_target_pairs={{0,2},{2,0},{4,6},{6,4},{8,10},{10,8},{12,14},{14,12},{1,3},{3,1},... | collective-permute-start | bytes 393224 | tf_op jit(solution)/shard_map/ppermute | solution.py:116
  5.8 20.3 %collective-permute-start = (bf16[64,1024]{1,0:T(8,128)(2,1)S(1)}, bf16[64,1024]{1,0:T(8,128)(2,1)S(1)}, u32[]{:S(2)}, u32[]{:S(2)}) collective-permute-start(bf16[64,1024]{1,0:T(8,128)(2,1)S(1)} %get-tuple-element.23), channel_id=1, source_target_pairs={{0,0},{14,14},{2,4},{4,2},{6,8},{8,6},{10,12},{12,10},{1,1},{15,15... | collective-permute-start | bytes 393224 | tf_op jit(solution)/shard_map/ppermute | solution.py:117
  9.2 16.8 %collective-permute-start.2 = (bf16[64,1024]{1,0:T(8,128)(2,1)S(1)}, bf16[64,1024]{1,0:T(8,128)(2,1)S(1)}, u32[]{:S(2)}, u32[]{:S(2)}) collective-permute-start(bf16[64,1024]{1,0:T(8,128)(2,1)S(1)} %get-tuple-element.19), channel_id=1, source_target_pairs={{0,0},{14,14},{2,4},{4,2},{6,8},{8,6},{10,12},{12,10},{1,1},{15,15... | collective-permute-start | bytes 393224 | tf_op jit(solution)/shard_map/ppermute | solution.py:118
  14.2 1.6 %copy-start = (bf16[1024,1024]{1,0:T(8,128)(2,1)S(1)}, bf16[1024,1024]{1,0:T(8,128)(2,1)}, u32[]{:S(2)}) copy-start(bf16[1024,1024]{1,0:T(8,128)(2,1)} %k_ref.3) | copy-start | bytes 6291460
  15.8 1.6 %copy-start.2 = (bf16[1024,1024]{1,0:T(8,128)(2,1)S(1)}, bf16[1024,1024]{1,0:T(8,128)(2,1)}, u32[]{:S(2)}) copy-start(bf16[1024,1024]{1,0:T(8,128)(2,1)} %v_ref.3) | copy-start | bytes 6291460
  17.4 8.6 %copy-start.1 = (bf16[1024,1024]{1,0:T(8,128)(2,1)S(1)}, bf16[1024,1024]{1,0:T(8,128)(2,1)}, u32[]{:S(2)}) copy-start(bf16[1024,1024]{1,0:T(8,128)(2,1)} %k_ref.3) | copy-start | bytes 6291460
  22.6 15.6 %collective-permute-start.6 = (bf16[64,1024]{1,0:T(8,128)(2,1)S(1)}, bf16[64,1024]{1,0:T(8,128)(2,1)S(1)}, u32[]{:S(2)}, u32[]{:S(2)}) collective-permute-start(bf16[64,1024]{1,0:T(8,128)(2,1)S(1)} %get-tuple-element.12), channel_id=1, source_target_pairs={{0,2},{2,0},{4,6},{6,4},{8,10},{10,8},{12,14},{14,12},{1,3},{3,1},... | collective-permute-start | bytes 393224 | tf_op jit(solution)/shard_map/ppermute | solution.py:120
  31.3 7.8 %collective-permute-start.3 = (bf16[64,1024]{1,0:T(8,128)(2,1)S(1)}, bf16[64,1024]{1,0:T(8,128)(2,1)S(1)}, u32[]{:S(2)}, u32[]{:S(2)}) collective-permute-start(bf16[64,1024]{1,0:T(8,128)(2,1)S(1)} %get-tuple-element.11), channel_id=1, source_target_pairs={{0,0},{14,14},{2,4},{4,2},{6,8},{8,6},{10,12},{12,10},{1,1},{15,15... | collective-permute-start | bytes 393224 | tf_op jit(solution)/shard_map/ppermute | solution.py:122

commit v2 on v1

v2 whole, which is shorter than its diff:
```python
import math

import jax
import jax.numpy as jnp
from jax import lax
from jax.experimental import pallas as pl
from jax.experimental.pallas import tpu as pltpu
from jax.sharding import PartitionSpec as P

HD = 128
WIN = 1024
BLK = 64
PAIR = 2 * HD
SCALE = 1.0 / math.sqrt(HD)
LOG2E = math.log2(math.e)
LAST = (((1,), (1,)), ((), ()))
FIRST = (((0,), (0,)), ((), ()))
WHOLE = pl.BlockSpec(memory_space=pltpu.VMEM)
RAW = pl.BlockSpec(memory_space=pltpu.HBM)


def params(mib):
    return pltpu.CompilerParams(vmem_limit_bytes=mib << 20)


def diagonal(rows):
    zeros = jnp.zeros((BLK, HD), rows.dtype)
    top = jnp.concatenate([rows[:, :HD], zeros], axis=1)
    low = jnp.concatenate([zeros, rows[:, HD:]], axis=1)
    return jnp.concatenate([top, low], axis=0)


def pack_kernel(q_ref, own_ref, other_ref, inside_ref, across_ref):
    width = q_ref.shape[1]
    odd = lax.axis_index("seq") % 2
    core = lax.axis_index("tp")
    cols = pl.ds(pl.multiple_of(core * width, HD), width)
    inside_ref[:BLK] = q_ref[pl.ds(pl.multiple_of((1 - odd) * BLK, BLK), BLK), :]
    across_ref[:BLK] = q_ref[pl.ds(pl.multiple_of(odd * BLK, BLK), BLK), :]

    @pl.when(core != odd)
    def _():
        inside_ref[BLK:] = own_ref[:, cols]
        across_ref[BLK:] = other_ref[:, cols]

    @pl.when(core == odd)
    def _():
        inside_ref[BLK:] = other_ref[:, cols]
        across_ref[BLK:] = own_ref[:, cols]


def pack(queries, own, other):
    part = jax.ShapeDtypeStruct(queries.shape, queries.dtype)
    return pl.pallas_call(
        pack_kernel,
        in_specs=[WHOLE] * 3,
        out_specs=[WHOLE] * 2,
        out_shape=[part] * 2,
        compiler_params=params(8),
        name="pack",
    )(queries, own, other)


def stage_kernel(k_hbm, v_hbm, k_ref, v_ref, sems):
    rows = WIN // 4
    moves = []
    for i in range(4):
        part = pl.ds(i * rows, rows)
        moves.append(pltpu.make_async_copy(k_hbm.at[part, :], k_ref.at[part, :], sems.at[0, i]))
        moves.append(pltpu.make_async_copy(v_hbm.at[part, :], v_ref.at[part, :], sems.at[1, i]))
    for move in moves:
        move.start()
    for move in moves:
        move.wait()


def stage(keys, values):
    part = jax.ShapeDtypeStruct(keys.shape, keys.dtype)
    return pl.pallas_call(
        stage_kernel,
        in_specs=[RAW] * 2,
        out_specs=[WHOLE] * 2,
        out_shape=[part] * 2,
        scratch_shapes=[pltpu.SemaphoreType.DMA((2, 4))],
        compiler_params=params(16),
        cost_estimate=pl.CostEstimate(flops=0, bytes_accessed=8 * keys.size, transcendentals=0),
        name="stage",
    )(keys, values)


def attend_kernel(m_ref, k_ref, v_ref, gq_ref, p_ref, ds_ref):
    pairs = m_ref.shape[1] // PAIR
    held = {}

    def products(j):
        cols = pl.ds(j * PAIR, PAIR)
        scores = lax.dot_general(
            k_ref[:, cols], diagonal(m_ref[:BLK, cols]), LAST, preferred_element_type=jnp.float32
        )
        dprobs = lax.dot_general(
            v_ref[:, cols], diagonal(m_ref[BLK:, cols]), LAST, preferred_element_type=jnp.float32
        )
        held[j] = (scores, jnp.max(scores, axis=0, keepdims=True), dprobs)

    def sums(j):
        scores, top, dprobs = held[j]
        grown = jnp.exp2((scores - top) * (SCALE * LOG2E))
        inverse = 1.0 / jnp.sum(grown, axis=0, keepdims=True)
        delta = jnp.sum(grown * dprobs, axis=0, keepdims=True) * inverse
        held[j] = (grown, inverse, dprobs, delta)

    def results(j):
        grown, inverse, dprobs, delta = held.pop(j)
        cols = pl.ds(j * 2 * BLK, 2 * BLK)
        p_ref[:, cols] = (grown * inverse).astype(jnp.bfloat16)
        dscores = (grown * (SCALE * inverse) * (dprobs - delta)).astype(jnp.bfloat16)
        ds_ref[:, cols] = dscores
        both = lax.dot_general(
            dscores, k_ref[:, pl.ds(j * PAIR, PAIR)], FIRST, preferred_element_type=jnp.float32
        )
        gq_ref[:, pl.ds(j * PAIR, HD)] = both[:BLK, :HD].astype(jnp.bfloat16)
        gq_ref[:, pl.ds(j * PAIR + HD, HD)] = both[BLK:, HD:].astype(jnp.bfloat16)

    for step in range(pairs + 2):
        for stage_of, lag in ((products, 0), (sums, 1), (results, 2)):
            if 0 <= step - lag < pairs:
                stage_of(step - lag)


def attend(message, keys, values):
    width = message.shape[1]
    staged = jax.ShapeDtypeStruct((WIN, width // HD * BLK), jnp.bfloat16)
    return pl.pallas_call(
        attend_kernel,
        in_specs=[WHOLE] * 3,
        out_specs=[WHOLE] * 3,
        out_shape=[jax.ShapeDtypeStruct((BLK, width), jnp.bfloat16), staged, staged],
        compiler_params=params(32),
        cost_estimate=pl.CostEstimate(
            flops=8 * BLK * WIN * width, bytes_accessed=6 * WIN * width, transcendentals=BLK * WIN * width // HD
        ),
        name="attend",
    )(message, keys, values)


def event_kernel(p0_ref, ds0_ref, m0_ref, p1_ref, ds1_ref, m1_ref, gk_ref, gv_ref):
    step = pl.program_id(0)
    probs = pl.ds(pl.multiple_of(step * 2 * BLK, 2 * BLK), 2 * BLK)
    cols = pl.ds(pl.multiple_of(step * PAIR, PAIR), PAIR)

    def product(a0, a1, b0, b1):
        left = jnp.concatenate([a0, a1], axis=1)
        right = jnp.concatenate([diagonal(b0), diagonal(b1)], axis=0)
        return jnp.dot(left, right, preferred_element_type=jnp.float32).astype(jnp.bfloat16)

    gk_ref[...] = product(ds0_ref[:, probs], ds1_ref[:, probs], m0_ref[:BLK, cols], m1_ref[:BLK, cols])
    gv_ref[...] = product(p0_ref[:, probs], p1_ref[:, probs], m0_ref[BLK:, cols], m1_ref[BLK:, cols])


def event_grads(*args):
    width = args[2].shape[1]
    win = pl.BlockSpec((WIN, PAIR), lambda i: (0, i))
    out = jax.ShapeDtypeStruct((WIN, width), jnp.bfloat16)
    return pl.pallas_call(
        event_kernel,
        grid=(width // PAIR,),
        in_specs=[WHOLE] * 6,
        out_specs=[win, win],
        out_shape=[out, out],
        compiler_params=params(32),
        cost_estimate=pl.CostEstimate(
            flops=8 * BLK * WIN * width, bytes_accessed=8 * WIN * width, transcendentals=0
        ),
        name="event_grads",
    )(*args)


def join_kernel(inside_ref, across_ref, out_hbm, sems):
    odd = lax.axis_index("seq") % 2
    moves = [
        pltpu.make_async_copy(
            ref, out_hbm.at[pl.ds(pl.multiple_of(row * BLK, BLK), BLK), :], sems.at[i]
        )
        for i, (ref, row) in enumerate(((inside_ref, 1 - odd), (across_ref, odd)))
    ]
    for move in moves:
        move.start()
    for move in moves:
        move.wait()


def join(back_inside, back_across):
    width = back_inside.shape[1]
    return pl.pallas_call(
        join_kernel,
        in_specs=[WHOLE] * 2,
        out_specs=RAW,
        out_shape=jax.ShapeDtypeStruct((2 * BLK, width), back_inside.dtype),
        scratch_shapes=[pltpu.SemaphoreType.DMA((2,))],
        compiler_params=params(8),
        name="join",
    )(back_inside, back_across)


def shards(queries, keys, values, out_grad, starts):
    del starts
    seq = lax.axis_size("seq")
    frames, width = queries.shape
    assert frames == 2 * BLK and keys.shape[0] == WIN and seq % 2 == 0
    inside = [(i, i ^ 1) for i in range(seq)]
    across = [(0, 0), (seq - 1, seq - 1)] + [(i, i + 1 if i % 2 else i - 1) for i in range(1, seq - 1)]

    other = lax.ppermute(out_grad, "tp", [(0, 1), (1, 0)])
    first, second = pack(queries, out_grad, other)
    first = lax.ppermute(first, "seq", inside)
    second = lax.ppermute(second, "seq", across)
    keys, values = stage(keys, values)
    gq0, p0, ds0 = attend(first, keys, values)
    back0 = lax.ppermute(gq0, "seq", inside)
    gq1, p1, ds1 = attend(second, keys, values)
    back1 = lax.ppermute(gq1, "seq", across)
    grad_keys, grad_values = event_grads(p0, ds0, first, p1, ds1, second)
    return join(back0, back1), grad_keys, grad_values


def solution(mesh):
    return jax.shard_map(
        shards,
        mesh=mesh,
        in_specs=(
            P(("group", "seq"), "tp"),
            P(("group", "seq"), "tp"),
            P(("group", "seq"), "tp"),
            P(("group", "seq", "tp"), None),
            P("group"),
        ),
        out_specs=(P(("group", "seq"), "tp"), P(("group", "seq"), "tp"), P(("group", "seq"), "tp")),
        check_vma=False,
    )
```

time: 40.1 us -> 31.3 us (0.78)
  the two profiles are of different devices: /device:TPU:20 before, /device:TPU:0 now
where the time goes in v2:
time: 31.3 us; the launch traced here: 31 us
  starting transfers between devices  10.5 us (34%)
  Pallas kernels  9.24 us (30%)
  waiting for transfers between devices  5.51 us (18%)
  local copies, waits for them, and re-layouts  5.08 us (16%)
  between operations  0.69 us (2%)
    ppermute x1, starting transfers between devices, shards(): first = lax.ppermute(first, 'seq', inside)  5.7 us
    unnamed x8, local copies, waits for them, and re-layouts  5.08 us
    pallas_call x2, Pallas kernels, attend(): pl.pallas_call(attend_kernel, in_specs=[WHOLE] * 3, out_specs=[WHOLE] * 3...  4.86 us
    ppermute x1, waiting for transfers between devices, shards(): first = lax.ppermute(first, 'seq', inside)  4.09 us
    pallas_call x1, Pallas kernels, event_grads(): pl.pallas_call(event_kernel, grid=(width // PAIR,), in_specs=[WHOLE] * 6,...  3.26 us
    ppermute x1, starting transfers between devices, shards(): back0 = lax.ppermute(gq0, 'seq', inside)  2.92 us
    ppermute x1, waiting for transfers between devices, shards(): other = lax.ppermute(out_grad, 'tp', [(0, 1), (1, 0)])  1.37 us
    pallas_call x1, Pallas kernels, join(): pl.pallas_call(join_kernel, in_specs=[WHOLE] * 2, out_specs=RAW, out_shap...  0.71 us
  transfers between devices with their start and end apart: 5, of which 2 were waited for; matrix products, arithmetic and copies ran while one was open for 0% of the time, Pallas kernels for 27%

profile of v2, /device:TPU:0, one launch (start us, length us, event | category | flops | bytes accessed | tf_op | source)
XLA Modules:
  0.0 31.0 jit_solution(13827167732144823536)
XLA Ops:
  0.6 0.5 %collective-permute-start = (bf16[64,2048]{1,0:T(8,128)(2,1)}, bf16[64,2048]{1,0:T(8,128)(2,1)S(1)}, u32[]{:S(2)}, u32[]{:S(2)}) collective-permute-start(bf16[64,2048]{1,0:T(8,128)(2,1)} %own_ref.1), channel_id=1, source_target_pairs={{0,1},{1,0},{2,3},{3,2},{4,5},{5,4},{6,7},{7,6},{8,9},{9,8},{10,11... | collective-permute-start | bytes 786440 | tf_op jit(solution)/shard_map/ppermute | solution.py:213
  1.1 1.4 %collective-permute-done.other_ref = bf16[64,2048]{1,0:T(8,128)(2,1)S(1)} collective-permute-done((bf16[64,2048]{1,0:T(8,128)(2,1)}, bf16[64,2048]{1,0:T(8,128)(2,1)S(1)}, u32[]{:S(2)}, u32[]{:S(2)}) %collective-permute-start) | collective-permute-done | bytes 262176 | tf_op jit(solution)/shard_map/ppermute | solution.py:213
  2.5 0.0 copy-start.2
  2.5 0.9 %copy-done.2 = bf16[128,1024]{1,0:T(8,128)(2,1)S(1)} copy-done((bf16[128,1024]{1,0:T(8,128)(2,1)S(1)}, bf16[128,1024]{1,0:T(8,128)(2,1)}, u32[]{:S(2)}) %copy-start.2) | copy-done | bytes 262168
  3.5 0.0 copy-start.3
  3.5 0.9 %copy-done.3 = bf16[64,2048]{1,0:T(8,128)(2,1)S(1)} copy-done((bf16[64,2048]{1,0:T(8,128)(2,1)S(1)}, bf16[64,2048]{1,0:T(8,128)(2,1)}, u32[]{:S(2)}) %copy-start.3) | copy-done | bytes 262168
  4.5 0.7 %collective-permute-start.3 = (bf16[128,1024]{1,0:T(8,128)(2,1)S(1)}, bf16[128,1024]{1,0:T(8,128)(2,1)S(1)}, u32[]{:S(2)}, u32[]{:S(2)}) collective-permute-start(bf16[128,1024]{1,0:T(8,128)(2,1)S(1)} %get-tuple-element.19), channel_id=1, source_target_pairs={{0,0},{14,14},{2,4},{4,2},{6,8},{8,6},{10,12},{12,10},{1,1},{15,15... | collective-permute-start | bytes 786440 | tf_op jit(solution)/shard_map/ppermute | solution.py:216
  5.1 5.7 %collective-permute-start.1 = (bf16[128,1024]{1,0:T(8,128)(2,1)S(1)}, bf16[128,1024]{1,0:T(8,128)(2,1)S(1)}, u32[]{:S(2)}, u32[]{:S(2)}) collective-permute-start(bf16[128,1024]{1,0:T(8,128)(2,1)S(1)} %get-tuple-element.15), channel_id=1, source_target_pairs={{0,2},{2,0},{4,6},{6,4},{8,10},{10,8},{12,14},{14,12},{1,3},{3,1},... | collective-permute-start | bytes 786440 | tf_op jit(solution)/shard_map/ppermute | solution.py:215
  10.9 0.0 copy-start
  10.9 1.6 %copy-done = bf16[1024,1024]{1,0:T(8,128)(2,1)S(1)} copy-done((bf16[1024,1024]{1,0:T(8,128)(2,1)S(1)}, bf16[1024,1024]{1,0:T(8,128)(2,1)}, u32[]{:S(2)}) %copy-start) | copy-done | bytes 2097176
  12.4 0.0 copy-start.1
  12.4 1.6 %copy-done.1 = bf16[1024,1024]{1,0:T(8,128)(2,1)S(1)} copy-done((bf16[1024,1024]{1,0:T(8,128)(2,1)S(1)}, bf16[1024,1024]{1,0:T(8,128)(2,1)}, u32[]{:S(2)}) %copy-start.1) | copy-done | bytes 2097176
  14.0 0.4 %stage.1 = (bf16[1024,1024]{1,0:T(8,128)(2,1)S(1)}, bf16[1024,1024]{1,0:T(8,128)(2,1)S(1)}) custom-call(bf16[1024,1024]{1,0:T(8,128)(2,1)S(1)} %copy-done, bf16[1024,1024]{1,0:T(8,128)(2,1)S(1)} %copy-done.1), custom_call_target="tpu_custom_call" | custom-call | bytes 8388608 | tf_op jit(solution)/shard_map/stage/pallas_call | solution.py:79
  14.4 0.0 collective-permute-done.3.m_ref.m1_ref
  14.4 2.4 %attend.3 = (bf16[64,1024]{1,0:T(8,128)(2,1)S(1)}, bf16[1024,512]{1,0:T(8,128)(2,1)S(1)}, bf16[1024,512]{1,0:T(8,128)(2,1)S(1)}) custom-call(bf16[128,1024]{1,0:T(8,128)(2,1)S(1)} %collective-permute-done.3.m_ref.m1_ref, bf16[1024,1024]{1,0:T(8,128)(2,1)S(1)} %get-tuple-element.16.k_ref, bf16[1024,1024]{1,0:T(8,128)(2,1)S(1)} %get-tuple-element.17.v_ref), custom_call_target="tpu_custom_call" | custom-call | flops 536870912 | bytes 6291456 | tf_op jit(solution)/shard_map/attend/pallas_call | solution.py:133
  16.9 0.7 %collective-permute-start.4 = (bf16[64,1024]{1,0:T(8,128)(2,1)S(1)}, bf16[64,1024]{1,0:T(8,128)(2,1)S(1)}, u32[]{:S(2)}, u32[]{:S(2)}) collective-permute-start(bf16[64,1024]{1,0:T(8,128)(2,1)S(1)} %get-tuple-element.20), channel_id=1, source_target_pairs={{0,0},{14,14},{2,4},{4,2},{6,8},{8,6},{10,12},{12,10},{1,1},{15,15... | collective-permute-start | bytes 393224 | tf_op jit(solution)/shard_map/ppermute | solution.py:221
  17.5 4.1 %collective-permute-done.1.m_ref.m0_ref = bf16[128,1024]{1,0:T(8,128)(2,1)S(1)} collective-permute-done((bf16[128,1024]{1,0:T(8,128)(2,1)S(1)}, bf16[128,1024]{1,0:T(8,128)(2,1)S(1)}, u32[]{:S(2)}, u32[]{:S(2)}) %collective-permute-start.1) | collective-permute-done | bytes 262176 | tf_op jit(solution)/shard_map/ppermute | solution.py:215
  21.6 2.4 %attend.2 = (bf16[64,1024]{1,0:T(8,128)(2,1)S(1)}, bf16[1024,512]{1,0:T(8,128)(2,1)S(1)}, bf16[1024,512]{1,0:T(8,128)(2,1)S(1)}) custom-call(bf16[128,1024]{1,0:T(8,128)(2,1)S(1)} %collective-permute-done.1.m_ref.m0_ref, bf16[1024,1024]{1,0:T(8,128)(2,1)S(1)} %get-tuple-element.16.k_ref, bf16[1024,1024]{1,0:T(8,128)(2,1)S(1)} %get-tuple-element.17.v_ref), custom_call_target="tpu_custom_call" | custom-call | flops 536870912 | bytes 6291456 | tf_op jit(solution)/shard_map/attend/pallas_call | solution.py:133
  24.1 2.9 %collective-permute-start.2 = (bf16[64,1024]{1,0:T(8,128)(2,1)S(1)}, bf16[64,1024]{1,0:T(8,128)(2,1)S(1)}, u32[]{:S(2)}, u32[]{:S(2)}) collective-permute-start(bf16[64,1024]{1,0:T(8,128)(2,1)S(1)} %get-tuple-element.18), channel_id=1, source_target_pairs={{0,2},{2,0},{4,6},{6,4},{8,10},{10,8},{12,14},{14,12},{1,3},{3,1},... | collective-permute-start | bytes 393224 | tf_op jit(solution)/shard_map/ppermute | solution.py:219
  27.0 3.3 %event_grads.1 = (bf16[1024,1024]{1,0:T(8,128)(2,1)}, bf16[1024,1024]{1,0:T(8,128)(2,1)}) custom-call(bf16[1024,512]{1,0:T(8,128)(2,1)S(1)} %get-tuple-element.21.p0_ref, bf16[1024,512]{1,0:T(8,128)(2,1)S(1)} %get-tuple-element.22.ds0_ref, bf16[128,1024]{1,0:T(8,128)(2,1)S(1)} %collective-permute-done.1.m_ref.m0_ref, ...), custom_call_target="tpu_custom_call" | custom-call | flops 536870912 | bytes 8388608 | tf_op jit(solution)/shard_map/event_grads/pallas_call | solution.py:164
  30.2 0.0 collective-permute-done.4.across_ref
  30.3 0.0 collective-permute-done.2.inside_ref
  30.3 0.7 %join.1 = bf16[128,1024]{1,0:T(8,128)(2,1)} custom-call(bf16[64,1024]{1,0:T(8,128)(2,1)S(1)} %collective-permute-done.2.inside_ref, bf16[64,1024]{1,0:T(8,128)(2,1)S(1)} %collective-permute-done.4.across_ref), custom_call_target="tpu_custom_call" | custom-call | tf_op jit(solution)/shard_map/join/pallas_call | solution.py:194
  (1 shorter events, 0.0 us)
Async XLA Ops:
  0.6 1.9 %collective-permute-start = (bf16[64,2048]{1,0:T(8,128)(2,1)}, bf16[64,2048]{1,0:T(8,128)(2,1)S(1)}, u32[]{:S(2)}, u32[]{:S(2)}) collective-permute-start(bf16[64,2048]{1,0:T(8,128)(2,1)} %own_ref.1), channel_id=1, source_target_pairs={{0,1},{1,0},{2,3},{3,2},{4,5},{5,4},{6,7},{7,6},{8,9},{9,8},{10,11... | collective-permute-start | bytes 786440 | tf_op jit(solution)/shard_map/ppermute | solution.py:213
  2.5 0.9 %copy-start.2 = (bf16[128,1024]{1,0:T(8,128)(2,1)S(1)}, bf16[128,1024]{1,0:T(8,128)(2,1)}, u32[]{:S(2)}) copy-start(bf16[128,1024]{1,0:T(8,128)(2,1)} %q_ref.1) | copy-start | bytes 786436
  3.5 0.9 %copy-start.3 = (bf16[64,2048]{1,0:T(8,128)(2,1)S(1)}, bf16[64,2048]{1,0:T(8,128)(2,1)}, u32[]{:S(2)}) copy-start(bf16[64,2048]{1,0:T(8,128)(2,1)} %own_ref.1) | copy-start | bytes 786436
  4.5 9.9 %collective-permute-start.3 = (bf16[128,1024]{1,0:T(8,128)(2,1)S(1)}, bf16[128,1024]{1,0:T(8,128)(2,1)S(1)}, u32[]{:S(2)}, u32[]{:S(2)}) collective-permute-start(bf16[128,1024]{1,0:T(8,128)(2,1)S(1)} %get-tuple-element.19), channel_id=1, source_target_pairs={{0,0},{14,14},{2,4},{4,2},{6,8},{8,6},{10,12},{12,10},{1,1},{15,15... | collective-permute-start | bytes 786440 | tf_op jit(solution)/shard_map/ppermute | solution.py:216
  5.1 16.5 %collective-permute-start.1 = (bf16[128,1024]{1,0:T(8,128)(2,1)S(1)}, bf16[128,1024]{1,0:T(8,128)(2,1)S(1)}, u32[]{:S(2)}, u32[]{:S(2)}) collective-permute-start(bf16[128,1024]{1,0:T(8,128)(2,1)S(1)} %get-tuple-element.15), channel_id=1, source_target_pairs={{0,2},{2,0},{4,6},{6,4},{8,10},{10,8},{12,14},{14,12},{1,3},{3,1},... | collective-permute-start | bytes 786440 | tf_op jit(solution)/shard_map/ppermute | solution.py:215
  10.9 1.6 %copy-start = (bf16[1024,1024]{1,0:T(8,128)(2,1)S(1)}, bf16[1024,1024]{1,0:T(8,128)(2,1)}, u32[]{:S(2)}) copy-start(bf16[1024,1024]{1,0:T(8,128)(2,1)} %k_hbm.1) | copy-start | bytes 6291460
  12.4 1.6 %copy-start.1 = (bf16[1024,1024]{1,0:T(8,128)(2,1)S(1)}, bf16[1024,1024]{1,0:T(8,128)(2,1)}, u32[]{:S(2)}) copy-start(bf16[1024,1024]{1,0:T(8,128)(2,1)} %v_hbm.1) | copy-start | bytes 6291460
  16.9 13.4 %collective-permute-start.4 = (bf16[64,1024]{1,0:T(8,128)(2,1)S(1)}, bf16[64,1024]{1,0:T(8,128)(2,1)S(1)}, u32[]{:S(2)}, u32[]{:S(2)}) collective-permute-start(bf16[64,1024]{1,0:T(8,128)(2,1)S(1)} %get-tuple-element.20), channel_id=1, source_target_pairs={{0,0},{14,14},{2,4},{4,2},{6,8},{8,6},{10,12},{12,10},{1,1},{15,15... | collective-permute-start | bytes 393224 | tf_op jit(solution)/shard_map/ppermute | solution.py:221
  24.1 6.2 %collective-permute-start.2 = (bf16[64,1024]{1,0:T(8,128)(2,1)S(1)}, bf16[64,1024]{1,0:T(8,128)(2,1)S(1)}, u32[]{:S(2)}, u32[]{:S(2)}) collective-permute-start(bf16[64,1024]{1,0:T(8,128)(2,1)S(1)} %get-tuple-element.18), channel_id=1, source_target_pairs={{0,2},{2,0},{4,6},{6,4},{8,10},{10,8},{12,14},{14,12},{1,3},{3,1},... | collective-permute-start | bytes 393224 | tf_op jit(solution)/shard_map/ppermute | solution.py:219

commit v3 on v2

--- a/solution.py
+++ b/solution.py
@@ -28,6 +28,29 @@
     top = jnp.concatenate([rows[:, :HD], zeros], axis=1)
     low = jnp.concatenate([zeros, rows[:, HD:]], axis=1)
     return jnp.concatenate([top, low], axis=0)
+
+
+def load_kernel(q_hbm, g_hbm, q_ref, g_ref, sems):
+    moves = [
+        pltpu.make_async_copy(q_hbm, q_ref, sems.at[0]),
+        pltpu.make_async_copy(g_hbm, g_ref, sems.at[1]),
+    ]
+    for move in moves:
+        move.start()
+    for move in moves:
+        move.wait()
+
+
+def load(queries, out_grad):
+    return pl.pallas_call(
+        load_kernel,
+        in_specs=[RAW] * 2,
+        out_specs=[WHOLE] * 2,
+        out_shape=[jax.ShapeDtypeStruct(x.shape, x.dtype) for x in (queries, out_grad)],
+        scratch_shapes=[pltpu.SemaphoreType.DMA((2,))],
+        compiler_params=params(8),
+        name="load",
+    )(queries, out_grad)
 
 
 def pack_kernel(q_ref, own_ref, other_ref, inside_ref, across_ref):
@@ -211,7 +234,7 @@
     across = [(0, 0), (seq - 1, seq - 1)] + [(i, i + 1 if i % 2 else i - 1) for i in range(1, seq - 1)]
 
     other = lax.ppermute(out_grad, "tp", [(0, 1), (1, 0)])
-    first, second = pack(queries, out_grad, other)
+    first, second = pack(*load(queries, out_grad), other)
     first = lax.ppermute(first, "seq", inside)
     second = lax.ppermute(second, "seq", across)
     keys, values = stage(keys, values)

time: 31.3 us -> 30 us (0.958)
  waiting for transfers between devices: 5.51 us -> 4.52 us
  starting transfers between devices: 10.5 us -> 10.1 us
    ppermute x1, waiting for transfers between devices: 1.37 us -> 0.01 us  [shards(): other = lax.ppermute(out_grad, 'tp', [(0, 1), (1, 0)])]
    ppermute x1, starting transfers between devices: 5.7 us -> 5.34 us  [shards(): first = lax.ppermute(first, 'seq', inside)]
    ppermute x1, waiting for transfers between devices: 4.09 us -> 4.45 us  [shards(): first = lax.ppermute(first, 'seq', inside)]
  transfers between devices with their start and end apart: 5 -> 5, of which waited for: 2 -> 2; matrix products, arithmetic and copies ran while one was open for 0% -> 0% of each run, Pallas kernels for 27% -> 29%
where the time goes in v3:
time: 30 us; the launch traced here: 29.8 us
  starting transfers between devices  10.1 us (34%)
  Pallas kernels  9.32 us (31%)
  local copies, waits for them, and re-layouts  5.08 us (17%)
  waiting for transfers between devices  4.52 us (15%)
  between operations  0.71 us (2%)
    ppermute x1, starting transfers between devices, shards(): first = lax.ppermute(first, 'seq', inside)  5.34 us
    unnamed x8, local copies, waits for them, and re-layouts  5.08 us
    pallas_call x2, Pallas kernels, attend(): pl.pallas_call(attend_kernel, in_specs=[WHOLE] * 3, out_specs=[WHOLE] * 3...  4.86 us
    ppermute x1, waiting for transfers between devices, shards(): first = lax.ppermute(first, 'seq', inside)  4.45 us
    pallas_call x1, Pallas kernels, event_grads(): pl.pallas_call(event_kernel, grid=(width // PAIR,), in_specs=[WHOLE] * 6,...  3.26 us
    ppermute x1, starting transfers between devices, shards(): back0 = lax.ppermute(gq0, 'seq', inside)  2.92 us
    pallas_call x1, Pallas kernels, join(): pl.pallas_call(join_kernel, in_specs=[WHOLE] * 2, out_specs=RAW, out_shap...  0.71 us
    ppermute x1, starting transfers between devices, shards(): second = lax.ppermute(second, 'seq', across)  0.68 us
  transfers between devices with their start and end apart: 5, of which 2 were waited for; matrix products, arithmetic and copies ran while one was open for 0% of the time, Pallas kernels for 29%

profile of v3, /device:TPU:0, one launch (start us, length us, event | category | flops | bytes accessed | tf_op | source)
XLA Modules:
  0.0 29.8 jit_solution(16256645215633781591)
XLA Ops:
  0.6 0.5 %collective-permute-start = (bf16[64,2048]{1,0:T(8,128)(2,1)}, bf16[64,2048]{1,0:T(8,128)(2,1)S(1)}, u32[]{:S(2)}, u32[]{:S(2)}) collective-permute-start(bf16[64,2048]{1,0:T(8,128)(2,1)} %g_hbm.1), channel_id=1, source_target_pairs={{0,1},{1,0},{2,3},{3,2},{4,5},{5,4},{6,7},{7,6},{8,9},{9,8},{10,11... | collective-permute-start | bytes 786440 | tf_op jit(solution)/shard_map/ppermute | solution.py:236
  1.1 0.0 copy-start.2
  1.1 0.9 %copy-done.2 = bf16[128,1024]{1,0:T(8,128)(2,1)S(1)} copy-done((bf16[128,1024]{1,0:T(8,128)(2,1)S(1)}, bf16[128,1024]{1,0:T(8,128)(2,1)}, u32[]{:S(2)}) %copy-start.2) | copy-done | bytes 262168
  2.1 0.0 copy-start.3
  2.1 0.9 %copy-done.3 = bf16[64,2048]{1,0:T(8,128)(2,1)S(1)} copy-done((bf16[64,2048]{1,0:T(8,128)(2,1)S(1)}, bf16[64,2048]{1,0:T(8,128)(2,1)}, u32[]{:S(2)}) %copy-start.3) | copy-done | bytes 262168
  3.0 0.1 load.1
  3.1 0.0 collective-permute-done.other_ref
  3.1 0.1 pack.1
  3.2 0.7 %collective-permute-start.3 = (bf16[128,1024]{1,0:T(8,128)(2,1)S(1)}, bf16[128,1024]{1,0:T(8,128)(2,1)S(1)}, u32[]{:S(2)}, u32[]{:S(2)}) collective-permute-start(bf16[128,1024]{1,0:T(8,128)(2,1)S(1)} %get-tuple-element.23), channel_id=1, source_target_pairs={{0,0},{14,14},{2,4},{4,2},{6,8},{8,6},{10,12},{12,10},{1,1},{15,15... | collective-permute-start | bytes 786440 | tf_op jit(solution)/shard_map/ppermute | solution.py:239
  3.9 5.3 %collective-permute-start.1 = (bf16[128,1024]{1,0:T(8,128)(2,1)S(1)}, bf16[128,1024]{1,0:T(8,128)(2,1)S(1)}, u32[]{:S(2)}, u32[]{:S(2)}) collective-permute-start(bf16[128,1024]{1,0:T(8,128)(2,1)S(1)} %get-tuple-element.19), channel_id=1, source_target_pairs={{0,2},{2,0},{4,6},{6,4},{8,10},{10,8},{12,14},{14,12},{1,3},{3,1},... | collective-permute-start | bytes 786440 | tf_op jit(solution)/shard_map/ppermute | solution.py:238
  9.2 0.0 copy-start
  9.2 1.6 %copy-done = bf16[1024,1024]{1,0:T(8,128)(2,1)S(1)} copy-done((bf16[1024,1024]{1,0:T(8,128)(2,1)S(1)}, bf16[1024,1024]{1,0:T(8,128)(2,1)}, u32[]{:S(2)}) %copy-start) | copy-done | bytes 2097176
  10.8 0.0 copy-start.1
  10.8 1.6 %copy-done.1 = bf16[1024,1024]{1,0:T(8,128)(2,1)S(1)} copy-done((bf16[1024,1024]{1,0:T(8,128)(2,1)S(1)}, bf16[1024,1024]{1,0:T(8,128)(2,1)}, u32[]{:S(2)}) %copy-start.1) | copy-done | bytes 2097176
  12.4 0.4 %stage.1 = (bf16[1024,1024]{1,0:T(8,128)(2,1)S(1)}, bf16[1024,1024]{1,0:T(8,128)(2,1)S(1)}) custom-call(bf16[1024,1024]{1,0:T(8,128)(2,1)S(1)} %copy-done, bf16[1024,1024]{1,0:T(8,128)(2,1)S(1)} %copy-done.1), custom_call_target="tpu_custom_call" | custom-call | bytes 8388608 | tf_op jit(solution)/shard_map/stage/pallas_call | solution.py:102
  12.8 0.0 collective-permute-done.3.m_ref.m1_ref
  12.8 2.4 %attend.3 = (bf16[64,1024]{1,0:T(8,128)(2,1)S(1)}, bf16[1024,512]{1,0:T(8,128)(2,1)S(1)}, bf16[1024,512]{1,0:T(8,128)(2,1)S(1)}) custom-call(bf16[128,1024]{1,0:T(8,128)(2,1)S(1)} %collective-permute-done.3.m_ref.m1_ref, bf16[1024,1024]{1,0:T(8,128)(2,1)S(1)} %get-tuple-element.20.k_ref, bf16[1024,1024]{1,0:T(8,128)(2,1)S(1)} %get-tuple-element.21.v_ref), custom_call_target="tpu_custom_call" | custom-call | flops 536870912 | bytes 6291456 | tf_op jit(solution)/shard_map/attend/pallas_call | solution.py:156
  15.2 0.7 %collective-permute-start.4 = (bf16[64,1024]{1,0:T(8,128)(2,1)S(1)}, bf16[64,1024]{1,0:T(8,128)(2,1)S(1)}, u32[]{:S(2)}, u32[]{:S(2)}) collective-permute-start(bf16[64,1024]{1,0:T(8,128)(2,1)S(1)} %get-tuple-element.24), channel_id=1, source_target_pairs={{0,0},{14,14},{2,4},{4,2},{6,8},{8,6},{10,12},{12,10},{1,1},{15,15... | collective-permute-start | bytes 393224 | tf_op jit(solution)/shard_map/ppermute | solution.py:244
  15.9 4.4 %collective-permute-done.1.m_ref.m0_ref = bf16[128,1024]{1,0:T(8,128)(2,1)S(1)} collective-permute-done((bf16[128,1024]{1,0:T(8,128)(2,1)S(1)}, bf16[128,1024]{1,0:T(8,128)(2,1)S(1)}, u32[]{:S(2)}, u32[]{:S(2)}) %collective-permute-start.1) | collective-permute-done | bytes 262176 | tf_op jit(solution)/shard_map/ppermute | solution.py:238
  20.4 2.4 %attend.2 = (bf16[64,1024]{1,0:T(8,128)(2,1)S(1)}, bf16[1024,512]{1,0:T(8,128)(2,1)S(1)}, bf16[1024,512]{1,0:T(8,128)(2,1)S(1)}) custom-call(bf16[128,1024]{1,0:T(8,128)(2,1)S(1)} %collective-permute-done.1.m_ref.m0_ref, bf16[1024,1024]{1,0:T(8,128)(2,1)S(1)} %get-tuple-element.20.k_ref, bf16[1024,1024]{1,0:T(8,128)(2,1)S(1)} %get-tuple-element.21.v_ref), custom_call_target="tpu_custom_call" | custom-call | flops 536870912 | bytes 6291456 | tf_op jit(solution)/shard_map/attend/pallas_call | solution.py:156
  22.8 2.9 %collective-permute-start.2 = (bf16[64,1024]{1,0:T(8,128)(2,1)S(1)}, bf16[64,1024]{1,0:T(8,128)(2,1)S(1)}, u32[]{:S(2)}, u32[]{:S(2)}) collective-permute-start(bf16[64,1024]{1,0:T(8,128)(2,1)S(1)} %get-tuple-element.22), channel_id=1, source_target_pairs={{0,2},{2,0},{4,6},{6,4},{8,10},{10,8},{12,14},{14,12},{1,3},{3,1},... | collective-permute-start | bytes 393224 | tf_op jit(solution)/shard_map/ppermute | solution.py:242
  25.7 3.3 %event_grads.1 = (bf16[1024,1024]{1,0:T(8,128)(2,1)}, bf16[1024,1024]{1,0:T(8,128)(2,1)}) custom-call(bf16[1024,512]{1,0:T(8,128)(2,1)S(1)} %get-tuple-element.25.p0_ref, bf16[1024,512]{1,0:T(8,128)(2,1)S(1)} %get-tuple-element.26.ds0_ref, bf16[128,1024]{1,0:T(8,128)(2,1)S(1)} %collective-permute-done.1.m_ref.m0_ref, ...), custom_call_target="tpu_custom_call" | custom-call | flops 536870912 | bytes 8388608 | tf_op jit(solution)/shard_map/event_grads/pallas_call | solution.py:187
  29.0 0.0 collective-permute-done.4.across_ref
  29.0 0.1 collective-permute-done.2.inside_ref
  29.0 0.7 %join.1 = bf16[128,1024]{1,0:T(8,128)(2,1)} custom-call(bf16[64,1024]{1,0:T(8,128)(2,1)S(1)} %collective-permute-done.2.inside_ref, bf16[64,1024]{1,0:T(8,128)(2,1)S(1)} %collective-permute-done.4.across_ref), custom_call_target="tpu_custom_call" | custom-call | tf_op jit(solution)/shard_map/join/pallas_call | solution.py:217
Async XLA Ops:
  0.6 2.5 %collective-permute-start = (bf16[64,2048]{1,0:T(8,128)(2,1)}, bf16[64,2048]{1,0:T(8,128)(2,1)S(1)}, u32[]{:S(2)}, u32[]{:S(2)}) collective-permute-start(bf16[64,2048]{1,0:T(8,128)(2,1)} %g_hbm.1), channel_id=1, source_target_pairs={{0,1},{1,0},{2,3},{3,2},{4,5},{5,4},{6,7},{7,6},{8,9},{9,8},{10,11... | collective-permute-start | bytes 786440 | tf_op jit(solution)/shard_map/ppermute | solution.py:236
  1.1 0.9 %copy-start.2 = (bf16[128,1024]{1,0:T(8,128)(2,1)S(1)}, bf16[128,1024]{1,0:T(8,128)(2,1)}, u32[]{:S(2)}) copy-start(bf16[128,1024]{1,0:T(8,128)(2,1)} %q_hbm.1) | copy-start | bytes 786436
  2.1 0.9 %copy-start.3 = (bf16[64,2048]{1,0:T(8,128)(2,1)S(1)}, bf16[64,2048]{1,0:T(8,128)(2,1)}, u32[]{:S(2)}) copy-start(bf16[64,2048]{1,0:T(8,128)(2,1)} %g_hbm.1) | copy-start | bytes 786436
  3.2 9.6 %collective-permute-start.3 = (bf16[128,1024]{1,0:T(8,128)(2,1)S(1)}, bf16[128,1024]{1,0:T(8,128)(2,1)S(1)}, u32[]{:S(2)}, u32[]{:S(2)}) collective-permute-start(bf16[128,1024]{1,0:T(8,128)(2,1)S(1)} %get-tuple-element.23), channel_id=1, source_target_pairs={{0,0},{14,14},{2,4},{4,2},{6,8},{8,6},{10,12},{12,10},{1,1},{15,15... | collective-permute-start | bytes 786440 | tf_op jit(solution)/shard_map/ppermute | solution.py:239
  3.9 16.5 %collective-permute-start.1 = (bf16[128,1024]{1,0:T(8,128)(2,1)S(1)}, bf16[128,1024]{1,0:T(8,128)(2,1)S(1)}, u32[]{:S(2)}, u32[]{:S(2)}) collective-permute-start(bf16[128,1024]{1,0:T(8,128)(2,1)S(1)} %get-tuple-element.19), channel_id=1, source_target_pairs={{0,2},{2,0},{4,6},{6,4},{8,10},{10,8},{12,14},{14,12},{1,3},{3,1},... | collective-permute-start | bytes 786440 | tf_op jit(solution)/shard_map/ppermute | solution.py:238
  9.2 1.6 %copy-start = (bf16[1024,1024]{1,0:T(8,128)(2,1)S(1)}, bf16[1024,1024]{1,0:T(8,128)(2,1)}, u32[]{:S(2)}) copy-start(bf16[1024,1024]{1,0:T(8,128)(2,1)} %k_hbm.1) | copy-start | bytes 6291460
  10.8 1.6 %copy-start.1 = (bf16[1024,1024]{1,0:T(8,128)(2,1)S(1)}, bf16[1024,1024]{1,0:T(8,128)(2,1)}, u32[]{:S(2)}) copy-start(bf16[1024,1024]{1,0:T(8,128)(2,1)} %v_hbm.1) | copy-start | bytes 6291460
  15.2 13.8 %collective-permute-start.4 = (bf16[64,1024]{1,0:T(8,128)(2,1)S(1)}, bf16[64,1024]{1,0:T(8,128)(2,1)S(1)}, u32[]{:S(2)}, u32[]{:S(2)}) collective-permute-start(bf16[64,1024]{1,0:T(8,128)(2,1)S(1)} %get-tuple-element.24), channel_id=1, source_target_pairs={{0,0},{14,14},{2,4},{4,2},{6,8},{8,6},{10,12},{12,10},{1,1},{15,15... | collective-permute-start | bytes 393224 | tf_op jit(solution)/shard_map/ppermute | solution.py:244
  22.8 6.3 %collective-permute-start.2 = (bf16[64,1024]{1,0:T(8,128)(2,1)S(1)}, bf16[64,1024]{1,0:T(8,128)(2,1)S(1)}, u32[]{:S(2)}, u32[]{:S(2)}) collective-permute-start(bf16[64,1024]{1,0:T(8,128)(2,1)S(1)} %get-tuple-element.22), channel_id=1, source_target_pairs={{0,2},{2,0},{4,6},{6,4},{8,10},{10,8},{12,14},{14,12},{1,3},{3,1},... | collective-permute-start | bytes 393224 | tf_op jit(solution)/shard_map/ppermute | solution.py:242

commit v4 on v3

--- a/solution.py
+++ b/solution.py
@@ -111,7 +111,28 @@
     )(keys, values)
 
 
-def attend_kernel(m_ref, k_ref, v_ref, gq_ref, p_ref, ds_ref):
+def at_end():
+    index = lax.axis_index("seq")
+    return (index == 0) | (index == lax.axis_size("seq") - 1)
+
+
+def attend_inside_kernel(m_ref, k_ref, v_ref, gq_ref, p_ref, ds_ref):
+    attend_body(m_ref, k_ref, v_ref, gq_ref, p_ref, ds_ref)
+
+
+def attend_across_kernel(own_ref, received_ref, k_ref, v_ref, gq_ref, p_ref, ds_ref, m_ref):
+    @pl.when(at_end())
+    def _():
+        m_ref[...] = own_ref[...]
+
+    @pl.when(jnp.logical_not(at_end()))
+    def _():
+        m_ref[...] = received_ref[...]
+
+    attend_body(m_ref, k_ref, v_ref, gq_ref, p_ref, ds_ref)
+
+
+def attend_body(m_ref, k_ref, v_ref, gq_ref, p_ref, ds_ref):
     pairs = m_ref.shape[1] // PAIR
     held = {}
 
@@ -150,20 +171,23 @@
                 stage_of(step - lag)
 
 
-def attend(message, keys, values):
-    width = message.shape[1]
+def attend(kernel, messages, keys, values):
+    width = keys.shape[1]
     staged = jax.ShapeDtypeStruct((WIN, width // HD * BLK), jnp.bfloat16)
-    return pl.pallas_call(
-        attend_kernel,
-        in_specs=[WHOLE] * 3,
-        out_specs=[WHOLE] * 3,
-        out_shape=[jax.ShapeDtypeStruct((BLK, width), jnp.bfloat16), staged, staged],
+    shapes = [jax.ShapeDtypeStruct((BLK, width), jnp.bfloat16), staged, staged]
+    if len(messages) == 2:
+        shapes.append(jax.ShapeDtypeStruct(messages[0].shape, messages[0].dtype))
+    return pl.pallas_call(
+        kernel,
+        in_specs=[WHOLE] * (len(messages) + 2),
+        out_specs=[WHOLE] * len(shapes),
+        out_shape=shapes,
         compiler_params=params(32),
         cost_estimate=pl.CostEstimate(
             flops=8 * BLK * WIN * width, bytes_accessed=6 * WIN * width, transcendentals=BLK * WIN * width // HD
         ),
         name="attend",
-    )(message, keys, values)
+    )(*messages, keys, values)
 
 
 def event_kernel(p0_ref, ds0_ref, m0_ref, p1_ref, ds1_ref, m1_ref, gk_ref, gv_ref):
@@ -198,52 +222,78 @@
     )(*args)
 
 
-def join_kernel(inside_ref, across_ref, out_hbm, sems):
+def join_across_kernel(across_ref, own_ref, out_hbm, sem):
     odd = lax.axis_index("seq") % 2
-    moves = [
-        pltpu.make_async_copy(
-            ref, out_hbm.at[pl.ds(pl.multiple_of(row * BLK, BLK), BLK), :], sems.at[i]
-        )
-        for i, (ref, row) in enumerate(((inside_ref, 1 - odd), (across_ref, odd)))
-    ]
-    for move in moves:
-        move.start()
-    for move in moves:
-        move.wait()
-
-
-def join(back_inside, back_across):
-    width = back_inside.shape[1]
-    return pl.pallas_call(
-        join_kernel,
+    rows = out_hbm.at[pl.ds(pl.multiple_of(odd * BLK, BLK), BLK), :]
+
+    @pl.when(at_end())
+    def _():
+        pltpu.make_async_copy(own_ref, rows, sem).start()
+
+    @pl.when(jnp.logical_not(at_end()))
+    def _():
+        pltpu.make_async_copy(across_ref, rows, sem).start()
+
+    pltpu.make_async_copy(across_ref, rows, sem).wait()
+
+
+def join_inside_kernel(inside_ref, half_hbm, out_hbm, sem):
+    odd = lax.axis_index("seq") % 2
+    move = pltpu.make_async_copy(
+        inside_ref, out_hbm.at[pl.ds(pl.multiple_of((1 - odd) * BLK, BLK), BLK), :], sem
+    )
+    move.start()
+    move.wait()
+
+
+def join_across(back_across, own_across):
+    width = back_across.shape[1]
+    return pl.pallas_call(
+        join_across_kernel,
         in_specs=[WHOLE] * 2,
         out_specs=RAW,
-        out_shape=jax.ShapeDtypeStruct((2 * BLK, width), back_inside.dtype),
-        scratch_shapes=[pltpu.SemaphoreType.DMA((2,))],
+        out_shape=jax.ShapeDtypeStruct((2 * BLK, width), back_across.dtype),
+        scratch_shapes=[pltpu.SemaphoreType.DMA],
         compiler_params=params(8),
-        name="join",
-    )(back_inside, back_across)
+        name="join_across",
+    )(back_across, own_across)
+
+
+def join_inside(back_inside, half):
+    return pl.pallas_call(
+        join_inside_kernel,
+        in_specs=[WHOLE, RAW],
+        out_specs=RAW,
+        out_shape=jax.ShapeDtypeStruct(half.shape, half.dtype),
+        scratch_shapes=[pltpu.SemaphoreType.DMA],
+        input_output_aliases={1: 0},
+        compiler_params=params(8),
+        name="join_inside",
+    )(back_inside, half)
 
 
 def shards(queries, keys, values, out_grad, starts):
     del starts
     seq = lax.axis_size("seq")
     frames, width = queries.shape
-    assert frames == 2 * BLK and keys.shape[0] == WIN and seq % 2 == 0
+    assert frames == 2 * BLK and keys.shape[0] == WIN and seq % 2 == 0 and lax.axis_size("tp") == 2
     inside = [(i, i ^ 1) for i in range(seq)]
-    across = [(0, 0), (seq - 1, seq - 1)] + [(i, i + 1 if i % 2 else i - 1) for i in range(1, seq - 1)]
+    across = [(0, 1), (1, 0), (2 * seq - 2, 2 * seq - 1), (2 * seq - 1, 2 * seq - 2)]
+    for i in range(1, seq - 1):
+        partner = i + 1 if i % 2 else i - 1
+        across += [(2 * i + core, 2 * partner + core) for core in range(2)]
 
     other = lax.ppermute(out_grad, "tp", [(0, 1), (1, 0)])
     first, second = pack(*load(queries, out_grad), other)
-    first = lax.ppermute(first, "seq", inside)
-    second = lax.ppermute(second, "seq", across)
+    got_first = lax.ppermute(first, "seq", inside)
+    got_second = lax.ppermute(second, ("seq", "tp"), across)
     keys, values = stage(keys, values)
-    gq0, p0, ds0 = attend(first, keys, values)
+    gq1, p1, ds1, used = attend(attend_across_kernel, [second, got_second], keys, values)
+    back1 = lax.ppermute(gq1, ("seq", "tp"), across)
+    gq0, p0, ds0 = attend(attend_inside_kernel, [got_first], keys, values)
     back0 = lax.ppermute(gq0, "seq", inside)
-    gq1, p1, ds1 = attend(second, keys, values)
-    back1 = lax.ppermute(gq1, "seq", across)
-    grad_keys, grad_values = event_grads(p0, ds0, first, p1, ds1, second)
-    return join(back0, back1), grad_keys, grad_values
+    grad_keys, grad_values = event_grads(p0, ds0, got_first, p1, ds1, used)
+    return join_inside(back0, join_across(back1, gq1)), grad_keys, grad_values
 
 
 def solution(mesh):

time: 30 us -> 28.4 us (0.947)
  starting transfers between devices: 10.1 us -> 7.25 us
  Pallas kernels: 9.32 us -> 10 us
  waiting for transfers between devices: 4.52 us -> 5.11 us
    ppermute x3, starting transfers between devices: 6.69 us -> 4.18 us  [the longest x1 3.99 us: shards(): got_first = lax.ppermute(first, 'seq', inside)]
    pallas_call x3 -> x4, Pallas kernels: 5.58 us -> 6.24 us  [the longest x2 4.9 us: attend(): pl.pallas_call(kernel, in_specs=[WHOLE] * (len(messages) + 2), out_specs=...]
    ppermute x3, waiting for transfers between devices: 4.45 us -> 5.1 us  [the longest x1 5.1 us: shards(): got_first = lax.ppermute(first, 'seq', inside)]
    ppermute x1, starting transfers between devices: 2.92 us -> 2.55 us  [shards(): back0 = lax.ppermute(gq0, 'seq', inside)]
  transfers between devices with their start and end apart: 5 -> 5, of which waited for: 2 -> 1; matrix products, arithmetic and copies ran while one was open for 0% -> 0% of each run, Pallas kernels for 29% -> 33%
where the time goes in v4:
time: 28.4 us; the launch traced here: 28.2 us
  Pallas kernels  10 us (35%)
  starting transfers between devices  7.25 us (26%)
  waiting for transfers between devices  5.11 us (18%)
  local copies, waits for them, and re-layouts  5.08 us (18%)
  between operations  0.72 us (3%)
    ppermute x1, waiting for transfers between devices, shards(): got_first = lax.ppermute(first, 'seq', inside)  5.1 us
    unnamed x8, local copies, waits for them, and re-layouts  5.08 us
    pallas_call x2, Pallas kernels, attend(): pl.pallas_call(kernel, in_specs=[WHOLE] * (len(messages) + 2), out_specs=...  4.9 us
    ppermute x1, starting transfers between devices, shards(): got_first = lax.ppermute(first, 'seq', inside)  3.99 us
    pallas_call x1, Pallas kernels, event_grads(): pl.pallas_call(event_kernel, grid=(width // PAIR,), in_specs=[WHOLE] * 6,...  3.27 us
    ppermute x1, starting transfers between devices, shards(): back0 = lax.ppermute(gq0, 'seq', inside)  2.55 us
    pallas_call x1, Pallas kernels, join_inside(): pl.pallas_call(join_inside_kernel, in_specs=[WHOLE, RAW], out_specs=RAW,...  0.68 us
    pallas_call x1, Pallas kernels, join_across(): pl.pallas_call(join_across_kernel, in_specs=[WHOLE] * 2, out_specs=RAW, o...  0.66 us
  transfers between devices with their start and end apart: 5, of which 1 were waited for; matrix products, arithmetic and copies ran while one was open for 0% of the time, Pallas kernels for 33%

profile of v4, /device:TPU:0, one launch (start us, length us, event | category | flops | bytes accessed | tf_op | source)
XLA Modules:
  0.0 28.2 jit_solution(10949688046774363435)
XLA Ops:
  0.6 0.5 %collective-permute-start = (bf16[64,2048]{1,0:T(8,128)(2,1)}, bf16[64,2048]{1,0:T(8,128)(2,1)S(1)}, u32[]{:S(2)}, u32[]{:S(2)}) collective-permute-start(bf16[64,2048]{1,0:T(8,128)(2,1)} %g_hbm.1), channel_id=1, source_target_pairs={{0,1},{1,0},{2,3},{3,2},{4,5},{5,4},{6,7},{7,6},{8,9},{9,8},{10,11... | collective-permute-start | bytes 786440 | tf_op jit(solution)/shard_map/ppermute | solution.py:286
  1.1 0.0 copy-start.2
  1.1 0.9 %copy-done.2 = bf16[128,1024]{1,0:T(8,128)(2,1)S(1)} copy-done((bf16[128,1024]{1,0:T(8,128)(2,1)S(1)}, bf16[128,1024]{1,0:T(8,128)(2,1)}, u32[]{:S(2)}) %copy-start.2) | copy-done | bytes 262168
  2.1 0.0 copy-start.3
  2.1 0.9 %copy-done.3 = bf16[64,2048]{1,0:T(8,128)(2,1)S(1)} copy-done((bf16[64,2048]{1,0:T(8,128)(2,1)S(1)}, bf16[64,2048]{1,0:T(8,128)(2,1)}, u32[]{:S(2)}) %copy-start.3) | copy-done | bytes 262168
  3.0 0.1 load.1
  3.1 0.0 collective-permute-done.other_ref
  3.1 0.1 pack.1
  3.2 0.1 collective-permute-start.3
  3.3 4.0 %collective-permute-start.1 = (bf16[128,1024]{1,0:T(8,128)(2,1)S(1)}, bf16[128,1024]{1,0:T(8,128)(2,1)S(1)}, u32[]{:S(2)}, u32[]{:S(2)}) collective-permute-start(bf16[128,1024]{1,0:T(8,128)(2,1)S(1)} %get-tuple-element.20), channel_id=1, source_target_pairs={{0,2},{2,0},{4,6},{6,4},{8,10},{10,8},{12,14},{14,12},{1,3},{3,1},... | collective-permute-start | bytes 786440 | tf_op jit(solution)/shard_map/ppermute | solution.py:288
  7.3 0.0 copy-start
  7.3 1.6 %copy-done = bf16[1024,1024]{1,0:T(8,128)(2,1)S(1)} copy-done((bf16[1024,1024]{1,0:T(8,128)(2,1)S(1)}, bf16[1024,1024]{1,0:T(8,128)(2,1)}, u32[]{:S(2)}) %copy-start) | copy-done | bytes 2097176
  8.9 0.0 copy-start.1
  8.9 1.6 %copy-done.1 = bf16[1024,1024]{1,0:T(8,128)(2,1)S(1)} copy-done((bf16[1024,1024]{1,0:T(8,128)(2,1)S(1)}, bf16[1024,1024]{1,0:T(8,128)(2,1)}, u32[]{:S(2)}) %copy-start.1) | copy-done | bytes 2097176
  10.5 0.4 %stage.1 = (bf16[1024,1024]{1,0:T(8,128)(2,1)S(1)}, bf16[1024,1024]{1,0:T(8,128)(2,1)S(1)}) custom-call(bf16[1024,1024]{1,0:T(8,128)(2,1)S(1)} %copy-done, bf16[1024,1024]{1,0:T(8,128)(2,1)S(1)} %copy-done.1), custom_call_target="tpu_custom_call" | custom-call | bytes 8388608 | tf_op jit(solution)/shard_map/stage/pallas_call | solution.py:102
  10.9 0.0 collective-permute-done.3.received_ref
  10.9 2.5 %attend.3 = (bf16[64,1024]{1,0:T(8,128)(2,1)S(1)}, bf16[1024,512]{1,0:T(8,128)(2,1)S(1)}, bf16[1024,512]{1,0:T(8,128)(2,1)S(1)}, bf16[128,1024]{1,0:T(8,128)(2,1)S(1)}) custom-call(bf16[128,1024]{1,0:T(8,128)(2,1)S(1)} %get-tuple-element.24.own_ref, bf16[128,1024]{1,0:T(8,128)(2,1)S(1)} %collective-permute-done.3.received_ref, ...), custom_call_target="tpu_custom_call" | custom-call | flops 536870912 | bytes 6291456 | tf_op jit(solution)/shard_map/attend/pallas_call | solution.py:180
  13.3 0.1 collective-permute-start.4
  13.4 5.1 %collective-permute-done.1.m_ref.m0_ref = bf16[128,1024]{1,0:T(8,128)(2,1)S(1)} collective-permute-done((bf16[128,1024]{1,0:T(8,128)(2,1)S(1)}, bf16[128,1024]{1,0:T(8,128)(2,1)S(1)}, u32[]{:S(2)}, u32[]{:S(2)}) %collective-permute-start.1) | collective-permute-done | bytes 262176 | tf_op jit(solution)/shard_map/ppermute | solution.py:288
  18.5 2.4 %attend.2 = (bf16[64,1024]{1,0:T(8,128)(2,1)S(1)}, bf16[1024,512]{1,0:T(8,128)(2,1)S(1)}, bf16[1024,512]{1,0:T(8,128)(2,1)S(1)}) custom-call(bf16[128,1024]{1,0:T(8,128)(2,1)S(1)} %collective-permute-done.1.m_ref.m0_ref, bf16[1024,1024]{1,0:T(8,128)(2,1)S(1)} %get-tuple-element.21.k_ref, bf16[1024,1024]{1,0:T(8,128)(2,1)S(1)} %get-tuple-element.22.v_ref), custom_call_target="tpu_custom_call" | custom-call | flops 536870912 | bytes 6291456 | tf_op jit(solution)/shard_map/attend/pallas_call | solution.py:180
  21.0 2.5 %collective-permute-start.2 = (bf16[64,1024]{1,0:T(8,128)(2,1)S(1)}, bf16[64,1024]{1,0:T(8,128)(2,1)S(1)}, u32[]{:S(2)}, u32[]{:S(2)}) collective-permute-start(bf16[64,1024]{1,0:T(8,128)(2,1)S(1)} %get-tuple-element.23), channel_id=1, source_target_pairs={{0,2},{2,0},{4,6},{6,4},{8,10},{10,8},{12,14},{14,12},{1,3},{3,1},... | collective-permute-start | bytes 393224 | tf_op jit(solution)/shard_map/ppermute | solution.py:294
  23.5 3.3 %event_grads.1 = (bf16[1024,1024]{1,0:T(8,128)(2,1)}, bf16[1024,1024]{1,0:T(8,128)(2,1)}) custom-call(bf16[1024,512]{1,0:T(8,128)(2,1)S(1)} %get-tuple-element.26.p0_ref, bf16[1024,512]{1,0:T(8,128)(2,1)S(1)} %get-tuple-element.27.ds0_ref, bf16[128,1024]{1,0:T(8,128)(2,1)S(1)} %collective-permute-done.1.m_ref.m0_ref, ...), custom_call_target="tpu_custom_call" | custom-call | flops 536870912 | bytes 8388608 | tf_op jit(solution)/shard_map/event_grads/pallas_call | solution.py:211
  26.8 0.0 collective-permute-done.4.across_ref
  26.8 0.7 %join_across.1.half_hbm = bf16[128,1024]{1,0:T(8,128)(2,1)} custom-call(bf16[64,1024]{1,0:T(8,128)(2,1)S(1)} %collective-permute-done.4.across_ref, bf16[64,1024]{1,0:T(8,128)(2,1)S(1)} %get-tuple-element.25.own_ref), custom_call_target="tpu_custom_call" | custom-call | tf_op jit(solution)/shard_map/join_across/pallas_call | solution.py:251
  27.5 0.0 collective-permute-done.2.inside_ref
  27.5 0.7 %join_inside.1 = bf16[128,1024]{1,0:T(8,128)(2,1)} custom-call(bf16[64,1024]{1,0:T(8,128)(2,1)S(1)} %collective-permute-done.2.inside_ref, bf16[128,1024]{1,0:T(8,128)(2,1)} %join_across.1.half_hbm), custom_call_target="tpu_custom_call", output_to_operand_aliasing={{}: (1, {})} | custom-call | tf_op jit(solution)/shard_map/join_inside/pallas_call | solution.py:263
Async XLA Ops:
  0.6 2.5 %collective-permute-start = (bf16[64,2048]{1,0:T(8,128)(2,1)}, bf16[64,2048]{1,0:T(8,128)(2,1)S(1)}, u32[]{:S(2)}, u32[]{:S(2)}) collective-permute-start(bf16[64,2048]{1,0:T(8,128)(2,1)} %g_hbm.1), channel_id=1, source_target_pairs={{0,1},{1,0},{2,3},{3,2},{4,5},{5,4},{6,7},{7,6},{8,9},{9,8},{10,11... | collective-permute-start | bytes 786440 | tf_op jit(solution)/shard_map/ppermute | solution.py:286
  1.1 0.9 %copy-start.2 = (bf16[128,1024]{1,0:T(8,128)(2,1)S(1)}, bf16[128,1024]{1,0:T(8,128)(2,1)}, u32[]{:S(2)}) copy-start(bf16[128,1024]{1,0:T(8,128)(2,1)} %q_hbm.1) | copy-start | bytes 786436
  2.1 0.9 %copy-start.3 = (bf16[64,2048]{1,0:T(8,128)(2,1)S(1)}, bf16[64,2048]{1,0:T(8,128)(2,1)}, u32[]{:S(2)}) copy-start(bf16[64,2048]{1,0:T(8,128)(2,1)} %g_hbm.1) | copy-start | bytes 786436
  3.2 7.7 %collective-permute-start.3 = (bf16[128,1024]{1,0:T(8,128)(2,1)S(1)}, bf16[128,1024]{1,0:T(8,128)(2,1)S(1)}, u32[]{:S(2)}, u32[]{:S(2)}) collective-permute-start(bf16[128,1024]{1,0:T(8,128)(2,1)S(1)} %get-tuple-element.24.own_ref), channel_id=1, source_target_pairs={{0,1},{1,0},{14,15},{15,14},{2,4},{3,5},{4,2},{5,3},{6,8},{7,9},{8... | collective-permute-start | bytes 786440 | tf_op jit(solution)/shard_map/ppermute | solution.py:289
  3.3 15.2 %collective-permute-start.1 = (bf16[128,1024]{1,0:T(8,128)(2,1)S(1)}, bf16[128,1024]{1,0:T(8,128)(2,1)S(1)}, u32[]{:S(2)}, u32[]{:S(2)}) collective-permute-start(bf16[128,1024]{1,0:T(8,128)(2,1)S(1)} %get-tuple-element.20), channel_id=1, source_target_pairs={{0,2},{2,0},{4,6},{6,4},{8,10},{10,8},{12,14},{14,12},{1,3},{3,1},... | collective-permute-start | bytes 786440 | tf_op jit(solution)/shard_map/ppermute | solution.py:288
  7.3 1.6 %copy-start = (bf16[1024,1024]{1,0:T(8,128)(2,1)S(1)}, bf16[1024,1024]{1,0:T(8,128)(2,1)}, u32[]{:S(2)}) copy-start(bf16[1024,1024]{1,0:T(8,128)(2,1)} %k_hbm.1) | copy-start | bytes 6291460
  8.9 1.6 %copy-start.1 = (bf16[1024,1024]{1,0:T(8,128)(2,1)S(1)}, bf16[1024,1024]{1,0:T(8,128)(2,1)}, u32[]{:S(2)}) copy-start(bf16[1024,1024]{1,0:T(8,128)(2,1)} %v_hbm.1) | copy-start | bytes 6291460
  13.3 13.4 %collective-permute-start.4 = (bf16[64,1024]{1,0:T(8,128)(2,1)S(1)}, bf16[64,1024]{1,0:T(8,128)(2,1)S(1)}, u32[]{:S(2)}, u32[]{:S(2)}) collective-permute-start(bf16[64,1024]{1,0:T(8,128)(2,1)S(1)} %get-tuple-element.25.own_ref), channel_id=1, source_target_pairs={{0,1},{1,0},{14,15},{15,14},{2,4},{3,5},{4,2},{5,3},{6,8},{7,9},{8... | collective-permute-start | bytes 393224 | tf_op jit(solution)/shard_map/ppermute | solution.py:292
  21.0 6.5 %collective-permute-start.2 = (bf16[64,1024]{1,0:T(8,128)(2,1)S(1)}, bf16[64,1024]{1,0:T(8,128)(2,1)S(1)}, u32[]{:S(2)}, u32[]{:S(2)}) collective-permute-start(bf16[64,1024]{1,0:T(8,128)(2,1)S(1)} %get-tuple-element.23), channel_id=1, source_target_pairs={{0,2},{2,0},{4,6},{6,4},{8,10},{10,8},{12,14},{14,12},{1,3},{3,1},... | collective-permute-start | bytes 393224 | tf_op jit(solution)/shard_map/ppermute | solution.py:294

commit v5 on v4

--- a/solution.py
+++ b/solution.py
@@ -53,32 +53,39 @@
     )(queries, out_grad)
 
 
-def pack_kernel(q_ref, own_ref, other_ref, inside_ref, across_ref):
+def pack_kernel(q_ref, own_ref, other_ref, left_ref, right_ref, across_ref):
     width = q_ref.shape[1]
     odd = lax.axis_index("seq") % 2
     core = lax.axis_index("tp")
     cols = pl.ds(pl.multiple_of(core * width, HD), width)
-    inside_ref[:BLK] = q_ref[pl.ds(pl.multiple_of((1 - odd) * BLK, BLK), BLK), :]
+    half = width // 2
+    rows = pl.ds(pl.multiple_of((1 - odd) * BLK, BLK), BLK)
+    left_ref[:BLK] = q_ref[rows, :half]
+    right_ref[:BLK] = q_ref[rows, half:]
     across_ref[:BLK] = q_ref[pl.ds(pl.multiple_of(odd * BLK, BLK), BLK), :]
+    lefts = pl.ds(pl.multiple_of(core * width, HD), half)
+    rights = pl.ds(pl.multiple_of(core * width + half, HD), half)
 
     @pl.when(core != odd)
     def _():
-        inside_ref[BLK:] = own_ref[:, cols]
+        left_ref[BLK:] = own_ref[:, lefts]
+        right_ref[BLK:] = own_ref[:, rights]
         across_ref[BLK:] = other_ref[:, cols]
 
     @pl.when(core == odd)
     def _():
-        inside_ref[BLK:] = other_ref[:, cols]
+        left_ref[BLK:] = other_ref[:, lefts]
+        right_ref[BLK:] = other_ref[:, rights]
         across_ref[BLK:] = own_ref[:, cols]
 
 
 def pack(queries, own, other):
-    part = jax.ShapeDtypeStruct(queries.shape, queries.dtype)
+    rows, width = queries.shape
     return pl.pallas_call(
         pack_kernel,
         in_specs=[WHOLE] * 3,
-        out_specs=[WHOLE] * 2,
-        out_shape=[part] * 2,
+        out_specs=[WHOLE] * 3,
+        out_shape=[jax.ShapeDtypeStruct((rows, cols), queries.dtype) for cols in (width // 2, width // 2, width)],
         compiler_params=params(8),
         name="pack",
     )(queries, own, other)
@@ -116,8 +123,15 @@
     return (index == 0) | (index == lax.axis_size("seq") - 1)
 
 
-def attend_inside_kernel(m_ref, k_ref, v_ref, gq_ref, p_ref, ds_ref):
-    attend_body(m_ref, k_ref, v_ref, gq_ref, p_ref, ds_ref)
+def attend_left_kernel(m_ref, after_ref, k_ref, v_ref, gq_ref, p_ref, ds_ref):
+    del after_ref
+    attend_body(m_ref, k_ref, v_ref, gq_ref, p_ref, ds_ref, 0)
+
+
+def attend_right_kernel(m_ref, left_ref, k_ref, v_ref, gq_ref, p_ref, ds_ref):
+    start = left_ref.shape[1]
+    gq_ref[:, :start] = left_ref[...]
+    attend_body(m_ref, k_ref, v_ref, gq_ref.at[:, start:], p_ref, ds_ref, start)
 
 
 def attend_across_kernel(own_ref, received_ref, k_ref, v_ref, gq_ref, p_ref, ds_ref, m_ref):
@@ -129,20 +143,21 @@
     def _():
         m_ref[...] = received_ref[...]
 
-    attend_body(m_ref, k_ref, v_ref, gq_ref, p_ref, ds_ref)
-
-
-def attend_body(m_ref, k_ref, v_ref, gq_ref, p_ref, ds_ref):
+    attend_body(m_ref, k_ref, v_ref, gq_ref, p_ref, ds_ref, 0)
+
+
+def attend_body(m_ref, k_ref, v_ref, gq_ref, p_ref, ds_ref, start):
     pairs = m_ref.shape[1] // PAIR
     held = {}
 
     def products(j):
         cols = pl.ds(j * PAIR, PAIR)
+        window = pl.ds(start + j * PAIR, PAIR)
         scores = lax.dot_general(
-            k_ref[:, cols], diagonal(m_ref[:BLK, cols]), LAST, preferred_element_type=jnp.float32
+            k_ref[:, window], diagonal(m_ref[:BLK, cols]), LAST, preferred_element_type=jnp.float32
         )
         dprobs = lax.dot_general(
-            v_ref[:, cols], diagonal(m_ref[BLK:, cols]), LAST, preferred_element_type=jnp.float32
+            v_ref[:, window], diagonal(m_ref[BLK:, cols]), LAST, preferred_element_type=jnp.float32
         )
         held[j] = (scores, jnp.max(scores, axis=0, keepdims=True), dprobs)
 
@@ -160,7 +175,7 @@
         dscores = (grown * (SCALE * inverse) * (dprobs - delta)).astype(jnp.bfloat16)
         ds_ref[:, cols] = dscores
         both = lax.dot_general(
-            dscores, k_ref[:, pl.ds(j * PAIR, PAIR)], FIRST, preferred_element_type=jnp.float32
+            dscores, k_ref[:, pl.ds(start + j * PAIR, PAIR)], FIRST, preferred_element_type=jnp.float32
         )
         gq_ref[:, pl.ds(j * PAIR, HD)] = both[:BLK, :HD].astype(jnp.bfloat16)
         gq_ref[:, pl.ds(j * PAIR + HD, HD)] = both[BLK:, HD:].astype(jnp.bfloat16)
@@ -171,49 +186,64 @@
                 stage_of(step - lag)
 
 
-def attend(kernel, messages, keys, values):
-    width = keys.shape[1]
-    staged = jax.ShapeDtypeStruct((WIN, width // HD * BLK), jnp.bfloat16)
+def attend(kernel, message, others, keys, values, width, copied=False):
+    heads = message.shape[1] // HD
+    staged = jax.ShapeDtypeStruct((WIN, heads * BLK), jnp.bfloat16)
     shapes = [jax.ShapeDtypeStruct((BLK, width), jnp.bfloat16), staged, staged]
-    if len(messages) == 2:
-        shapes.append(jax.ShapeDtypeStruct(messages[0].shape, messages[0].dtype))
+    if copied:
+        shapes.append(jax.ShapeDtypeStruct(message.shape, message.dtype))
     return pl.pallas_call(
         kernel,
-        in_specs=[WHOLE] * (len(messages) + 2),
+        in_specs=[WHOLE] * (len(others) + 3),
         out_specs=[WHOLE] * len(shapes),
         out_shape=shapes,
         compiler_params=params(32),
         cost_estimate=pl.CostEstimate(
-            flops=8 * BLK * WIN * width, bytes_accessed=6 * WIN * width, transcendentals=BLK * WIN * width // HD
+            flops=8 * BLK * WIN * HD * heads, bytes_accessed=6 * WIN * HD * heads, transcendentals=BLK * WIN * heads
         ),
         name="attend",
-    )(*messages, keys, values)
-
-
-def event_kernel(p0_ref, ds0_ref, m0_ref, p1_ref, ds1_ref, m1_ref, gk_ref, gv_ref):
-    step = pl.program_id(0)
-    probs = pl.ds(pl.multiple_of(step * 2 * BLK, 2 * BLK), 2 * BLK)
-    cols = pl.ds(pl.multiple_of(step * PAIR, PAIR), PAIR)
-
-    def product(a0, a1, b0, b1):
-        left = jnp.concatenate([a0, a1], axis=1)
-        right = jnp.concatenate([diagonal(b0), diagonal(b1)], axis=0)
-        return jnp.dot(left, right, preferred_element_type=jnp.float32).astype(jnp.bfloat16)
-
-    gk_ref[...] = product(ds0_ref[:, probs], ds1_ref[:, probs], m0_ref[:BLK, cols], m1_ref[:BLK, cols])
-    gv_ref[...] = product(p0_ref[:, probs], p1_ref[:, probs], m0_ref[BLK:, cols], m1_ref[BLK:, cols])
+    )(message, *others, keys, values)
+
+
+def event_kernel(pl_ref, dsl_ref, ml_ref, pr_ref, dsr_ref, mr_ref, p1_ref, ds1_ref, m1_ref, gk_hbm, gv_hbm, gk_ref, gv_ref, sems):
+    parts = sems.shape[1]
+    rows = WIN // parts
+    moves = []
+    pairs = gk_ref.shape[1] // PAIR
+    half = pairs // 2
+    for out, (left_ref, right_ref, a1, held, hbm, low) in enumerate(
+        ((dsl_ref, dsr_ref, ds1_ref, gk_ref, gk_hbm, 0), (pl_ref, pr_ref, p1_ref, gv_ref, gv_hbm, BLK))
+    ):
+        block = pl.ds(low, BLK)
+        rights = []
+        for j in range(pairs):
+            inside = (ml_ref if j < half else mr_ref)[block, pl.ds(j % half * PAIR, PAIR)]
+            across = m1_ref[block, pl.ds(j * PAIR, PAIR)]
+            rights.append(jnp.concatenate([diagonal(inside), diagonal(across)], axis=0))
+        for part in range(parts):
+            here = pl.ds(part * rows, rows)
+            for j, right in enumerate(rights):
+                inside = (left_ref if j < half else right_ref)[here, pl.ds(j % half * 2 * BLK, 2 * BLK)]
+                left = jnp.concatenate([inside, a1[here, pl.ds(j * 2 * BLK, 2 * BLK)]], axis=1)
+                held[here, pl.ds(j * PAIR, PAIR)] = jnp.dot(
+                    left, right, preferred_element_type=jnp.float32
+                ).astype(jnp.bfloat16)
+            move = pltpu.make_async_copy(held.at[here, :], hbm.at[here, :], sems.at[out, part])
+            move.start()
+            moves.append(move)
+    for move in moves:
+        move.wait()
 
 
 def event_grads(*args):
-    width = args[2].shape[1]
-    win = pl.BlockSpec((WIN, PAIR), lambda i: (0, i))
+    width = args[-1].shape[1]
     out = jax.ShapeDtypeStruct((WIN, width), jnp.bfloat16)
     return pl.pallas_call(
         event_kernel,
-        grid=(width // PAIR,),
-        in_specs=[WHOLE] * 6,
-        out_specs=[win, win],
-        out_shape=[out, out],
+        in_specs=[WHOLE] * 9,
+        out_specs=[RAW] * 2,
+        out_shape=[out] * 2,
+        scratch_shapes=[pltpu.VMEM((WIN, width), jnp.bfloat16)] * 2 + [pltpu.SemaphoreType.DMA((2, 4))],
         compiler_params=params(32),
         cost_estimate=pl.CostEstimate(
             flops=8 * BLK * WIN * width, bytes_accessed=8 * WIN * width, transcendentals=0
@@ -284,15 +314,17 @@
         across += [(2 * i + core, 2 * partner + core) for core in range(2)]
 
     other = lax.ppermute(out_grad, "tp", [(0, 1), (1, 0)])
-    first, second = pack(*load(queries, out_grad), other)
-    got_first = lax.ppermute(first, "seq", inside)
+    left, right, second = pack(*load(queries, out_grad), other)
     got_second = lax.ppermute(second, ("seq", "tp"), across)
+    got_left = lax.ppermute(left, "seq", inside)
+    got_right = lax.ppermute(right, "seq", inside)
     keys, values = stage(keys, values)
-    gq1, p1, ds1, used = attend(attend_across_kernel, [second, got_second], keys, values)
+    gq1, p1, ds1, used = attend(attend_across_kernel, second, [got_second], keys, values, width, True)
     back1 = lax.ppermute(gq1, ("seq", "tp"), across)
-    gq0, p0, ds0 = attend(attend_inside_kernel, [got_first], keys, values)
+    gql, *lefts = attend(attend_left_kernel, got_left, [p1], keys, values, width // 2)
+    gq0, *rights = attend(attend_right_kernel, got_right, [gql], keys, values, width)
     back0 = lax.ppermute(gq0, "seq", inside)
-    grad_keys, grad_values = event_grads(p0, ds0, got_first, p1, ds1, used)
+    grad_keys, grad_values = event_grads(*lefts, got_left, *rights, got_right, p1, ds1, used)
     return join_inside(back0, join_across(back1, gq1)), grad_keys, grad_values
 
 

time: 28.4 us -> 27.2 us (0.958)
  waiting for transfers between devices: 5.11 us -> 4.09 us
  Pallas kernels: 10 us -> 9.71 us
    ppermute x1 -> x2, waiting for transfers between devices: 5.1 us -> 3.54 us  [the longest x1 2.32 us: shards(): got_left = lax.ppermute(left, 'seq', inside)]
    ppermute x1, waiting for transfers between devices: 0.01 us -> 0.54 us  [shards(): back0 = lax.ppermute(gq0, 'seq', inside)]
    pallas_call x4 -> x5, Pallas kernels: 8.23 us -> 7.94 us  [the longest x3 5.52 us: attend(): pl.pallas_call(kernel, in_specs=[WHOLE] * (len(others) + 3), out_specs=[W...]
    ppermute x1 -> x2, starting transfers between devices: 3.99 us -> 4.02 us  [the longest x1 3.99 us: shards(): got_left = lax.ppermute(left, 'seq', inside)]
  transfers between devices with their start and end apart: 5 -> 6, of which waited for: 1 -> 3; matrix products, arithmetic and copies ran while one was open for 0% -> 0% of each run, Pallas kernels for 33% -> 33%
where the time goes in v5:
time: 27.2 us; the launch traced here: 27 us
  Pallas kernels  9.71 us (36%)
  starting transfers between devices  7.37 us (27%)
  local copies, waits for them, and re-layouts  5.08 us (19%)
  waiting for transfers between devices  4.09 us (15%)
  between operations  0.73 us (3%)
    pallas_call x3, Pallas kernels, attend(): pl.pallas_call(kernel, in_specs=[WHOLE] * (len(others) + 3), out_specs=[W...  5.52 us
    unnamed x8, local copies, waits for them, and re-layouts  5.08 us
    ppermute x1, starting transfers between devices, shards(): got_left = lax.ppermute(left, 'seq', inside)  3.99 us
    ppermute x1, starting transfers between devices, shards(): back0 = lax.ppermute(gq0, 'seq', inside)  2.64 us
    pallas_call x1, Pallas kernels, event_grads(): pl.pallas_call(event_kernel, in_specs=[WHOLE] * 9, out_specs=[RAW] * 2, o...  2.37 us
    ppermute x1, waiting for transfers between devices, shards(): got_left = lax.ppermute(left, 'seq', inside)  2.32 us
    ppermute x1, waiting for transfers between devices, shards(): got_right = lax.ppermute(right, 'seq', inside)  1.22 us
    pallas_call x1, Pallas kernels, join_across(): pl.pallas_call(join_across_kernel, in_specs=[WHOLE] * 2, out_specs=RAW, o...  0.68 us
  transfers between devices with their start and end apart: 6, of which 3 were waited for; matrix products, arithmetic and copies ran while one was open for 0% of the time, Pallas kernels for 33%

profile of v5, /device:TPU:0, one launch (start us, length us, event | category | flops | bytes accessed | tf_op | source)
XLA Modules:
  0.0 27.0 jit_solution(2328490250764513610)
XLA Ops:
  0.6 0.5 %collective-permute-start = (bf16[64,2048]{1,0:T(8,128)(2,1)}, bf16[64,2048]{1,0:T(8,128)(2,1)S(1)}, u32[]{:S(2)}, u32[]{:S(2)}) collective-permute-start(bf16[64,2048]{1,0:T(8,128)(2,1)} %g_hbm.1), channel_id=1, source_target_pairs={{0,1},{1,0},{2,3},{3,2},{4,5},{5,4},{6,7},{7,6},{8,9},{9,8},{10,11... | collective-permute-start | bytes 786440 | tf_op jit(solution)/shard_map/ppermute | solution.py:316
  1.1 0.0 copy-start.2
  1.1 0.9 %copy-done.2 = bf16[128,1024]{1,0:T(8,128)(2,1)S(1)} copy-done((bf16[128,1024]{1,0:T(8,128)(2,1)S(1)}, bf16[128,1024]{1,0:T(8,128)(2,1)}, u32[]{:S(2)}) %copy-start.2) | copy-done | bytes 262168
  2.1 0.0 copy-start.3
  2.1 0.9 %copy-done.3 = bf16[64,2048]{1,0:T(8,128)(2,1)S(1)} copy-done((bf16[64,2048]{1,0:T(8,128)(2,1)S(1)}, bf16[64,2048]{1,0:T(8,128)(2,1)}, u32[]{:S(2)}) %copy-start.3) | copy-done | bytes 262168
  3.0 0.1 load.1
  3.1 0.0 collective-permute-done.other_ref
  3.1 0.1 pack.1
  3.2 0.1 collective-permute-start.3
  3.3 4.0 %collective-permute-start.2 = (bf16[128,512]{1,0:T(8,128)(2,1)S(1)}, bf16[128,512]{1,0:T(8,128)(2,1)S(1)}, u32[]{:S(2)}, u32[]{:S(2)}) collective-permute-start(bf16[128,512]{1,0:T(8,128)(2,1)S(1)} %get-tuple-element.25), channel_id=1, source_target_pairs={{0,2},{2,0},{4,6},{6,4},{8,10},{10,8},{12,14},{14,12},{1,3},{3,1},... | collective-permute-start | bytes 393224 | tf_op jit(solution)/shard_map/ppermute | solution.py:319
  7.3 0.0 collective-permute-start.1
  7.3 0.0 copy-start
  7.3 1.6 %copy-done = bf16[1024,1024]{1,0:T(8,128)(2,1)S(1)} copy-done((bf16[1024,1024]{1,0:T(8,128)(2,1)S(1)}, bf16[1024,1024]{1,0:T(8,128)(2,1)}, u32[]{:S(2)}) %copy-start) | copy-done | bytes 2097176
  8.9 0.0 copy-start.1
  8.9 1.6 %copy-done.1 = bf16[1024,1024]{1,0:T(8,128)(2,1)S(1)} copy-done((bf16[1024,1024]{1,0:T(8,128)(2,1)S(1)}, bf16[1024,1024]{1,0:T(8,128)(2,1)}, u32[]{:S(2)}) %copy-start.1) | copy-done | bytes 2097176
  10.5 0.4 %stage.1 = (bf16[1024,1024]{1,0:T(8,128)(2,1)S(1)}, bf16[1024,1024]{1,0:T(8,128)(2,1)S(1)}) custom-call(bf16[1024,1024]{1,0:T(8,128)(2,1)S(1)} %copy-done, bf16[1024,1024]{1,0:T(8,128)(2,1)S(1)} %copy-done.1), custom_call_target="tpu_custom_call" | custom-call | bytes 8388608 | tf_op jit(solution)/shard_map/stage/pallas_call | solution.py:109
  10.9 0.0 collective-permute-done.3.received_ref
  10.9 2.5 %attend.3 = (bf16[64,1024]{1,0:T(8,128)(2,1)S(1)}, bf16[1024,512]{1,0:T(8,128)(2,1)S(1)}, bf16[1024,512]{1,0:T(8,128)(2,1)S(1)}, bf16[128,1024]{1,0:T(8,128)(2,1)S(1)}) custom-call(bf16[128,1024]{1,0:T(8,128)(2,1)S(1)} %get-tuple-element.26.own_ref, bf16[128,1024]{1,0:T(8,128)(2,1)S(1)} %collective-permute-done.3.received_ref, ...), custom_call_target="tpu_custom_call" | custom-call | flops 536870912 | bytes 6291456 | tf_op jit(solution)/shard_map/attend/pallas_call | solution.py:195
  13.4 0.1 collective-permute-start.5
  13.5 2.3 %collective-permute-done.2.m_ref.ml_ref = bf16[128,512]{1,0:T(8,128)(2,1)S(1)} collective-permute-done((bf16[128,512]{1,0:T(8,128)(2,1)S(1)}, bf16[128,512]{1,0:T(8,128)(2,1)S(1)}, u32[]{:S(2)}, u32[]{:S(2)}) %collective-permute-start.2) | collective-permute-done | bytes 131104 | tf_op jit(solution)/shard_map/ppermute | solution.py:319
  15.8 1.5 %attend.4 = (bf16[64,512]{1,0:T(8,128)(2,1)S(1)}, bf16[1024,256]{1,0:T(8,128)(2,1)S(1)}, bf16[1024,256]{1,0:T(8,128)(2,1)S(1)}) custom-call(bf16[128,512]{1,0:T(8,128)(2,1)S(1)} %collective-permute-done.2.m_ref.ml_ref, bf16[1024,512]{1,0:T(8,128)(2,1)S(1)} %get-tuple-element.29.after_ref.p1_ref, bf16[1024,1024]{1,0:T(8,128)(2,1)S(1)} %get-tuple-element.27.k_ref, ...), custom_call_target="tpu_custom_call" | custom-call | flops 268435456 | bytes 3145728 | tf_op jit(solution)/shard_map/attend/pallas_call | solution.py:195
  17.3 1.2 %collective-permute-done.1.m_ref.mr_ref = bf16[128,512]{1,0:T(8,128)(2,1)S(1)} collective-permute-done((bf16[128,512]{1,0:T(8,128)(2,1)S(1)}, bf16[128,512]{1,0:T(8,128)(2,1)S(1)}, u32[]{:S(2)}, u32[]{:S(2)}) %collective-permute-start.1) | collective-permute-done | bytes 131104 | tf_op jit(solution)/shard_map/ppermute | solution.py:320
  18.5 1.5 %attend.5 = (bf16[64,1024]{1,0:T(8,128)(2,1)S(1)}, bf16[1024,256]{1,0:T(8,128)(2,1)S(1)}, bf16[1024,256]{1,0:T(8,128)(2,1)S(1)}) custom-call(bf16[128,512]{1,0:T(8,128)(2,1)S(1)} %collective-permute-done.1.m_ref.mr_ref, bf16[64,512]{1,0:T(8,128)(2,1)S(1)} %get-tuple-element.30.left_ref, bf16[1024,1024]{1,0:T(8,128)(2,1)S(1)} %get-tuple-element.27.k_ref, ...), custom_call_target="tpu_custom_call" | custom-call | flops 268435456 | bytes 3145728 | tf_op jit(solution)/shard_map/attend/pallas_call | solution.py:195
  20.1 2.6 %collective-permute-start.4 = (bf16[64,1024]{1,0:T(8,128)(2,1)S(1)}, bf16[64,1024]{1,0:T(8,128)(2,1)S(1)}, u32[]{:S(2)}, u32[]{:S(2)}) collective-permute-start(bf16[64,1024]{1,0:T(8,128)(2,1)S(1)} %get-tuple-element.31), channel_id=1, source_target_pairs={{0,2},{2,0},{4,6},{6,4},{8,10},{10,8},{12,14},{14,12},{1,3},{3,1},... | collective-permute-start | bytes 393224 | tf_op jit(solution)/shard_map/ppermute | solution.py:326
  22.7 2.4 %event_grads.1 = (bf16[1024,1024]{1,0:T(8,128)(2,1)}, bf16[1024,1024]{1,0:T(8,128)(2,1)}) custom-call(bf16[1024,256]{1,0:T(8,128)(2,1)S(1)} %get-tuple-element.33.pl_ref, bf16[1024,256]{1,0:T(8,128)(2,1)S(1)} %get-tuple-element.34.dsl_ref, bf16[128,512]{1,0:T(8,128)(2,1)S(1)} %collective-permute-done.2.m_ref.ml_ref, ...), custom_call_target="tpu_custom_call" | custom-call | flops 536870912 | bytes 8388608 | tf_op jit(solution)/shard_map/event_grads/pallas_call | solution.py:241
  25.1 0.0 collective-permute-done.5.across_ref
  25.1 0.7 %join_across.1.half_hbm = bf16[128,1024]{1,0:T(8,128)(2,1)} custom-call(bf16[64,1024]{1,0:T(8,128)(2,1)S(1)} %collective-permute-done.5.across_ref, bf16[64,1024]{1,0:T(8,128)(2,1)S(1)} %get-tuple-element.32.own_ref), custom_call_target="tpu_custom_call" | custom-call | tf_op jit(solution)/shard_map/join_across/pallas_call | solution.py:281
  25.8 0.5 %collective-permute-done.4.inside_ref = bf16[64,1024]{1,0:T(8,128)(2,1)S(1)} collective-permute-done((bf16[64,1024]{1,0:T(8,128)(2,1)S(1)}, bf16[64,1024]{1,0:T(8,128)(2,1)S(1)}, u32[]{:S(2)}, u32[]{:S(2)}) %collective-permute-start.4) | collective-permute-done | bytes 131104 | tf_op jit(solution)/shard_map/ppermute | solution.py:326
  26.3 0.7 %join_inside.1 = bf16[128,1024]{1,0:T(8,128)(2,1)} custom-call(bf16[64,1024]{1,0:T(8,128)(2,1)S(1)} %collective-permute-done.4.inside_ref, bf16[128,1024]{1,0:T(8,128)(2,1)} %join_across.1.half_hbm), custom_call_target="tpu_custom_call", output_to_operand_aliasing={{}: (1, {})} | custom-call | tf_op jit(solution)/shard_map/join_inside/pallas_call | solution.py:293
Async XLA Ops:
  0.6 2.5 %collective-permute-start = (bf16[64,2048]{1,0:T(8,128)(2,1)}, bf16[64,2048]{1,0:T(8,128)(2,1)S(1)}, u32[]{:S(2)}, u32[]{:S(2)}) collective-permute-start(bf16[64,2048]{1,0:T(8,128)(2,1)} %g_hbm.1), channel_id=1, source_target_pairs={{0,1},{1,0},{2,3},{3,2},{4,5},{5,4},{6,7},{7,6},{8,9},{9,8},{10,11... | collective-permute-start | bytes 786440 | tf_op jit(solution)/shard_map/ppermute | solution.py:316
  1.1 0.9 %copy-start.2 = (bf16[128,1024]{1,0:T(8,128)(2,1)S(1)}, bf16[128,1024]{1,0:T(8,128)(2,1)}, u32[]{:S(2)}) copy-start(bf16[128,1024]{1,0:T(8,128)(2,1)} %q_hbm.1) | copy-start | bytes 786436
  2.1 0.9 %copy-start.3 = (bf16[64,2048]{1,0:T(8,128)(2,1)S(1)}, bf16[64,2048]{1,0:T(8,128)(2,1)}, u32[]{:S(2)}) copy-start(bf16[64,2048]{1,0:T(8,128)(2,1)} %g_hbm.1) | copy-start | bytes 786436
  3.2 7.7 %collective-permute-start.3 = (bf16[128,1024]{1,0:T(8,128)(2,1)S(1)}, bf16[128,1024]{1,0:T(8,128)(2,1)S(1)}, u32[]{:S(2)}, u32[]{:S(2)}) collective-permute-start(bf16[128,1024]{1,0:T(8,128)(2,1)S(1)} %get-tuple-element.26.own_ref), channel_id=1, source_target_pairs={{0,1},{1,0},{14,15},{15,14},{2,4},{3,5},{4,2},{5,3},{6,8},{7,9},{8... | collective-permute-start | bytes 786440 | tf_op jit(solution)/shard_map/ppermute | solution.py:318
  3.3 12.5 %collective-permute-start.2 = (bf16[128,512]{1,0:T(8,128)(2,1)S(1)}, bf16[128,512]{1,0:T(8,128)(2,1)S(1)}, u32[]{:S(2)}, u32[]{:S(2)}) collective-permute-start(bf16[128,512]{1,0:T(8,128)(2,1)S(1)} %get-tuple-element.25), channel_id=1, source_target_pairs={{0,2},{2,0},{4,6},{6,4},{8,10},{10,8},{12,14},{14,12},{1,3},{3,1},... | collective-permute-start | bytes 393224 | tf_op jit(solution)/shard_map/ppermute | solution.py:319
  7.3 11.2 %collective-permute-start.1 = (bf16[128,512]{1,0:T(8,128)(2,1)S(1)}, bf16[128,512]{1,0:T(8,128)(2,1)S(1)}, u32[]{:S(2)}, u32[]{:S(2)}) collective-permute-start(bf16[128,512]{1,0:T(8,128)(2,1)S(1)} %get-tuple-element.24), channel_id=1, source_target_pairs={{0,2},{2,0},{4,6},{6,4},{8,10},{10,8},{12,14},{14,12},{1,3},{3,1},... | collective-permute-start | bytes 393224 | tf_op jit(solution)/shard_map/ppermute | solution.py:320
  7.3 1.6 %copy-start = (bf16[1024,1024]{1,0:T(8,128)(2,1)S(1)}, bf16[1024,1024]{1,0:T(8,128)(2,1)}, u32[]{:S(2)}) copy-start(bf16[1024,1024]{1,0:T(8,128)(2,1)} %k_hbm.1) | copy-start | bytes 6291460
  8.9 1.6 %copy-start.1 = (bf16[1024,1024]{1,0:T(8,128)(2,1)S(1)}, bf16[1024,1024]{1,0:T(8,128)(2,1)}, u32[]{:S(2)}) copy-start(bf16[1024,1024]{1,0:T(8,128)(2,1)} %v_hbm.1) | copy-start | bytes 6291460
  13.4 11.7 %collective-permute-start.5 = (bf16[64,1024]{1,0:T(8,128)(2,1)S(1)}, bf16[64,1024]{1,0:T(8,128)(2,1)S(1)}, u32[]{:S(2)}, u32[]{:S(2)}) collective-permute-start(bf16[64,1024]{1,0:T(8,128)(2,1)S(1)} %get-tuple-element.32.own_ref), channel_id=1, source_target_pairs={{0,1},{1,0},{14,15},{15,14},{2,4},{3,5},{4,2},{5,3},{6,8},{7,9},{8... | collective-permute-start | bytes 393224 | tf_op jit(solution)/shard_map/ppermute | solution.py:323
  20.1 6.3 %collective-permute-start.4 = (bf16[64,1024]{1,0:T(8,128)(2,1)S(1)}, bf16[64,1024]{1,0:T(8,128)(2,1)S(1)}, u32[]{:S(2)}, u32[]{:S(2)}) collective-permute-start(bf16[64,1024]{1,0:T(8,128)(2,1)S(1)} %get-tuple-element.31), channel_id=1, source_target_pairs={{0,2},{2,0},{4,6},{6,4},{8,10},{10,8},{12,14},{14,12},{1,3},{3,1},... | collective-permute-start | bytes 393224 | tf_op jit(solution)/shard_map/ppermute | solution.py:326

commit v6 on v5

--- a/solution.py
+++ b/solution.py
@@ -23,6 +23,10 @@
     return pltpu.CompilerParams(vmem_limit_bytes=mib << 20)
 
 
+def pinned(array):
+    return pltpu.with_memory_space_constraint(array, pltpu.HBM)
+
+
 def diagonal(rows):
     zeros = jnp.zeros((BLK, HD), rows.dtype)
     top = jnp.concatenate([rows[:, :HD], zeros], axis=1)
@@ -50,7 +54,7 @@
         scratch_shapes=[pltpu.SemaphoreType.DMA((2,))],
         compiler_params=params(8),
         name="load",
-    )(queries, out_grad)
+    )(pinned(queries), pinned(out_grad))
 
 
 def pack_kernel(q_ref, own_ref, other_ref, left_ref, right_ref, across_ref):
@@ -115,7 +119,7 @@
         compiler_params=params(16),
         cost_estimate=pl.CostEstimate(flops=0, bytes_accessed=8 * keys.size, transcendentals=0),
         name="stage",
-    )(keys, values)
+    )(pinned(keys), pinned(values))
 
 
 def at_end():
@@ -186,12 +190,28 @@
                 stage_of(step - lag)
 
 
-def attend(kernel, message, others, keys, values, width, copied=False):
+def after_kernel(array_ref, message_ref, out_ref):
+    del message_ref
+    out_ref[...] = array_ref[...]
+
+
+def after(array, message):
+    return pl.pallas_call(
+        after_kernel,
+        in_specs=[WHOLE] * 2,
+        out_specs=WHOLE,
+        out_shape=jax.ShapeDtypeStruct(array.shape, array.dtype),
+        compiler_params=params(8),
+        name="after",
+    )(array, message)
+
+
+def attend(kernel, message, others, keys, values, width, copied=None):
     heads = message.shape[1] // HD
     staged = jax.ShapeDtypeStruct((WIN, heads * BLK), jnp.bfloat16)
     shapes = [jax.ShapeDtypeStruct((BLK, width), jnp.bfloat16), staged, staged]
-    if copied:
-        shapes.append(jax.ShapeDtypeStruct(message.shape, message.dtype))
+    if copied is not None:
+        shapes.append(jax.ShapeDtypeStruct(copied.shape, copied.dtype))
     return pl.pallas_call(
         kernel,
         in_specs=[WHOLE] * (len(others) + 3),
@@ -319,9 +339,10 @@
     got_left = lax.ppermute(left, "seq", inside)
     got_right = lax.ppermute(right, "seq", inside)
     keys, values = stage(keys, values)
-    gq1, p1, ds1, used = attend(attend_across_kernel, second, [got_second], keys, values, width, True)
-    back1 = lax.ppermute(gq1, ("seq", "tp"), across)
-    gql, *lefts = attend(attend_left_kernel, got_left, [p1], keys, values, width // 2)
+    gq1, p1, ds1, used = attend(attend_across_kernel, second, [got_second], keys, values, width, second)
+    sent = after(gq1, got_left)
+    back1 = lax.ppermute(sent, ("seq", "tp"), across)
+    gql, *lefts = attend(attend_left_kernel, got_left, [sent], keys, values, width // 2)
     gq0, *rights = attend(attend_right_kernel, got_right, [gql], keys, values, width)
     back0 = lax.ppermute(gq0, "seq", inside)
     grad_keys, grad_values = event_grads(*lefts, got_left, *rights, got_right, p1, ds1, used)

time: 27.2 us -> 26.5 us (0.974)
  local copies, waits for them, and re-layouts: 5.08 us -> 0 us
  Pallas kernels: 9.71 us -> 12.5 us
  waiting for transfers between devices: 4.09 us -> 5.05 us
  starting transfers between devices: 7.37 us -> 8.07 us
    unnamed x8 -> x0, local copies, waits for them, and re-layouts: 5.08 us -> none
    pallas_call x1, Pallas kernels: 0.37 us -> 2.21 us  [stage(): pl.pallas_call(stage_kernel, in_specs=[RAW] * 2, out_specs=[WHOLE] * 2, o...]
    ppermute x1, waiting for transfers between devices: 2.32 us -> 3.4 us  [shards(): got_left = lax.ppermute(left, 'seq', inside)]
    pallas_call x1, Pallas kernels: 0.06 us -> 1.04 us  [load(): pl.pallas_call(load_kernel, in_specs=[RAW] * 2, out_specs=[WHOLE] * 2, ou...]
    ppermute x1, starting transfers between devices: 2.64 us -> 2.97 us  [shards(): back0 = lax.ppermute(gq0, 'seq', inside)]
    ppermute x1, waiting for transfers between devices: 0.01 us -> 0.32 us  [shards(): other = lax.ppermute(out_grad, 'tp', [(0, 1), (1, 0)])]
    ppermute x1, starting transfers between devices: 0.12 us -> 0.44 us  [shards(): got_second = lax.ppermute(second, ('seq', 'tp'), across)]
    ppermute x1, waiting for transfers between devices: 0.54 us -> 0.23 us  [shards(): back0 = lax.ppermute(gq0, 'seq', inside)]
  transfers between devices with their start and end apart: 6 -> 6, of which waited for: 3 -> 4; matrix products, arithmetic and copies ran while one was open for 0% -> 0% of each run, Pallas kernels for 33% -> 45%
where the time goes in v6:
time: 26.5 us; the launch traced here: 26.4 us
  Pallas kernels  12.5 us (47%)
  starting transfers between devices  8.07 us (30%)
  waiting for transfers between devices  5.05 us (19%)
  between operations  0.72 us (3%)
    pallas_call x3, Pallas kernels, attend(): pl.pallas_call(kernel, in_specs=[WHOLE] * (len(others) + 3), out_specs=[W...  5.52 us
    ppermute x1, starting transfers between devices, shards(): got_left = lax.ppermute(left, 'seq', inside)  4.03 us
    ppermute x1, waiting for transfers between devices, shards(): got_left = lax.ppermute(left, 'seq', inside)  3.4 us
    ppermute x1, starting transfers between devices, shards(): back0 = lax.ppermute(gq0, 'seq', inside)  2.97 us
    pallas_call x1, Pallas kernels, event_grads(): pl.pallas_call(event_kernel, in_specs=[WHOLE] * 9, out_specs=[RAW] * 2, o...  2.37 us
    pallas_call x1, Pallas kernels, stage(): pl.pallas_call(stage_kernel, in_specs=[RAW] * 2, out_specs=[WHOLE] * 2, o...  2.21 us
    ppermute x1, waiting for transfers between devices, shards(): got_right = lax.ppermute(right, 'seq', inside)  1.1 us
    pallas_call x1, Pallas kernels, load(): pl.pallas_call(load_kernel, in_specs=[RAW] * 2, out_specs=[WHOLE] * 2, ou...  1.04 us
  transfers between devices with their start and end apart: 6, of which 4 were waited for; matrix products, arithmetic and copies ran while one was open for 0% of the time, Pallas kernels for 45%

profile of v6, /device:TPU:0, one launch (start us, length us, event | category | flops | bytes accessed | tf_op | source)
XLA Modules:
  0.0 26.4 jit_solution(15124748165396970783)
XLA Ops:
  0.6 0.5 %collective-permute-start = (bf16[64,2048]{1,0:T(8,128)(2,1)}, bf16[64,2048]{1,0:T(8,128)(2,1)S(1)}, u32[]{:S(2)}, u32[]{:S(2)}) collective-permute-start(bf16[64,2048]{1,0:T(8,128)(2,1)} %g_hbm.1), channel_id=1, source_target_pairs={{0,1},{1,0},{2,3},{3,2},{4,5},{5,4},{6,7},{7,6},{8,9},{9,8},{10,11... | collective-permute-start | bytes 786440 | tf_op jit(solution)/shard_map/ppermute | solution.py:336
  1.1 1.0 %load.1 = (bf16[128,1024]{1,0:T(8,128)(2,1)S(1)}, bf16[64,2048]{1,0:T(8,128)(2,1)S(1)}) custom-call(bf16[128,1024]{1,0:T(8,128)(2,1)} %q_hbm.1, bf16[64,2048]{1,0:T(8,128)(2,1)} %g_hbm.1), custom_call_target="tpu_custom_call" | custom-call | tf_op jit(solution)/shard_map/load/pallas_call | solution.py:49
  2.2 0.3 %collective-permute-done.other_ref = bf16[64,2048]{1,0:T(8,128)(2,1)S(1)} collective-permute-done((bf16[64,2048]{1,0:T(8,128)(2,1)}, bf16[64,2048]{1,0:T(8,128)(2,1)S(1)}, u32[]{:S(2)}, u32[]{:S(2)}) %collective-permute-start) | collective-permute-done | bytes 262176 | tf_op jit(solution)/shard_map/ppermute | solution.py:336
  2.6 0.4 %collective-permute-start.3 = (bf16[128,1024]{1,0:T(8,128)(2,1)S(1)}, bf16[128,1024]{1,0:T(8,128)(2,1)S(1)}, u32[]{:S(2)}, u32[]{:S(2)}) collective-permute-start(bf16[128,1024]{1,0:T(8,128)(2,1)S(1)} %get-tuple-element.26.own_ref), channel_id=1, source_target_pairs={{0,1},{1,0},{14,15},{15,14},{2,4},{3,5},{4,2},{5,3},{6,8},{7,9},{8... | collective-permute-start | bytes 786440 | tf_op jit(solution)/shard_map/ppermute | solution.py:338
  3.0 4.0 %collective-permute-start.2 = (bf16[128,512]{1,0:T(8,128)(2,1)S(1)}, bf16[128,512]{1,0:T(8,128)(2,1)S(1)}, u32[]{:S(2)}, u32[]{:S(2)}) collective-permute-start(bf16[128,512]{1,0:T(8,128)(2,1)S(1)} %get-tuple-element.25), channel_id=1, source_target_pairs={{0,2},{2,0},{4,6},{6,4},{8,10},{10,8},{12,14},{14,12},{1,3},{3,1},... | collective-permute-start | bytes 393224 | tf_op jit(solution)/shard_map/ppermute | solution.py:339
  7.0 0.0 collective-permute-start.1
  7.1 2.2 %stage.1 = (bf16[1024,1024]{1,0:T(8,128)(2,1)S(1)}, bf16[1024,1024]{1,0:T(8,128)(2,1)S(1)}) custom-call(bf16[1024,1024]{1,0:T(8,128)(2,1)} %k_hbm.1, bf16[1024,1024]{1,0:T(8,128)(2,1)} %v_hbm.1), custom_call_target="tpu_custom_call" | custom-call | bytes 8388608 | tf_op jit(solution)/shard_map/stage/pallas_call | solution.py:113
  9.3 0.0 collective-permute-done.3.received_ref
  9.3 2.5 %attend.3 = (bf16[64,1024]{1,0:T(8,128)(2,1)S(1)}, bf16[1024,512]{1,0:T(8,128)(2,1)S(1)}, bf16[1024,512]{1,0:T(8,128)(2,1)S(1)}, bf16[128,1024]{1,0:T(8,128)(2,1)S(1)}) custom-call(bf16[128,1024]{1,0:T(8,128)(2,1)S(1)} %get-tuple-element.26.own_ref, bf16[128,1024]{1,0:T(8,128)(2,1)S(1)} %collective-permute-done.3.received_ref, ...), custom_call_target="tpu_custom_call" | custom-call | flops 536870912 | bytes 6291456 | tf_op jit(solution)/shard_map/attend/pallas_call | solution.py:215
  11.8 3.4 %collective-permute-done.2.message_ref.m_ref.ml_ref = bf16[128,512]{1,0:T(8,128)(2,1)S(1)} collective-permute-done((bf16[128,512]{1,0:T(8,128)(2,1)S(1)}, bf16[128,512]{1,0:T(8,128)(2,1)S(1)}, u32[]{:S(2)}, u32[]{:S(2)}) %collective-permute-start.2) | collective-permute-done | bytes 131104 | tf_op jit(solution)/shard_map/ppermute | solution.py:339
  15.2 0.1 collective-permute-start.5
  15.3 1.5 %attend.4 = (bf16[64,512]{1,0:T(8,128)(2,1)S(1)}, bf16[1024,256]{1,0:T(8,128)(2,1)S(1)}, bf16[1024,256]{1,0:T(8,128)(2,1)S(1)}) custom-call(bf16[128,512]{1,0:T(8,128)(2,1)S(1)} %collective-permute-done.2.message_ref.m_ref.ml_ref, bf16[64,1024]{1,0:T(8,128)(2,1)S(1)} %after.1.after_ref, bf16[1024,1024]{1,0:T(8,128)(2,1)S(1)} %get-tuple-element.27.k_ref, ...), custom_call_target="tpu_custom_call" | custom-call | flops 268435456 | bytes 3145728 | tf_op jit(solution)/shard_map/attend/pallas_call | solution.py:215
  16.8 1.1 %collective-permute-done.1.m_ref.mr_ref = bf16[128,512]{1,0:T(8,128)(2,1)S(1)} collective-permute-done((bf16[128,512]{1,0:T(8,128)(2,1)S(1)}, bf16[128,512]{1,0:T(8,128)(2,1)S(1)}, u32[]{:S(2)}, u32[]{:S(2)}) %collective-permute-start.1) | collective-permute-done | bytes 131104 | tf_op jit(solution)/shard_map/ppermute | solution.py:340
  17.9 1.5 %attend.5 = (bf16[64,1024]{1,0:T(8,128)(2,1)S(1)}, bf16[1024,256]{1,0:T(8,128)(2,1)S(1)}, bf16[1024,256]{1,0:T(8,128)(2,1)S(1)}) custom-call(bf16[128,512]{1,0:T(8,128)(2,1)S(1)} %collective-permute-done.1.m_ref.mr_ref, bf16[64,512]{1,0:T(8,128)(2,1)S(1)} %get-tuple-element.30.left_ref, bf16[1024,1024]{1,0:T(8,128)(2,1)S(1)} %get-tuple-element.27.k_ref, ...), custom_call_target="tpu_custom_call" | custom-call | flops 268435456 | bytes 3145728 | tf_op jit(solution)/shard_map/attend/pallas_call | solution.py:215
  19.4 3.0 %collective-permute-start.4 = (bf16[64,1024]{1,0:T(8,128)(2,1)S(1)}, bf16[64,1024]{1,0:T(8,128)(2,1)S(1)}, u32[]{:S(2)}, u32[]{:S(2)}) collective-permute-start(bf16[64,1024]{1,0:T(8,128)(2,1)S(1)} %get-tuple-element.31), channel_id=1, source_target_pairs={{0,2},{2,0},{4,6},{6,4},{8,10},{10,8},{12,14},{14,12},{1,3},{3,1},... | collective-permute-start | bytes 393224 | tf_op jit(solution)/shard_map/ppermute | solution.py:347
  22.4 2.4 %event_grads.1 = (bf16[1024,1024]{1,0:T(8,128)(2,1)}, bf16[1024,1024]{1,0:T(8,128)(2,1)}) custom-call(bf16[1024,256]{1,0:T(8,128)(2,1)S(1)} %get-tuple-element.32.pl_ref, bf16[1024,256]{1,0:T(8,128)(2,1)S(1)} %get-tuple-element.33.dsl_ref, bf16[128,512]{1,0:T(8,128)(2,1)S(1)} %collective-permute-done.2.message_ref.m_ref.ml_ref, ...), custom_call_target="tpu_custom_call" | custom-call | flops 536870912 | bytes 8388608 | tf_op jit(solution)/shard_map/event_grads/pallas_call | solution.py:261
  24.8 0.0 collective-permute-done.5.across_ref
  24.8 0.7 %join_across.1.half_hbm = bf16[128,1024]{1,0:T(8,128)(2,1)} custom-call(bf16[64,1024]{1,0:T(8,128)(2,1)S(1)} %collective-permute-done.5.across_ref, bf16[64,1024]{1,0:T(8,128)(2,1)S(1)} %get-tuple-element.29.array_ref.own_ref), custom_call_target="tpu_custom_call" | custom-call | tf_op jit(solution)/shard_map/join_across/pallas_call | solution.py:301
  25.5 0.2 collective-permute-done.4.inside_ref
  25.7 0.7 %join_inside.1 = bf16[128,1024]{1,0:T(8,128)(2,1)} custom-call(bf16[64,1024]{1,0:T(8,128)(2,1)S(1)} %collective-permute-done.4.inside_ref, bf16[128,1024]{1,0:T(8,128)(2,1)} %join_across.1.half_hbm), custom_call_target="tpu_custom_call", output_to_operand_aliasing={{}: (1, {})} | custom-call | tf_op jit(solution)/shard_map/join_inside/pallas_call | solution.py:313
  (2 shorter events, 0.0 us)
Async XLA Ops:
  0.6 1.9 %collective-permute-start = (bf16[64,2048]{1,0:T(8,128)(2,1)}, bf16[64,2048]{1,0:T(8,128)(2,1)S(1)}, u32[]{:S(2)}, u32[]{:S(2)}) collective-permute-start(bf16[64,2048]{1,0:T(8,128)(2,1)} %g_hbm.1), channel_id=1, source_target_pairs={{0,1},{1,0},{2,3},{3,2},{4,5},{5,4},{6,7},{7,6},{8,9},{9,8},{10,11... | collective-permute-start | bytes 786440 | tf_op jit(solution)/shard_map/ppermute | solution.py:336
  2.6 6.7 %collective-permute-start.3 = (bf16[128,1024]{1,0:T(8,128)(2,1)S(1)}, bf16[128,1024]{1,0:T(8,128)(2,1)S(1)}, u32[]{:S(2)}, u32[]{:S(2)}) collective-permute-start(bf16[128,1024]{1,0:T(8,128)(2,1)S(1)} %get-tuple-element.26.own_ref), channel_id=1, source_target_pairs={{0,1},{1,0},{14,15},{15,14},{2,4},{3,5},{4,2},{5,3},{6,8},{7,9},{8... | collective-permute-start | bytes 786440 | tf_op jit(solution)/shard_map/ppermute | solution.py:338
  3.0 12.2 %collective-permute-start.2 = (bf16[128,512]{1,0:T(8,128)(2,1)S(1)}, bf16[128,512]{1,0:T(8,128)(2,1)S(1)}, u32[]{:S(2)}, u32[]{:S(2)}) collective-permute-start(bf16[128,512]{1,0:T(8,128)(2,1)S(1)} %get-tuple-element.25), channel_id=1, source_target_pairs={{0,2},{2,0},{4,6},{6,4},{8,10},{10,8},{12,14},{14,12},{1,3},{3,1},... | collective-permute-start | bytes 393224 | tf_op jit(solution)/shard_map/ppermute | solution.py:339
  7.0 10.9 %collective-permute-start.1 = (bf16[128,512]{1,0:T(8,128)(2,1)S(1)}, bf16[128,512]{1,0:T(8,128)(2,1)S(1)}, u32[]{:S(2)}, u32[]{:S(2)}) collective-permute-start(bf16[128,512]{1,0:T(8,128)(2,1)S(1)} %get-tuple-element.24), channel_id=1, source_target_pairs={{0,2},{2,0},{4,6},{6,4},{8,10},{10,8},{12,14},{14,12},{1,3},{3,1},... | collective-permute-start | bytes 393224 | tf_op jit(solution)/shard_map/ppermute | solution.py:340
  15.2 9.6 %collective-permute-start.5 = (bf16[64,1024]{1,0:T(8,128)(2,1)S(1)}, bf16[64,1024]{1,0:T(8,128)(2,1)S(1)}, u32[]{:S(2)}, u32[]{:S(2)}) collective-permute-start(bf16[64,1024]{1,0:T(8,128)(2,1)S(1)} %after.1.after_ref), channel_id=1, source_target_pairs={{0,1},{1,0},{14,15},{15,14},{2,4},{3,5},{4,2},{5,3},{6,8},{7,9},{8... | collective-permute-start | bytes 393224 | tf_op jit(solution)/shard_map/ppermute | solution.py:344
  19.4 6.3 %collective-permute-start.4 = (bf16[64,1024]{1,0:T(8,128)(2,1)S(1)}, bf16[64,1024]{1,0:T(8,128)(2,1)S(1)}, u32[]{:S(2)}, u32[]{:S(2)}) collective-permute-start(bf16[64,1024]{1,0:T(8,128)(2,1)S(1)} %get-tuple-element.31), channel_id=1, source_target_pairs={{0,2},{2,0},{4,6},{6,4},{8,10},{10,8},{12,14},{14,12},{1,3},{3,1},... | collective-permute-start | bytes 393224 | tf_op jit(solution)/shard_map/ppermute | solution.py:347

commit v7 on v6

--- a/solution.py
+++ b/solution.py
@@ -175,8 +175,9 @@
     def results(j):
         grown, inverse, dprobs, delta = held.pop(j)
         cols = pl.ds(j * 2 * BLK, 2 * BLK)
-        p_ref[:, cols] = (grown * inverse).astype(jnp.bfloat16)
-        dscores = (grown * (SCALE * inverse) * (dprobs - delta)).astype(jnp.bfloat16)
+        probs = grown * inverse
+        p_ref[:, cols] = probs.astype(jnp.bfloat16)
+        dscores = (probs * ((dprobs - delta) * SCALE)).astype(jnp.bfloat16)
         ds_ref[:, cols] = dscores
         both = lax.dot_general(
             dscores, k_ref[:, pl.ds(start + j * PAIR, PAIR)], FIRST, preferred_element_type=jnp.float32
@@ -225,7 +226,18 @@
     )(message, *others, keys, values)
 
 
-def event_kernel(pl_ref, dsl_ref, ml_ref, pr_ref, dsr_ref, mr_ref, p1_ref, ds1_ref, m1_ref, gk_hbm, gv_hbm, gk_ref, gv_ref, sems):
+def event_kernel(pl_ref, dsl_ref, ml_ref, pr_ref, dsr_ref, mr_ref, p1_ref, ds1_ref, m1_ref, back_ref, own_ref, gk_hbm, gv_hbm, gq_hbm, gk_ref, gv_ref, sems, sem):
+    odd = lax.axis_index("seq") % 2
+    block_rows = gq_hbm.at[pl.ds(pl.multiple_of(odd * BLK, BLK), BLK), :]
+
+    @pl.when(at_end())
+    def _():
+        pltpu.make_async_copy(own_ref, block_rows, sem).start()
+
+    @pl.when(jnp.logical_not(at_end()))
+    def _():
+        pltpu.make_async_copy(back_ref, block_rows, sem).start()
+
     parts = sems.shape[1]
     rows = WIN // parts
     moves = []
@@ -253,6 +265,7 @@
             moves.append(move)
     for move in moves:
         move.wait()
+    pltpu.make_async_copy(back_ref, block_rows, sem).wait()
 
 
 def event_grads(*args):
@@ -260,31 +273,16 @@
     out = jax.ShapeDtypeStruct((WIN, width), jnp.bfloat16)
     return pl.pallas_call(
         event_kernel,
-        in_specs=[WHOLE] * 9,
-        out_specs=[RAW] * 2,
-        out_shape=[out] * 2,
-        scratch_shapes=[pltpu.VMEM((WIN, width), jnp.bfloat16)] * 2 + [pltpu.SemaphoreType.DMA((2, 4))],
+        in_specs=[WHOLE] * 11,
+        out_specs=[RAW] * 3,
+        out_shape=[out, out, jax.ShapeDtypeStruct((2 * BLK, width), jnp.bfloat16)],
+        scratch_shapes=[pltpu.VMEM((WIN, width), jnp.bfloat16)] * 2 + [pltpu.SemaphoreType.DMA((2, 4)), pltpu.SemaphoreType.DMA],
         compiler_params=params(32),
         cost_estimate=pl.CostEstimate(
             flops=8 * BLK * WIN * width, bytes_accessed=8 * WIN * width, transcendentals=0
         ),
         name="event_grads",
     )(*args)
-
-
-def join_across_kernel(across_ref, own_ref, out_hbm, sem):
-    odd = lax.axis_index("seq") % 2
-    rows = out_hbm.at[pl.ds(pl.multiple_of(odd * BLK, BLK), BLK), :]
-
-    @pl.when(at_end())
-    def _():
-        pltpu.make_async_copy(own_ref, rows, sem).start()
-
-    @pl.when(jnp.logical_not(at_end()))
-    def _():
-        pltpu.make_async_copy(across_ref, rows, sem).start()
-
-    pltpu.make_async_copy(across_ref, rows, sem).wait()
 
 
 def join_inside_kernel(inside_ref, half_hbm, out_hbm, sem):
@@ -294,19 +292,6 @@
     )
     move.start()
     move.wait()
-
-
-def join_across(back_across, own_across):
-    width = back_across.shape[1]
-    return pl.pallas_call(
-        join_across_kernel,
-        in_specs=[WHOLE] * 2,
-        out_specs=RAW,
-        out_shape=jax.ShapeDtypeStruct((2 * BLK, width), back_across.dtype),
-        scratch_shapes=[pltpu.SemaphoreType.DMA],
-        compiler_params=params(8),
-        name="join_across",
-    )(back_across, own_across)
 
 
 def join_inside(back_inside, half):
@@ -345,8 +330,8 @@
     gql, *lefts = attend(attend_left_kernel, got_left, [sent], keys, values, width // 2)
     gq0, *rights = attend(attend_right_kernel, got_right, [gql], keys, values, width)
     back0 = lax.ppermute(gq0, "seq", inside)
-    grad_keys, grad_values = event_grads(*lefts, got_left, *rights, got_right, p1, ds1, used)
-    return join_inside(back0, join_across(back1, gq1)), grad_keys, grad_values
+    grad_keys, grad_values, half = event_grads(*lefts, got_left, *rights, got_right, p1, ds1, used, back1, gq1)
+    return join_inside(back0, half), grad_keys, grad_values
 
 
 def solution(mesh):

time: 26.5 us -> 26.4 us (level)
  Pallas kernels: 12.5 us -> 11.7 us
  waiting for transfers between devices: 5.05 us -> 5.85 us
    ppermute x1, waiting for transfers between devices: 0.23 us -> 0.87 us  [shards(): back0 = lax.ppermute(gq0, 'seq', inside)]
    pallas_call x2 -> x1, Pallas kernels: 3.05 us -> 2.42 us  [event_grads(): pl.pallas_call(event_kernel, in_specs=[WHOLE] * 11, out_specs=[RAW] * 3,...]
  transfers between devices with their start and end apart: 6 -> 6, of which waited for: 4 -> 4; matrix products, arithmetic and copies ran while one was open for 0% -> 0% of each run, Pallas kernels for 45% -> 42%
where the time goes in v7:
time: 26.4 us; the launch traced here: 26.3 us
  Pallas kernels  11.7 us (44%)
  starting transfers between devices  8.02 us (30%)
  waiting for transfers between devices  5.85 us (22%)
  between operations  0.71 us (3%)
    pallas_call x3, Pallas kernels, attend(): pl.pallas_call(kernel, in_specs=[WHOLE] * (len(others) + 3), out_specs=[W...  5.31 us
    ppermute x1, starting transfers between devices, shards(): got_left = lax.ppermute(left, 'seq', inside)  4.03 us
    ppermute x1, waiting for transfers between devices, shards(): got_left = lax.ppermute(left, 'seq', inside)  3.51 us
    ppermute x1, starting transfers between devices, shards(): back0 = lax.ppermute(gq0, 'seq', inside)  2.92 us
    pallas_call x1, Pallas kernels, event_grads(): pl.pallas_call(event_kernel, in_specs=[WHOLE] * 11, out_specs=[RAW] * 3,...  2.42 us
    pallas_call x1, Pallas kernels, stage(): pl.pallas_call(stage_kernel, in_specs=[RAW] * 2, out_specs=[WHOLE] * 2, o...  2.21 us
    ppermute x1, waiting for transfers between devices, shards(): got_right = lax.ppermute(right, 'seq', inside)  1.14 us
    pallas_call x1, Pallas kernels, load(): pl.pallas_call(load_kernel, in_specs=[RAW] * 2, out_specs=[WHOLE] * 2, ou...  1.04 us
  transfers between devices with their start and end apart: 6, of which 4 were waited for; matrix products, arithmetic and copies ran while one was open for 0% of the time, Pallas kernels for 42%

profile of v7, /device:TPU:0, one launch (start us, length us, event | category | flops | bytes accessed | tf_op | source)
XLA Modules:
  0.0 26.3 jit_solution(3473718602132707184)
XLA Ops:
  0.6 0.5 %collective-permute-start = (bf16[64,2048]{1,0:T(8,128)(2,1)}, bf16[64,2048]{1,0:T(8,128)(2,1)S(1)}, u32[]{:S(2)}, u32[]{:S(2)}) collective-permute-start(bf16[64,2048]{1,0:T(8,128)(2,1)} %g_hbm.1), channel_id=1, source_target_pairs={{0,1},{1,0},{2,3},{3,2},{4,5},{5,4},{6,7},{7,6},{8,9},{9,8},{10,11... | collective-permute-start | bytes 786440 | tf_op jit(solution)/shard_map/ppermute | solution.py:321
  1.1 1.0 %load.1 = (bf16[128,1024]{1,0:T(8,128)(2,1)S(1)}, bf16[64,2048]{1,0:T(8,128)(2,1)S(1)}) custom-call(bf16[128,1024]{1,0:T(8,128)(2,1)} %q_hbm.1, bf16[64,2048]{1,0:T(8,128)(2,1)} %g_hbm.1), custom_call_target="tpu_custom_call" | custom-call | tf_op jit(solution)/shard_map/load/pallas_call | solution.py:49
  2.2 0.3 %collective-permute-done.other_ref = bf16[64,2048]{1,0:T(8,128)(2,1)S(1)} collective-permute-done((bf16[64,2048]{1,0:T(8,128)(2,1)}, bf16[64,2048]{1,0:T(8,128)(2,1)S(1)}, u32[]{:S(2)}, u32[]{:S(2)}) %collective-permute-start) | collective-permute-done | bytes 262176 | tf_op jit(solution)/shard_map/ppermute | solution.py:321
  2.6 0.4 %collective-permute-start.3 = (bf16[128,1024]{1,0:T(8,128)(2,1)S(1)}, bf16[128,1024]{1,0:T(8,128)(2,1)S(1)}, u32[]{:S(2)}, u32[]{:S(2)}) collective-permute-start(bf16[128,1024]{1,0:T(8,128)(2,1)S(1)} %get-tuple-element.27.own_ref), channel_id=1, source_target_pairs={{0,1},{1,0},{14,15},{15,14},{2,4},{3,5},{4,2},{5,3},{6,8},{7,9},{8... | collective-permute-start | bytes 786440 | tf_op jit(solution)/shard_map/ppermute | solution.py:323
  3.0 4.0 %collective-permute-start.2 = (bf16[128,512]{1,0:T(8,128)(2,1)S(1)}, bf16[128,512]{1,0:T(8,128)(2,1)S(1)}, u32[]{:S(2)}, u32[]{:S(2)}) collective-permute-start(bf16[128,512]{1,0:T(8,128)(2,1)S(1)} %get-tuple-element.26), channel_id=1, source_target_pairs={{0,2},{2,0},{4,6},{6,4},{8,10},{10,8},{12,14},{14,12},{1,3},{3,1},... | collective-permute-start | bytes 393224 | tf_op jit(solution)/shard_map/ppermute | solution.py:324
  7.0 0.0 collective-permute-start.1
  7.1 2.2 %stage.1 = (bf16[1024,1024]{1,0:T(8,128)(2,1)S(1)}, bf16[1024,1024]{1,0:T(8,128)(2,1)S(1)}) custom-call(bf16[1024,1024]{1,0:T(8,128)(2,1)} %k_hbm.1, bf16[1024,1024]{1,0:T(8,128)(2,1)} %v_hbm.1), custom_call_target="tpu_custom_call" | custom-call | bytes 8388608 | tf_op jit(solution)/shard_map/stage/pallas_call | solution.py:113
  9.3 0.0 collective-permute-done.3.received_ref
  9.3 2.4 %attend.3 = (bf16[64,1024]{1,0:T(8,128)(2,1)S(1)}, bf16[1024,512]{1,0:T(8,128)(2,1)S(1)}, bf16[1024,512]{1,0:T(8,128)(2,1)S(1)}, bf16[128,1024]{1,0:T(8,128)(2,1)S(1)}) custom-call(bf16[128,1024]{1,0:T(8,128)(2,1)S(1)} %get-tuple-element.27.own_ref, bf16[128,1024]{1,0:T(8,128)(2,1)S(1)} %collective-permute-done.3.received_ref, ...), custom_call_target="tpu_custom_call" | custom-call | flops 536870912 | bytes 6291456 | tf_op jit(solution)/shard_map/attend/pallas_call | solution.py:216
  11.7 3.5 %collective-permute-done.2.message_ref.m_ref.ml_ref = bf16[128,512]{1,0:T(8,128)(2,1)S(1)} collective-permute-done((bf16[128,512]{1,0:T(8,128)(2,1)S(1)}, bf16[128,512]{1,0:T(8,128)(2,1)S(1)}, u32[]{:S(2)}, u32[]{:S(2)}) %collective-permute-start.2) | collective-permute-done | bytes 131104 | tf_op jit(solution)/shard_map/ppermute | solution.py:324
  15.2 0.1 collective-permute-start.5
  15.3 1.5 %attend.4 = (bf16[64,512]{1,0:T(8,128)(2,1)S(1)}, bf16[1024,256]{1,0:T(8,128)(2,1)S(1)}, bf16[1024,256]{1,0:T(8,128)(2,1)S(1)}) custom-call(bf16[128,512]{1,0:T(8,128)(2,1)S(1)} %collective-permute-done.2.message_ref.m_ref.ml_ref, bf16[64,1024]{1,0:T(8,128)(2,1)S(1)} %after.1.after_ref, bf16[1024,1024]{1,0:T(8,128)(2,1)S(1)} %get-tuple-element.28.k_ref, ...), custom_call_target="tpu_custom_call" | custom-call | flops 268435456 | bytes 3145728 | tf_op jit(solution)/shard_map/attend/pallas_call | solution.py:216
  16.8 1.1 %collective-permute-done.1.m_ref.mr_ref = bf16[128,512]{1,0:T(8,128)(2,1)S(1)} collective-permute-done((bf16[128,512]{1,0:T(8,128)(2,1)S(1)}, bf16[128,512]{1,0:T(8,128)(2,1)S(1)}, u32[]{:S(2)}, u32[]{:S(2)}) %collective-permute-start.1) | collective-permute-done | bytes 131104 | tf_op jit(solution)/shard_map/ppermute | solution.py:325
  17.9 1.5 %attend.5 = (bf16[64,1024]{1,0:T(8,128)(2,1)S(1)}, bf16[1024,256]{1,0:T(8,128)(2,1)S(1)}, bf16[1024,256]{1,0:T(8,128)(2,1)S(1)}) custom-call(bf16[128,512]{1,0:T(8,128)(2,1)S(1)} %collective-permute-done.1.m_ref.mr_ref, bf16[64,512]{1,0:T(8,128)(2,1)S(1)} %get-tuple-element.31.left_ref, bf16[1024,1024]{1,0:T(8,128)(2,1)S(1)} %get-tuple-element.28.k_ref, ...), custom_call_target="tpu_custom_call" | custom-call | flops 268435456 | bytes 3145728 | tf_op jit(solution)/shard_map/attend/pallas_call | solution.py:216
  19.4 2.9 %collective-permute-start.4 = (bf16[64,1024]{1,0:T(8,128)(2,1)S(1)}, bf16[64,1024]{1,0:T(8,128)(2,1)S(1)}, u32[]{:S(2)}, u32[]{:S(2)}) collective-permute-start(bf16[64,1024]{1,0:T(8,128)(2,1)S(1)} %get-tuple-element.32), channel_id=1, source_target_pairs={{0,2},{2,0},{4,6},{6,4},{8,10},{10,8},{12,14},{14,12},{1,3},{3,1},... | collective-permute-start | bytes 393224 | tf_op jit(solution)/shard_map/ppermute | solution.py:332
  22.3 0.0 collective-permute-done.5.back_ref
  22.3 2.4 %event_grads.1 = (bf16[1024,1024]{1,0:T(8,128)(2,1)}, bf16[1024,1024]{1,0:T(8,128)(2,1)}, bf16[128,1024]{1,0:T(8,128)(2,1)}) custom-call(bf16[1024,256]{1,0:T(8,128)(2,1)S(1)} %get-tuple-element.33.pl_ref, bf16[1024,256]{1,0:T(8,128)(2,1)S(1)} %get-tuple-element.34.dsl_ref, bf16[128,512]{1,0:T(8,128)(2,1)S(1)} %collective-permute-done.2.message_ref.m_ref.ml_ref, ...), custom_call_target="tpu_custom_call" | custom-call | flops 536870912 | bytes 8388608 | tf_op jit(solution)/shard_map/event_grads/pallas_call | solution.py:274
  24.7 0.9 %collective-permute-done.4.inside_ref = bf16[64,1024]{1,0:T(8,128)(2,1)S(1)} collective-permute-done((bf16[64,1024]{1,0:T(8,128)(2,1)S(1)}, bf16[64,1024]{1,0:T(8,128)(2,1)S(1)}, u32[]{:S(2)}, u32[]{:S(2)}) %collective-permute-start.4) | collective-permute-done | bytes 131104 | tf_op jit(solution)/shard_map/ppermute | solution.py:332
  25.6 0.7 %join_inside.1 = bf16[128,1024]{1,0:T(8,128)(2,1)} custom-call(bf16[64,1024]{1,0:T(8,128)(2,1)S(1)} %collective-permute-done.4.inside_ref, bf16[128,1024]{1,0:T(8,128)(2,1)} %get-tuple-element.40.half_hbm), custom_call_target="tpu_custom_call", output_to_operand_aliasing={{}: (1, {})} | custom-call | tf_op jit(solution)/shard_map/join_inside/pallas_call | solution.py:298
  (2 shorter events, 0.0 us)
Async XLA Ops:
  0.6 1.9 %collective-permute-start = (bf16[64,2048]{1,0:T(8,128)(2,1)}, bf16[64,2048]{1,0:T(8,128)(2,1)S(1)}, u32[]{:S(2)}, u32[]{:S(2)}) collective-permute-start(bf16[64,2048]{1,0:T(8,128)(2,1)} %g_hbm.1), channel_id=1, source_target_pairs={{0,1},{1,0},{2,3},{3,2},{4,5},{5,4},{6,7},{7,6},{8,9},{9,8},{10,11... | collective-permute-start | bytes 786440 | tf_op jit(solution)/shard_map/ppermute | solution.py:321
  2.6 6.7 %collective-permute-start.3 = (bf16[128,1024]{1,0:T(8,128)(2,1)S(1)}, bf16[128,1024]{1,0:T(8,128)(2,1)S(1)}, u32[]{:S(2)}, u32[]{:S(2)}) collective-permute-start(bf16[128,1024]{1,0:T(8,128)(2,1)S(1)} %get-tuple-element.27.own_ref), channel_id=1, source_target_pairs={{0,1},{1,0},{14,15},{15,14},{2,4},{3,5},{4,2},{5,3},{6,8},{7,9},{8... | collective-permute-start | bytes 786440 | tf_op jit(solution)/shard_map/ppermute | solution.py:323
  3.0 12.2 %collective-permute-start.2 = (bf16[128,512]{1,0:T(8,128)(2,1)S(1)}, bf16[128,512]{1,0:T(8,128)(2,1)S(1)}, u32[]{:S(2)}, u32[]{:S(2)}) collective-permute-start(bf16[128,512]{1,0:T(8,128)(2,1)S(1)} %get-tuple-element.26), channel_id=1, source_target_pairs={{0,2},{2,0},{4,6},{6,4},{8,10},{10,8},{12,14},{14,12},{1,3},{3,1},... | collective-permute-start | bytes 393224 | tf_op jit(solution)/shard_map/ppermute | solution.py:324
  7.0 10.9 %collective-permute-start.1 = (bf16[128,512]{1,0:T(8,128)(2,1)S(1)}, bf16[128,512]{1,0:T(8,128)(2,1)S(1)}, u32[]{:S(2)}, u32[]{:S(2)}) collective-permute-start(bf16[128,512]{1,0:T(8,128)(2,1)S(1)} %get-tuple-element.25), channel_id=1, source_target_pairs={{0,2},{2,0},{4,6},{6,4},{8,10},{10,8},{12,14},{14,12},{1,3},{3,1},... | collective-permute-start | bytes 393224 | tf_op jit(solution)/shard_map/ppermute | solution.py:325
  15.2 7.1 %collective-permute-start.5 = (bf16[64,1024]{1,0:T(8,128)(2,1)S(1)}, bf16[64,1024]{1,0:T(8,128)(2,1)S(1)}, u32[]{:S(2)}, u32[]{:S(2)}) collective-permute-start(bf16[64,1024]{1,0:T(8,128)(2,1)S(1)} %after.1.after_ref), channel_id=1, source_target_pairs={{0,1},{1,0},{14,15},{15,14},{2,4},{3,5},{4,2},{5,3},{6,8},{7,9},{8... | collective-permute-start | bytes 393224 | tf_op jit(solution)/shard_map/ppermute | solution.py:329
  19.4 6.2 %collective-permute-start.4 = (bf16[64,1024]{1,0:T(8,128)(2,1)S(1)}, bf16[64,1024]{1,0:T(8,128)(2,1)S(1)}, u32[]{:S(2)}, u32[]{:S(2)}) collective-permute-start(bf16[64,1024]{1,0:T(8,128)(2,1)S(1)} %get-tuple-element.32), channel_id=1, source_target_pairs={{0,2},{2,0},{4,6},{6,4},{8,10},{10,8},{12,14},{14,12},{1,3},{3,1},... | collective-permute-start | bytes 393224 | tf_op jit(solution)/shard_map/ppermute | solution.py:332

commit v8 on v6

--- a/solution.py
+++ b/solution.py
@@ -175,8 +175,9 @@
     def results(j):
         grown, inverse, dprobs, delta = held.pop(j)
         cols = pl.ds(j * 2 * BLK, 2 * BLK)
-        p_ref[:, cols] = (grown * inverse).astype(jnp.bfloat16)
-        dscores = (grown * (SCALE * inverse) * (dprobs - delta)).astype(jnp.bfloat16)
+        probs = grown * inverse
+        p_ref[:, cols] = probs.astype(jnp.bfloat16)
+        dscores = (probs * ((dprobs - delta) * SCALE)).astype(jnp.bfloat16)
         ds_ref[:, cols] = dscores
         both = lax.dot_general(
             dscores, k_ref[:, pl.ds(start + j * PAIR, PAIR)], FIRST, preferred_element_type=jnp.float32

time: 26.5 us -> 26.4 us (level)
  transfers between devices with their start and end apart: 6 -> 6, of which waited for: 4 -> 4; matrix products, arithmetic and copies ran while one was open for 0% -> 0% of each run, Pallas kernels for 45% -> 44%
where the time goes in v8:
time: 26.4 us; the launch traced here: 26.3 us
  Pallas kernels  12.3 us (47%)
  starting transfers between devices  8.02 us (30%)
  waiting for transfers between devices  5.2 us (20%)
  between operations  0.72 us (3%)
    pallas_call x3, Pallas kernels, attend(): pl.pallas_call(kernel, in_specs=[WHOLE] * (len(others) + 3), out_specs=[W...  5.31 us
    ppermute x1, starting transfers between devices, shards(): got_left = lax.ppermute(left, 'seq', inside)  4.03 us
    ppermute x1, waiting for transfers between devices, shards(): got_left = lax.ppermute(left, 'seq', inside)  3.51 us
    ppermute x1, starting transfers between devices, shards(): back0 = lax.ppermute(gq0, 'seq', inside)  2.92 us
    pallas_call x1, Pallas kernels, event_grads(): pl.pallas_call(event_kernel, in_specs=[WHOLE] * 9, out_specs=[RAW] * 2, o...  2.37 us
    pallas_call x1, Pallas kernels, stage(): pl.pallas_call(stage_kernel, in_specs=[RAW] * 2, out_specs=[WHOLE] * 2, o...  2.21 us
    ppermute x1, waiting for transfers between devices, shards(): got_right = lax.ppermute(right, 'seq', inside)  1.14 us
    pallas_call x1, Pallas kernels, load(): pl.pallas_call(load_kernel, in_specs=[RAW] * 2, out_specs=[WHOLE] * 2, ou...  1.04 us
  transfers between devices with their start and end apart: 6, of which 4 were waited for; matrix products, arithmetic and copies ran while one was open for 0% of the time, Pallas kernels for 44%

profile of v8, /device:TPU:0, one launch (start us, length us, event | category | flops | bytes accessed | tf_op | source)
XLA Modules:
  0.0 26.3 jit_solution(2055563741512210729)
XLA Ops:
  0.6 0.5 %collective-permute-start = (bf16[64,2048]{1,0:T(8,128)(2,1)}, bf16[64,2048]{1,0:T(8,128)(2,1)S(1)}, u32[]{:S(2)}, u32[]{:S(2)}) collective-permute-start(bf16[64,2048]{1,0:T(8,128)(2,1)} %g_hbm.1), channel_id=1, source_target_pairs={{0,1},{1,0},{2,3},{3,2},{4,5},{5,4},{6,7},{7,6},{8,9},{9,8},{10,11... | collective-permute-start | bytes 786440 | tf_op jit(solution)/shard_map/ppermute | solution.py:337
  1.1 1.0 %load.1 = (bf16[128,1024]{1,0:T(8,128)(2,1)S(1)}, bf16[64,2048]{1,0:T(8,128)(2,1)S(1)}) custom-call(bf16[128,1024]{1,0:T(8,128)(2,1)} %q_hbm.1, bf16[64,2048]{1,0:T(8,128)(2,1)} %g_hbm.1), custom_call_target="tpu_custom_call" | custom-call | tf_op jit(solution)/shard_map/load/pallas_call | solution.py:49
  2.2 0.3 %collective-permute-done.other_ref = bf16[64,2048]{1,0:T(8,128)(2,1)S(1)} collective-permute-done((bf16[64,2048]{1,0:T(8,128)(2,1)}, bf16[64,2048]{1,0:T(8,128)(2,1)S(1)}, u32[]{:S(2)}, u32[]{:S(2)}) %collective-permute-start) | collective-permute-done | bytes 262176 | tf_op jit(solution)/shard_map/ppermute | solution.py:337
  2.6 0.4 %collective-permute-start.3 = (bf16[128,1024]{1,0:T(8,128)(2,1)S(1)}, bf16[128,1024]{1,0:T(8,128)(2,1)S(1)}, u32[]{:S(2)}, u32[]{:S(2)}) collective-permute-start(bf16[128,1024]{1,0:T(8,128)(2,1)S(1)} %get-tuple-element.26.own_ref), channel_id=1, source_target_pairs={{0,1},{1,0},{14,15},{15,14},{2,4},{3,5},{4,2},{5,3},{6,8},{7,9},{8... | collective-permute-start | bytes 786440 | tf_op jit(solution)/shard_map/ppermute | solution.py:339
  3.0 4.0 %collective-permute-start.2 = (bf16[128,512]{1,0:T(8,128)(2,1)S(1)}, bf16[128,512]{1,0:T(8,128)(2,1)S(1)}, u32[]{:S(2)}, u32[]{:S(2)}) collective-permute-start(bf16[128,512]{1,0:T(8,128)(2,1)S(1)} %get-tuple-element.25), channel_id=1, source_target_pairs={{0,2},{2,0},{4,6},{6,4},{8,10},{10,8},{12,14},{14,12},{1,3},{3,1},... | collective-permute-start | bytes 393224 | tf_op jit(solution)/shard_map/ppermute | solution.py:340
  7.0 0.0 collective-permute-start.1
  7.1 2.2 %stage.1 = (bf16[1024,1024]{1,0:T(8,128)(2,1)S(1)}, bf16[1024,1024]{1,0:T(8,128)(2,1)S(1)}) custom-call(bf16[1024,1024]{1,0:T(8,128)(2,1)} %k_hbm.1, bf16[1024,1024]{1,0:T(8,128)(2,1)} %v_hbm.1), custom_call_target="tpu_custom_call" | custom-call | bytes 8388608 | tf_op jit(solution)/shard_map/stage/pallas_call | solution.py:113
  9.3 0.0 collective-permute-done.3.received_ref
  9.3 2.4 %attend.3 = (bf16[64,1024]{1,0:T(8,128)(2,1)S(1)}, bf16[1024,512]{1,0:T(8,128)(2,1)S(1)}, bf16[1024,512]{1,0:T(8,128)(2,1)S(1)}, bf16[128,1024]{1,0:T(8,128)(2,1)S(1)}) custom-call(bf16[128,1024]{1,0:T(8,128)(2,1)S(1)} %get-tuple-element.26.own_ref, bf16[128,1024]{1,0:T(8,128)(2,1)S(1)} %collective-permute-done.3.received_ref, ...), custom_call_target="tpu_custom_call" | custom-call | flops 536870912 | bytes 6291456 | tf_op jit(solution)/shard_map/attend/pallas_call | solution.py:216
  11.7 3.5 %collective-permute-done.2.message_ref.m_ref.ml_ref = bf16[128,512]{1,0:T(8,128)(2,1)S(1)} collective-permute-done((bf16[128,512]{1,0:T(8,128)(2,1)S(1)}, bf16[128,512]{1,0:T(8,128)(2,1)S(1)}, u32[]{:S(2)}, u32[]{:S(2)}) %collective-permute-start.2) | collective-permute-done | bytes 131104 | tf_op jit(solution)/shard_map/ppermute | solution.py:340
  15.2 0.1 collective-permute-start.5
  15.3 1.5 %attend.4 = (bf16[64,512]{1,0:T(8,128)(2,1)S(1)}, bf16[1024,256]{1,0:T(8,128)(2,1)S(1)}, bf16[1024,256]{1,0:T(8,128)(2,1)S(1)}) custom-call(bf16[128,512]{1,0:T(8,128)(2,1)S(1)} %collective-permute-done.2.message_ref.m_ref.ml_ref, bf16[64,1024]{1,0:T(8,128)(2,1)S(1)} %after.1.after_ref, bf16[1024,1024]{1,0:T(8,128)(2,1)S(1)} %get-tuple-element.27.k_ref, ...), custom_call_target="tpu_custom_call" | custom-call | flops 268435456 | bytes 3145728 | tf_op jit(solution)/shard_map/attend/pallas_call | solution.py:216
  16.8 1.1 %collective-permute-done.1.m_ref.mr_ref = bf16[128,512]{1,0:T(8,128)(2,1)S(1)} collective-permute-done((bf16[128,512]{1,0:T(8,128)(2,1)S(1)}, bf16[128,512]{1,0:T(8,128)(2,1)S(1)}, u32[]{:S(2)}, u32[]{:S(2)}) %collective-permute-start.1) | collective-permute-done | bytes 131104 | tf_op jit(solution)/shard_map/ppermute | solution.py:341
  17.9 1.5 %attend.5 = (bf16[64,1024]{1,0:T(8,128)(2,1)S(1)}, bf16[1024,256]{1,0:T(8,128)(2,1)S(1)}, bf16[1024,256]{1,0:T(8,128)(2,1)S(1)}) custom-call(bf16[128,512]{1,0:T(8,128)(2,1)S(1)} %collective-permute-done.1.m_ref.mr_ref, bf16[64,512]{1,0:T(8,128)(2,1)S(1)} %get-tuple-element.30.left_ref, bf16[1024,1024]{1,0:T(8,128)(2,1)S(1)} %get-tuple-element.27.k_ref, ...), custom_call_target="tpu_custom_call" | custom-call | flops 268435456 | bytes 3145728 | tf_op jit(solution)/shard_map/attend/pallas_call | solution.py:216
  19.4 2.9 %collective-permute-start.4 = (bf16[64,1024]{1,0:T(8,128)(2,1)S(1)}, bf16[64,1024]{1,0:T(8,128)(2,1)S(1)}, u32[]{:S(2)}, u32[]{:S(2)}) collective-permute-start(bf16[64,1024]{1,0:T(8,128)(2,1)S(1)} %get-tuple-element.31), channel_id=1, source_target_pairs={{0,2},{2,0},{4,6},{6,4},{8,10},{10,8},{12,14},{14,12},{1,3},{3,1},... | collective-permute-start | bytes 393224 | tf_op jit(solution)/shard_map/ppermute | solution.py:348
  22.3 2.4 %event_grads.1 = (bf16[1024,1024]{1,0:T(8,128)(2,1)}, bf16[1024,1024]{1,0:T(8,128)(2,1)}) custom-call(bf16[1024,256]{1,0:T(8,128)(2,1)S(1)} %get-tuple-element.32.pl_ref, bf16[1024,256]{1,0:T(8,128)(2,1)S(1)} %get-tuple-element.33.dsl_ref, bf16[128,512]{1,0:T(8,128)(2,1)S(1)} %collective-permute-done.2.message_ref.m_ref.ml_ref, ...), custom_call_target="tpu_custom_call" | custom-call | flops 536870912 | bytes 8388608 | tf_op jit(solution)/shard_map/event_grads/pallas_call | solution.py:262
  24.7 0.0 collective-permute-done.5.across_ref
  24.7 0.7 %join_across.1.half_hbm = bf16[128,1024]{1,0:T(8,128)(2,1)} custom-call(bf16[64,1024]{1,0:T(8,128)(2,1)S(1)} %collective-permute-done.5.across_ref, bf16[64,1024]{1,0:T(8,128)(2,1)S(1)} %get-tuple-element.29.array_ref.own_ref), custom_call_target="tpu_custom_call" | custom-call | tf_op jit(solution)/shard_map/join_across/pallas_call | solution.py:302
  25.4 0.2 collective-permute-done.4.inside_ref
  25.6 0.7 %join_inside.1 = bf16[128,1024]{1,0:T(8,128)(2,1)} custom-call(bf16[64,1024]{1,0:T(8,128)(2,1)S(1)} %collective-permute-done.4.inside_ref, bf16[128,1024]{1,0:T(8,128)(2,1)} %join_across.1.half_hbm), custom_call_target="tpu_custom_call", output_to_operand_aliasing={{}: (1, {})} | custom-call | tf_op jit(solution)/shard_map/join_inside/pallas_call | solution.py:314
  (2 shorter events, 0.0 us)
Async XLA Ops:
  0.6 1.9 %collective-permute-start = (bf16[64,2048]{1,0:T(8,128)(2,1)}, bf16[64,2048]{1,0:T(8,128)(2,1)S(1)}, u32[]{:S(2)}, u32[]{:S(2)}) collective-permute-start(bf16[64,2048]{1,0:T(8,128)(2,1)} %g_hbm.1), channel_id=1, source_target_pairs={{0,1},{1,0},{2,3},{3,2},{4,5},{5,4},{6,7},{7,6},{8,9},{9,8},{10,11... | collective-permute-start | bytes 786440 | tf_op jit(solution)/shard_map/ppermute | solution.py:337
  2.6 6.7 %collective-permute-start.3 = (bf16[128,1024]{1,0:T(8,128)(2,1)S(1)}, bf16[128,1024]{1,0:T(8,128)(2,1)S(1)}, u32[]{:S(2)}, u32[]{:S(2)}) collective-permute-start(bf16[128,1024]{1,0:T(8,128)(2,1)S(1)} %get-tuple-element.26.own_ref), channel_id=1, source_target_pairs={{0,1},{1,0},{14,15},{15,14},{2,4},{3,5},{4,2},{5,3},{6,8},{7,9},{8... | collective-permute-start | bytes 786440 | tf_op jit(solution)/shard_map/ppermute | solution.py:339
  3.0 12.2 %collective-permute-start.2 = (bf16[128,512]{1,0:T(8,128)(2,1)S(1)}, bf16[128,512]{1,0:T(8,128)(2,1)S(1)}, u32[]{:S(2)}, u32[]{:S(2)}) collective-permute-start(bf16[128,512]{1,0:T(8,128)(2,1)S(1)} %get-tuple-element.25), channel_id=1, source_target_pairs={{0,2},{2,0},{4,6},{6,4},{8,10},{10,8},{12,14},{14,12},{1,3},{3,1},... | collective-permute-start | bytes 393224 | tf_op jit(solution)/shard_map/ppermute | solution.py:340
  7.0 10.9 %collective-permute-start.1 = (bf16[128,512]{1,0:T(8,128)(2,1)S(1)}, bf16[128,512]{1,0:T(8,128)(2,1)S(1)}, u32[]{:S(2)}, u32[]{:S(2)}) collective-permute-start(bf16[128,512]{1,0:T(8,128)(2,1)S(1)} %get-tuple-element.24), channel_id=1, source_target_pairs={{0,2},{2,0},{4,6},{6,4},{8,10},{10,8},{12,14},{14,12},{1,3},{3,1},... | collective-permute-start | bytes 393224 | tf_op jit(solution)/shard_map/ppermute | solution.py:341
  15.2 9.5 %collective-permute-start.5 = (bf16[64,1024]{1,0:T(8,128)(2,1)S(1)}, bf16[64,1024]{1,0:T(8,128)(2,1)S(1)}, u32[]{:S(2)}, u32[]{:S(2)}) collective-permute-start(bf16[64,1024]{1,0:T(8,128)(2,1)S(1)} %after.1.after_ref), channel_id=1, source_target_pairs={{0,1},{1,0},{14,15},{15,14},{2,4},{3,5},{4,2},{5,3},{6,8},{7,9},{8... | collective-permute-start | bytes 393224 | tf_op jit(solution)/shard_map/ppermute | solution.py:345
  19.4 6.2 %collective-permute-start.4 = (bf16[64,1024]{1,0:T(8,128)(2,1)S(1)}, bf16[64,1024]{1,0:T(8,128)(2,1)S(1)}, u32[]{:S(2)}, u32[]{:S(2)}) collective-permute-start(bf16[64,1024]{1,0:T(8,128)(2,1)S(1)} %get-tuple-element.31), channel_id=1, source_target_pairs={{0,2},{2,0},{4,6},{6,4},{8,10},{10,8},{12,14},{14,12},{1,3},{3,1},... | collective-permute-start | bytes 393224 | tf_op jit(solution)/shard_map/ppermute | solution.py:348
